TPU v7x, 32 devices: a whole 2x2x4 slice. The times are simulated.
32 devices in a mesh: dp: 8 (over y, x, core), seq: 4 (over z).
Axes of the slice: x: 2, y: 2, z: 4, core: 2. Of those that a mesh axis runs over, the one named last changes fastest.
Arguments:
- block_input: float32 [8, 1024, 1536], P('dp', 'seq'), may hold values from -6 to 6
- cotangent: float32 [8, 1024, 1536], P('dp', 'seq'), may hold values from -6 to 6
- norm_gain: float32 [1536], P(('dp', 'seq')), may hold values from 0.5 to 1.5
- in_weight: float32 [1536, 6448], P(('dp', 'seq')), may hold values from -0.15625 to 0.15625
- conv_weight: float32 [4, 3328], P(None, ('dp', 'seq')), may hold values from -3 to 3
- conv_bias: float32 [3328], P(('dp', 'seq')), may hold values from -0.5 to 0.5
- step_bias: float32 [48], replicated, may hold values from -7 to 0.5
- decay_log: float32 [48], replicated, may hold values from -2.5 to -1.5
- skip_gain: float32 [48], replicated, may hold values from 0.5 to 1.5
- gated_gain: float32 [3072], P(('dp', 'seq')), may hold values from 0.5 to 1.5
- out_weight: float32 [1536, 3072], P(('dp', 'seq')), may hold values from -0.109375 to 0.109375
- first_norm_gain: float32 [1536], P(('dp', 'seq')), may hold values from -28 to 28
- second_norm_gain: float32 [1536], P(('dp', 'seq')), may hold values from 16.384 to 163.84
- first_in_weight: float32 [1536, 6448], P(('dp', 'seq')), may hold values from -14 to 14
- second_in_weight: float32 [1536, 6448], P(('dp', 'seq')), may hold values from 4.096 to 40.96
- first_conv_weight: float32 [4, 3328], P(None, ('dp', 'seq')), may hold values from -14 to 14
- second_conv_weight: float32 [4, 3328], P(None, ('dp', 'seq')), may hold values from 4.096 to 40.96
- first_conv_bias: float32 [3328], P(('dp', 'seq')), may hold values from -14 to 14
- second_conv_bias: float32 [3328], P(('dp', 'seq')), may hold values from 4.096 to 40.96
- first_step_bias: float32 [48], replicated, may hold values from -28 to 28
- second_step_bias: float32 [48], replicated, may hold values from 16.384 to 163.84
- first_decay_log: float32 [48], replicated, may hold values from -28 to 28
- second_decay_log: float32 [48], replicated, may hold values from 16.384 to 163.84
- first_skip_gain: float32 [48], replicated, may hold values from -56 to 56
- second_skip_gain: float32 [48], replicated, may hold values from 81.92 to 819.2
- first_gated_gain: float32 [3072], P(('dp', 'seq')), may hold values from -14 to 14
- second_gated_gain: float32 [3072], P(('dp', 'seq')), may hold values from 4.096 to 40.96
- first_out_weight: float32 [1536, 3072], P(('dp', 'seq')), may hold values from -28 to 28
- second_out_weight: float32 [1536, 3072], P(('dp', 'seq')), may hold values from 16.384 to 163.84
Outputs:
- block_output: float32 [8, 1024, 1536], P('dp', 'seq')
- input_grad: float32 [8, 1024, 1536], P('dp', 'seq')
- grad_norm_gain: float32 [1536], P(('dp', 'seq'))
- grad_in_weight: float32 [1536, 6448], P(('dp', 'seq'))
- grad_conv_weight: float32 [4, 3328], P(None, ('dp', 'seq'))
- grad_conv_bias: float32 [3328], P(('dp', 'seq'))
- grad_step_bias: float32 [48], replicated
- grad_decay_log: float32 [48], replicated
- grad_skip_gain: float32 [48], replicated
- grad_gated_gain: float32 [3072], P(('dp', 'seq'))
- grad_out_weight: float32 [1536, 3072], P(('dp', 'seq'))
- new_norm_gain: float32 [1536], P(('dp', 'seq'))
- new_first_norm_gain: float32 [1536], P(('dp', 'seq'))
- new_second_norm_gain: float32 [1536], P(('dp', 'seq'))
- new_in_weight: float32 [1536, 6448], P(('dp', 'seq'))
- new_first_in_weight: float32 [1536, 6448], P(('dp', 'seq'))
- new_second_in_weight: float32 [1536, 6448], P(('dp', 'seq'))
- new_conv_weight: float32 [4, 3328], P(None, ('dp', 'seq'))
- new_first_conv_weight: float32 [4, 3328], P(None, ('dp', 'seq'))
- new_second_conv_weight: float32 [4, 3328], P(None, ('dp', 'seq'))
- new_conv_bias: float32 [3328], P(('dp', 'seq'))
- new_first_conv_bias: float32 [3328], P(('dp', 'seq'))
- new_second_conv_bias: float32 [3328], P(('dp', 'seq'))
- new_step_bias: float32 [48], replicated
- new_first_step_bias: float32 [48], replicated
- new_second_step_bias: float32 [48], replicated
- new_decay_log: float32 [48], replicated
- new_first_decay_log: float32 [48], replicated
- new_second_decay_log: float32 [48], replicated
- new_skip_gain: float32 [48], replicated
- new_first_skip_gain: float32 [48], replicated
- new_second_skip_gain: float32 [48], replicated
- new_gated_gain: float32 [3072], P(('dp', 'seq'))
- new_first_gated_gain: float32 [3072], P(('dp', 'seq'))
- new_second_gated_gain: float32 [3072], P(('dp', 'seq'))
- new_out_weight: float32 [1536, 3072], P(('dp', 'seq'))
- new_first_out_weight: float32 [1536, 3072], P(('dp', 'seq'))
- new_second_out_weight: float32 [1536, 3072], P(('dp', 'seq'))
All inputs are finite; a program needn't handle non-finite values.
Results may differ from a plain program's by a relative error of at most 0.00115.
The roundings to bfloat16 on the way count: a program that leaves them out, or rounds other values in their place, can miss the bound.
Values may be sent and summed in bfloat16 or wider, within the bound.
No kernel may reach another device: no remote copies, remote signals or barrier semaphores. Data moves between devices by JAX's collectives and lax.ppermute only.
A program may use at most 320 MiB of HBM per device.

v0:
```python
import functools
import math

import jax
import jax.numpy as jnp
from jax import lax
from jax.experimental import pallas as pl
from jax.experimental.pallas import tpu as pltpu
from jax.sharding import PartitionSpec as P


E = 3072
NST = 128
NHEADS = 48
HDIM = 64
CONVW = 4
SPAN = 256
LANES = 128


low = jnp.bfloat16
half = jnp.float16
highest = lax.Precision.HIGHEST
beta_one = 0.9
beta_two = 0.95
adam_step = 10.0
adam_eps = 1e-08
rate_matrix = 0.01
rate_vector = 0.3
weight_decay = 0.1
norm_eps = 1e-05


def shift(block, axis, distance):
    size = lax.axis_size(axis)
    return lax.ppermute(block, axis, [(i, (i + distance) % size) for i in range(size)])


def swap(block, axis, bit):
    return lax.ppermute(block, axis, [(i, i ^ bit) for i in range(lax.axis_size(axis))])


def pick(stacked, index):
    return lax.dynamic_index_in_dim(stacked, index, 0, keepdims=False)


def exchange_sum(stacked, axis):
    size, here = lax.axis_size(axis), lax.axis_index(axis)
    arrived = [shift(pick(stacked, (here + turn) % size), axis, turn) for turn in range(1, size)]
    total = pick(stacked, here)
    for part in arrived:
        total = total + part
    return total


def after(value, *others):
    return lax.optimization_barrier((value,) + others)[0]


def pack_half(parts, bound):
    power = jnp.clip(jnp.ceil(jnp.log2(bound)) - 14.0, -120.0, 120.0)
    scaled = (parts * jnp.exp2(-power)).astype(half)
    return jnp.concatenate([scaled, jnp.broadcast_to(power.astype(half), parts.shape[:-1] + (LANES,))], axis=-1)


def unpack_half(message):
    width = message.shape[-1] - LANES
    return message[..., :width].astype(jnp.float32) * jnp.exp2(message[..., width : width + 1].astype(jnp.float32))


def gather_near(block, axis):
    return jnp.stack([block] + [shift(block, axis, turn) for turn in range(1, lax.axis_size(axis))])


def send_near(stacked, axis):
    return [shift(stacked[turn], axis, lax.axis_size(axis) - turn) for turn in range(1, lax.axis_size(axis))]


def gather_direct(block, axis):
    size, here = lax.axis_size(axis), lax.axis_index(axis)
    arrived = [block] + [shift(block, axis, turn) for turn in range(1, size)]
    result = jnp.stack(arrived)
    return jnp.take(result, (here + size - jnp.arange(size)) % size, axis=0)


def sum_near(stacked, axis):
    total = stacked
    for turn in range(1, lax.axis_size(axis)):
        total = total + jnp.roll(shift(stacked, axis, turn), turn, axis=0)
    return total


def gather_bits(block, axis):
    here = lax.axis_index(axis)
    result, bit = block[None], 1
    while bit < lax.axis_size(axis):
        other = swap(result, axis, bit)
        upper = (here & bit) > 0
        result = jnp.concatenate(
            [jnp.where(upper, other, result), jnp.where(upper, result, other)], axis=0
        )
        bit *= 2
    return result


def scatter_bits(stacked, axis):
    here, size = lax.axis_index(axis), lax.axis_size(axis)
    bit = 1
    rest = stacked
    while bit < size:
        pairs = rest.reshape((rest.shape[0] // 2, 2) + rest.shape[1:])
        own = (here & bit) // bit
        keep = lax.dynamic_index_in_dim(pairs, own, 1, keepdims=False)
        send = lax.dynamic_index_in_dim(pairs, 1 - own, 1, keepdims=False)
        rest = keep + swap(send, axis, bit)
        bit *= 2
    return rest[0]


def halves(value):
    high = value.astype(low)
    return high, (value - high.astype(jnp.float32)).astype(low)


def product(left, right, right_dim=0):
    dims = (((1,), (right_dim,)), ((), ()))

    def one(a, b):
        return lax.dot_general(a, b, dims, preferred_element_type=jnp.float32)

    return one(left[0], right[0]) + (one(left[0], right[1]) + one(left[1], right[0]))


def exact_dot(left, right):
    return jnp.dot(left, right, precision=highest, preferred_element_type=jnp.float32)


def softplus(value):
    small = jnp.exp(-jnp.abs(value))
    ratio = small / (2.0 + small)
    square = ratio * ratio
    series = jnp.full_like(square, 1.0 / 17.0)
    for power in (15, 13, 11, 9, 7, 5, 3, 1):
        series = series * square + 1.0 / power
    return jnp.maximum(value, 0.0) + 2.0 * ratio * series


def lane_of_head(pair, base, transposed=False):
    shape = (LANES, LANES)
    head = lax.broadcasted_iota(jnp.int32, shape, 1 if transposed else 0)
    lane = lax.broadcasted_iota(jnp.int32, shape, 0 if transposed else 1)
    return (head == base + 2 * pair + lane // HDIM).astype(jnp.float32)


def taps_of(extended, size, kernel, offset):
    total = offset + kernel[0:1] * extended[pl.ds(8 - CONVW + 1, size), :]
    for index in range(1, CONVW):
        total = total + kernel[index : index + 1] * extended[pl.ds(8 - CONVW + 1 + index, size), :]
    return total


def step_sizes(raw, heads):
    delta = softplus(raw + heads[0:1])
    change = -delta * jnp.exp(heads[1:2])
    size = raw.shape[0]
    below = lax.broadcasted_iota(jnp.int32, (size, size), 0) >= lax.broadcasted_iota(jnp.int32, (size, size), 1)
    return delta, change, exact_dot(below.astype(jnp.float32), change)


def forward_kernel(
    table_ref, z_ref, x_ref, shared_ref, step_ref, chan_ref, shared_chan_ref, head_ref,
    gated_ref, mixed_ref, state_ref, square_ref,
    tails, shared_tail, states,
    extended, shared_extended, meet, read_high, read_low, keys_high, keys_low,
    delta_all, run_all, run_rows,
):
    chunk, pair = pl.program_id(0), pl.program_id(1)
    size = x_ref.shape[0]
    base = table_ref[pl.num_programs(0)]

    @pl.when(pair == 0)
    def _():
        @pl.when(chunk == 0)
        def _():
            shared_tail[...] = jnp.zeros_like(shared_tail)
            tails[...] = jnp.zeros_like(tails)
            states[...] = jnp.zeros_like(states)

        shared_extended[0:8, :] = shared_tail[...]
        shared_extended[8:, :] = shared_ref[...]
        shared_tail[...] = shared_ref[size - 8 :, :]
        pre = taps_of(shared_extended, size, shared_chan_ref[...], shared_chan_ref[4:5, :])
        active = pre * jax.nn.sigmoid(pre)
        keys, read = halves(active[:, :NST]), halves(active[:, NST:])
        meet[...] = product(read, keys, 1)
        read_high[...], read_low[...] = read
        keys_high[...], keys_low[...] = halves(active[:, :NST].T)
        delta, _, running = step_sizes(step_ref[...], head_ref[...])
        delta_all[...] = delta
        run_all[...] = running
        run_rows[...] = running.T
        square_ref[...] = jnp.zeros_like(square_ref)

    chan = chan_ref[...]
    extended[0:8, :] = tails[pair]
    extended[8:, :] = x_ref[...]
    tails[pair] = x_ref[size - 8 :, :]
    pre = taps_of(extended, size, chan, chan[4:5])
    values = pre * jax.nn.sigmoid(pre)
    lanes = lane_of_head(pair, base)
    delta = exact_dot(delta_all[...], lanes)
    running = exact_dot(run_all[...], lanes)
    stepped = delta * values
    causal = lax.broadcasted_iota(jnp.int32, (size, size), 0) >= lax.broadcasted_iota(jnp.int32, (size, size), 1)
    locals_ = []
    for side in range(2):
        column = running[:, side * HDIM : side * HDIM + 1]
        row = run_rows[pl.ds(base + 2 * pair + side, 1), :]
        decay = jnp.exp(jnp.where(causal, column - row, -1e30))
        mixing = halves(decay * meet[...])
        locals_.append(product(mixing, halves(stepped[:, side * HDIM : (side + 1) * HDIM])))
    state = states[pair]
    state_ref[0, 0] = state
    carried = product((read_high[...], read_low[...]), halves(state))
    scanned = jnp.concatenate(locals_, axis=1) + jnp.exp(running) * carried
    last = running[size - 1 :, :]
    tail = halves(stepped * jnp.exp(last - running))
    states[pair] = jnp.exp(last) * state + product((keys_high[...], keys_low[...]), tail)
    mixed = scanned + chan[5:6] * values
    z = z_ref[...]
    gated = mixed * (z * jax.nn.sigmoid(z))
    mixed_ref[...] = mixed
    gated_ref[...] = gated
    square_ref[...] += gated * gated


def gate_kernel(
    z_ref, gated_ref, mixed_ref, up_ref, chan_ref, stats_ref,
    z_grad_ref, mix_grad_ref, square_ref, gain_grad_ref,
):
    @pl.when(pl.program_id(0) == 0)
    def _():
        gain_grad_ref[...] = jnp.zeros_like(gain_grad_ref)

    stats = stats_ref[...].T
    scale, pull = stats[:, 0:1], stats[:, 1:2]
    z, gated = z_ref[...], gated_ref[...]
    scaled = up_ref[...] * scale
    z_gain = jax.nn.sigmoid(z)
    gated_grad = scaled * chan_ref[6:7, :] - gated * pull
    z_gate = gated_grad * z_gain
    mix_grad_ref[...] = z_gate * z
    z_grad = (z_gate * mixed_ref[...] * (1.0 + z * (1.0 - z_gain))).astype(z_grad_ref.dtype)
    z_grad_ref[...] = z_grad
    wide_grad = z_grad.astype(jnp.float32)
    square_ref[...] = jnp.sum(wide_grad * wide_grad, axis=1, keepdims=True)
    gain_grad_ref[0:1, :] += jnp.sum(scaled * gated, axis=0, keepdims=True)


def backward_kernel(
    first, chunks, table_ref, x_ref, x_before_ref, shared_ref, shared_before_ref, step_ref, chan_ref, shared_chan_ref, head_ref,
    mixed_ref, mix_grad_ref, state_ref, state_after_ref, carried_in, *refs
):
    carried_in = (carried_in,) + refs[:5]
    (
        x_grad_ref, square_ref, shared_grad_ref,
        state_grads, heads_after, shared_after, chan_grad_ref, shared_chan_grad_ref, head_grad_ref,
        extended, shared_extended, later, shared_later, shared_pre,
        meet, read_high, read_low, keys_high, keys_low, read_rows_high, read_rows_low,
        delta_all, change_all, run_all, run_rows, meet_grad, keys_grad, read_grad, run_grad, delta_grad, last_grad,
    ) = refs[-31:]
    carried_out = (state_grads, heads_after, shared_after, chan_grad_ref, shared_chan_grad_ref, head_grad_ref)
    pair, pairs = pl.program_id(0), pl.num_programs(0)
    size = x_ref.shape[0]
    base = table_ref[chunks]

    @pl.when(pair == 0)
    def _():
        for new, old in zip(carried_out, carried_in):
            new[...] = old[...]

        shared_extended[0:8, :] = jnp.zeros(shared_before_ref.shape, jnp.float32) if first else shared_before_ref[...]
        shared_extended[8:, :] = shared_ref[...]
        pre = taps_of(shared_extended, size, shared_chan_ref[...], shared_chan_ref[4:5, :])
        shared_pre[...] = pre
        active = pre * jax.nn.sigmoid(pre)
        keys, read = halves(active[:, :NST]), halves(active[:, NST:])
        meet[...] = product(keys, read, 1)
        read_high[...], read_low[...] = read
        keys_high[...], keys_low[...] = keys
        read_rows_high[...], read_rows_low[...] = halves(active[:, NST:].T)
        delta, change, running = step_sizes(step_ref[...], head_ref[...])
        delta_all[...] = delta
        change_all[...] = change
        run_all[...] = running
        run_rows[...] = running.T
        meet_grad[...] = jnp.zeros_like(meet_grad)
        keys_grad[...] = jnp.zeros_like(keys_grad)
        read_grad[...] = jnp.zeros_like(read_grad)
        run_grad[...] = jnp.zeros_like(run_grad)
        delta_grad[...] = jnp.zeros_like(delta_grad)
        last_grad[...] = jnp.zeros_like(last_grad)
        square_ref[...] = jnp.zeros_like(square_ref)

    chan = chan_ref[...]
    extended[0:8, :] = jnp.zeros(x_before_ref.shape, jnp.float32) if first else x_before_ref[...]
    extended[8:, :] = x_ref[...]
    pre = taps_of(extended, size, chan, chan[4:5])
    gain = jax.nn.sigmoid(pre)
    values = pre * gain
    lanes = lane_of_head(pair, base)
    delta = exact_dot(delta_all[...], lanes)
    running = exact_dot(run_all[...], lanes)
    stepped = delta * values

    mixed, mix_grad = mixed_ref[...], mix_grad_ref[...]
    last = running[size - 1 :, :]
    fall = jnp.exp(last - running)
    rise = jnp.exp(running)
    state, state_grad = state_ref[0, 0], state_grads[pair]
    state_halves, state_grad_halves = halves(state), halves(state_grad)
    keys = (keys_high[...], keys_low[...])
    stepped_grad = fall * product(keys, state_grad_halves)
    keys_grad[...] += product(halves(stepped * fall), state_grad_halves, 1)
    risen = halves(mix_grad * rise)
    read_grad[...] += product(risen, state_halves, 1)
    ended = jnp.sum(state_grad * state_after_ref[0, 0], axis=0, keepdims=True)
    state_grads[pair] = jnp.exp(last) * state_grad + product((read_rows_high[...], read_rows_low[...]), risen)

    causal = lax.broadcasted_iota(jnp.int32, (size, size), 0) <= lax.broadcasted_iota(jnp.int32, (size, size), 1)
    parts = []
    for side in range(2):
        own = slice(side * HDIM, (side + 1) * HDIM)
        column = running[:, side * HDIM : side * HDIM + 1]
        row = run_rows[pl.ds(base + 2 * pair + side, 1), :]
        decay = jnp.exp(jnp.where(causal, row - column, -1e30))
        mixing = halves(decay * meet[...])
        grad_halves = halves(mix_grad[:, own])
        parts.append(product(mixing, grad_halves))
        meet_grad[...] += decay * product(halves(stepped[:, own]), grad_halves, 1)
    stepped_grad = stepped_grad + jnp.concatenate(parts, axis=1)
    to_head = lane_of_head(pair, base, transposed=True)
    scanned = mixed - chan[5:6] * values
    run_grad[...] += exact_dot(mix_grad * scanned - stepped * stepped_grad, to_head)
    delta_grad[...] += exact_dot(values * stepped_grad, to_head)
    last_grad[0:1, :] += exact_dot(jnp.broadcast_to(ended, (8, LANES)), to_head)[0:1]

    values_grad = chan[5:6] * mix_grad + delta * stepped_grad
    pre_grad = values_grad * (gain * (1.0 + pre * (1.0 - gain)))
    later[0:size, :] = pre_grad
    later[size:, :] = heads_after[pair]
    heads_after[pair] = pre_grad[0:8]
    x_grad = chan[0:1] * later[pl.ds(CONVW - 1, size), :]
    for index in range(1, CONVW):
        x_grad = x_grad + chan[index : index + 1] * later[pl.ds(CONVW - 1 - index, size), :]
    x_grad = x_grad.astype(x_grad_ref.dtype)
    x_grad_ref[:, pl.ds(pl.multiple_of(pair * LANES, LANES), LANES)] = x_grad
    wide_grad = x_grad.astype(jnp.float32)
    square_ref[...] += wide_grad * wide_grad
    for index in range(CONVW):
        seen = extended[pl.ds(8 - CONVW + 1 + index, size), :]
        chan_grad_ref[pair, index : index + 1, :] += jnp.sum(pre_grad * seen, axis=0, keepdims=True)
    chan_grad_ref[pair, 4:5, :] += jnp.sum(pre_grad, axis=0, keepdims=True)
    chan_grad_ref[pair, 5:6, :] += jnp.sum(mix_grad * values, axis=0, keepdims=True)

    @pl.when(pair == pairs - 1)
    def _():
        meet_halves = halves(meet_grad[...])
        keys_all = keys_grad[...] + product(meet_halves, (read_high[...], read_low[...]))
        read_all = read_grad[...] + product(halves(meet_grad[...].T), (keys_high[...], keys_low[...]))
        pre_s = shared_pre[...]
        gain_s = jax.nn.sigmoid(pre_s)
        chan_s = shared_chan_ref[...]
        grad_s = jnp.concatenate([keys_all, read_all], axis=1) * (gain_s * (1.0 + pre_s * (1.0 - gain_s)))
        shared_later[0:size, :] = grad_s
        shared_later[size:, :] = shared_after[...]
        shared_after[...] = grad_s[0:8]
        out = chan_s[0:1] * shared_later[pl.ds(CONVW - 1, size), :]
        for index in range(1, CONVW):
            out = out + chan_s[index : index + 1] * shared_later[pl.ds(CONVW - 1 - index, size), :]
        shared_grad_ref[...] = out
        for index in range(CONVW):
            seen = shared_extended[pl.ds(8 - CONVW + 1 + index, size), :]
            shared_chan_grad_ref[index : index + 1, :] += jnp.sum(grad_s * seen, axis=0, keepdims=True)
        shared_chan_grad_ref[4:5, :] += jnp.sum(grad_s, axis=0, keepdims=True)

        above = lax.broadcasted_iota(jnp.int32, (size, size), 0) <= lax.broadcasted_iota(jnp.int32, (size, size), 1)
        change_grad = exact_dot(above.astype(jnp.float32), run_grad[...]) + last_grad[0:1, :]
        rate = jnp.exp(head_ref[1:2, :])
        raw = step_ref[...] + head_ref[0:1, :]
        raw_grad = (delta_grad[...] - change_grad * rate) * jax.nn.sigmoid(raw)
        raw_low = raw_grad.astype(x_grad_ref.dtype)
        x_grad_ref[:, x_grad_ref.shape[1] - LANES :] = raw_low
        wide_raw = raw_low.astype(jnp.float32)
        square_ref[...] += wide_raw * wide_raw
        head_grad_ref[0:1, :] += jnp.sum(raw_grad, axis=0, keepdims=True)
        head_grad_ref[1:2, :] += jnp.sum(change_grad * change_all[...], axis=0, keepdims=True)


def run_forward(table, projected, chan, shared_chan, head_rows):
    length, wide = projected.shape[0], chan.shape[1]
    chunks, pairs = length // SPAN, wide // LANES
    f32 = jnp.float32
    block = pl.BlockSpec((SPAN, LANES), lambda c, p, t: (t[c], p))
    return pl.pallas_call(
        forward_kernel,
        grid_spec=pltpu.PrefetchScalarGridSpec(
            num_scalar_prefetch=1,
            grid=(chunks, pairs),
            in_specs=[
                block,
                pl.BlockSpec((SPAN, LANES), lambda c, p, t: (t[c], pairs + 2 + p)),
                pl.BlockSpec((SPAN, 2 * NST), lambda c, p, t: (t[c], pairs // 2)),
                pl.BlockSpec((SPAN, LANES), lambda c, p, t: (t[c], 2 * pairs + 2)),
                pl.BlockSpec((8, LANES), lambda c, p, t: (0, p)),
                pl.BlockSpec((8, 2 * NST), lambda c, p, t: (0, 0)),
                pl.BlockSpec((8, LANES), lambda c, p, t: (0, 0)),
            ],
            out_specs=[
                block,
                block,
                pl.BlockSpec((1, 1, NST, LANES), lambda c, p, t: (c, p, 0, 0)),
                pl.BlockSpec((SPAN, LANES), lambda c, p, t: (t[c], 0)),
            ],
            scratch_shapes=[
                pltpu.VMEM((pairs, 8, LANES), f32),
                pltpu.VMEM((8, 2 * NST), f32),
                pltpu.VMEM((pairs, NST, LANES), f32),
                pltpu.VMEM((SPAN + 8, LANES), f32),
                pltpu.VMEM((SPAN + 8, 2 * NST), f32),
                pltpu.VMEM((SPAN, SPAN), f32),
                pltpu.VMEM((SPAN, NST), low),
                pltpu.VMEM((SPAN, NST), low),
                pltpu.VMEM((NST, SPAN), low),
                pltpu.VMEM((NST, SPAN), low),
                pltpu.VMEM((SPAN, LANES), f32),
                pltpu.VMEM((SPAN, LANES), f32),
                pltpu.VMEM((LANES, SPAN), f32),
            ],
        ),
        out_shape=[
            jax.ShapeDtypeStruct((length, wide), f32),
            jax.ShapeDtypeStruct((length, wide), f32),
            jax.ShapeDtypeStruct((chunks, pairs, NST, LANES), f32),
            jax.ShapeDtypeStruct((length, LANES), f32),
        ],
        name="mixer_forward",
    )(table, projected, projected, projected, projected, chan, shared_chan, head_rows)


def run_gate(projected, gated, mixed, up, chan, stats):
    length, wide = gated.shape
    f32 = jnp.float32
    size = SPAN // 2
    block = pl.BlockSpec((size, wide), lambda c: (c, 0))
    whole = pl.BlockSpec((8, wide), lambda c: (0, 0))
    return pl.pallas_call(
        gate_kernel,
        grid=(length // size,),
        in_specs=[block, block, block, block, whole, pl.BlockSpec((8, size), lambda c: (0, c))],
        out_specs=[block, block, pl.BlockSpec((size, 1), lambda c: (c, 0)), whole],
        out_shape=[
            jax.ShapeDtypeStruct((length, wide), low),
            jax.ShapeDtypeStruct((length, wide), f32),
            jax.ShapeDtypeStruct((length, 1), f32),
            jax.ShapeDtypeStruct((8, wide), f32),
        ],
        name="gate_backward",
    )(projected, gated, mixed, up, chan, stats)


def run_backward(chunk, table, projected, chan, shared_chan, head_rows, mixed, mix_grad, states, carried, before):
    length, wide = projected.shape[0], chan.shape[1]
    chunks, pairs = length // SPAN, wide // LANES
    f32 = jnp.float32
    lines = SPAN // 8
    earlier, following = max(chunk - 1, 0), min(chunk + 1, chunks - 1)
    block = pl.BlockSpec((SPAN, LANES), lambda p, t: (t[chunk], p))
    flat = pl.BlockSpec((8, 2 * NST), lambda p, t: (0, 0))
    head = pl.BlockSpec((8, LANES), lambda p, t: (0, 0))
    carries = [
        pl.BlockSpec((pairs, NST, LANES), lambda p, t: (0, 0, 0)),
        pl.BlockSpec((pairs, 8, LANES), lambda p, t: (0, 0, 0)),
        flat,
        pl.BlockSpec((pairs, 8, LANES), lambda p, t: (0, 0, 0)),
        flat,
        head,
    ]
    carried_shapes = [jax.ShapeDtypeStruct(c.shape, f32) for c in carried]
    return pl.pallas_call(
        functools.partial(backward_kernel, chunk == 0, chunks),
        grid_spec=pltpu.PrefetchScalarGridSpec(
            num_scalar_prefetch=1,
            grid=(pairs,),
            in_specs=[
                pl.BlockSpec((SPAN, LANES), lambda p, t: (t[chunk], pairs + 2 + p)),
                pl.BlockSpec((8, LANES), lambda p, t: (t[earlier] * lines + lines - 1, pairs + 2 + p)),
                pl.BlockSpec((SPAN, 2 * NST), lambda p, t: (t[chunk], pairs // 2)),
                pl.BlockSpec((8, 2 * NST), lambda p, t: (t[earlier] * lines + lines - 1, pairs // 2)),
                pl.BlockSpec((SPAN, LANES), lambda p, t: (t[chunk], 2 * pairs + 2)),
                pl.BlockSpec((8, LANES), lambda p, t: (0, p)),
                flat,
                head,
                block,
                block,
                pl.BlockSpec((1, 1, NST, LANES), lambda p, t: (chunk, p, 0, 0)),
                pl.BlockSpec((1, 1, NST, LANES), lambda p, t: (following, p, 0, 0)),
            ]
            + carries
            + [pl.BlockSpec(memory_space=pl.ANY)] * len(before),
            out_specs=[
                pl.BlockSpec((SPAN, wide + LANES), lambda p, t: (t[chunk], 0)),
                pl.BlockSpec((SPAN, LANES), lambda p, t: (t[chunk], 0)),
                pl.BlockSpec((SPAN, 2 * NST), lambda p, t: (t[chunk], 0)),
            ]
            + carries,
            scratch_shapes=[
                pltpu.VMEM((SPAN + 8, LANES), f32),
                pltpu.VMEM((SPAN + 8, 2 * NST), f32),
                pltpu.VMEM((SPAN + 8, LANES), f32),
                pltpu.VMEM((SPAN + 8, 2 * NST), f32),
                pltpu.VMEM((SPAN, 2 * NST), f32),
                pltpu.VMEM((SPAN, SPAN), f32),
                pltpu.VMEM((SPAN, NST), low),
                pltpu.VMEM((SPAN, NST), low),
                pltpu.VMEM((SPAN, NST), low),
                pltpu.VMEM((SPAN, NST), low),
                pltpu.VMEM((NST, SPAN), low),
                pltpu.VMEM((NST, SPAN), low),
                pltpu.VMEM((SPAN, LANES), f32),
                pltpu.VMEM((SPAN, LANES), f32),
                pltpu.VMEM((SPAN, LANES), f32),
                pltpu.VMEM((LANES, SPAN), f32),
                pltpu.VMEM((SPAN, SPAN), f32),
                pltpu.VMEM((SPAN, NST), f32),
                pltpu.VMEM((SPAN, NST), f32),
                pltpu.VMEM((SPAN, LANES), f32),
                pltpu.VMEM((SPAN, LANES), f32),
                pltpu.VMEM((8, LANES), f32),
            ],
        ),
        out_shape=[
            jax.ShapeDtypeStruct((length, wide + LANES), low),
            jax.ShapeDtypeStruct((length, LANES), f32),
            jax.ShapeDtypeStruct((length, 2 * NST), f32),
        ]
        + carried_shapes,
        input_output_aliases={19 + k: k for k in range(len(before))},
        name="mixer_backward",
    )(
        table, projected, projected, projected, projected, projected, chan, shared_chan, head_rows,
        mixed, mix_grad, states, states, *carried, *before,
    )


def halve(block, left, bit, axis):
    place = left.index(bit)
    own = (lax.axis_index(axis) & bit) // bit
    keep = lax.dynamic_index_in_dim(block, own, place, keepdims=False)
    send = lax.dynamic_index_in_dim(block, 1 - own, place, keepdims=False)
    return keep + swap(send, axis, bit), [b for b in left if b != bit]


class Scatter:
    def __init__(self, arrays, axis):
        self.axis = axis
        size = lax.axis_size(axis)
        bits = [1 << k for k in range(size.bit_length() - 1)]
        upper = bits[1:]
        turned = upper[len(upper) // 2 :] + upper[: len(upper) // 2]
        self.orders = [bits[:1] + (upper if k % 2 == 0 else turned) for k in range(len(arrays))]
        self.left = [bits[::-1] for _ in arrays]
        self.blocks = [
            a.reshape((2,) * len(bits) + (a.shape[0] // size,) + a.shape[1:]) for a in arrays
        ]
        self.steps = len(bits)
        self.done = 0

    def step(self):
        for k in range(len(self.blocks)):
            self.blocks[k], self.left[k] = halve(
                self.blocks[k], self.left[k], self.orders[k][self.done], self.axis
            )
        self.done += 1

    def finish(self):
        while self.done < self.steps:
            self.step()
        return self.blocks


def adamw_update(param, grad, first, second, rate, decay):
    first_new = beta_one * first + (1.0 - beta_one) * grad
    second_new = beta_two * second + (1.0 - beta_two) * grad * grad
    corrected_first = first_new / (1.0 - beta_one**adam_step)
    corrected_second = second_new / (1.0 - beta_two**adam_step)
    param_new = param - rate * (
        corrected_first / (jnp.sqrt(corrected_second) + adam_eps) + decay * param
    )
    return (param_new, first_new, second_new)


def dot(left, right):
    return jnp.dot(left, right, preferred_element_type=jnp.float32)


def body(
    block_input,
    cotangent,
    norm_gain,
    in_weight,
    conv_weight,
    conv_bias,
    step_bias,
    decay_log,
    skip_gain,
    gated_gain,
    out_weight,
    first_norm_gain,
    second_norm_gain,
    first_in_weight,
    second_in_weight,
    first_conv_weight,
    second_conv_weight,
    first_conv_bias,
    second_conv_bias,
    first_step_bias,
    second_step_bias,
    first_decay_log,
    second_decay_log,
    first_skip_gain,
    second_skip_gain,
    first_gated_gain,
    second_gated_gain,
    first_out_weight,
    second_out_weight,
):
    ranks, rank = lax.axis_size("seq"), lax.axis_index("seq")
    groups = lax.axis_size("dp")
    devices = ranks * groups
    wide, heads = E // ranks, NHEADS // ranks
    rows = in_weight.shape[0]
    width = rows * devices
    taps = conv_bias.shape[0]
    channels = taps * devices
    step_at = 2 * E + 2 * NST
    spare = LANES - (in_weight.shape[1] - step_at)

    packed = jnp.concatenate(
        [norm_gain, conv_weight.reshape(-1), conv_bias, gated_gain]
    ).astype(low).astype(jnp.float32)
    gains = gated_gain.shape[0]
    filled = packed.shape[0]
    lines = -(-filled // LANES)
    packed = jnp.pad(packed, (0, lines * LANES - filled)).reshape(lines, LANES)
    small_line = gather_direct(packed, "seq")
    small = gather_bits(small_line, "dp")
    small = small.reshape(devices, lines * LANES)
    norm_float = small[:, :rows].reshape(-1)
    kernel_float = small[:, rows : rows + CONVW * taps].reshape(devices, CONVW, taps)
    kernel_float = kernel_float.transpose(1, 0, 2).reshape(CONVW, channels)
    offset_float = small[:, rows + CONVW * taps : rows + (CONVW + 1) * taps].reshape(-1)
    gated_float = small[:, rows + (CONVW + 1) * taps : filled].reshape(-1)
    kernel_own = lax.dynamic_slice_in_dim(kernel_float, rank * wide, wide, 1)
    offset_own = lax.dynamic_slice_in_dim(offset_float, rank * wide, wide, 0)
    gated_own = lax.dynamic_slice_in_dim(gated_float, rank * wide, wide, 0)
    skip_own = lax.dynamic_slice_in_dim(skip_gain, rank * heads, heads, 0)

    in_low = after(in_weight.astype(low), small_line)
    out_low = after(out_weight.astype(low), small_line)

    def for_rank(j):
        return jnp.concatenate(
            [
                lax.dynamic_slice_in_dim(in_low, j * wide, wide, 1),
                in_low[:, 2 * E : step_at],
                lax.dynamic_slice_in_dim(in_low, E + j * wide, wide, 1),
                jnp.pad(in_low[:, step_at:], ((0, 0), (0, spare))),
                lax.dynamic_slice_in_dim(out_low, j * wide, wide, 1),
            ],
            axis=1,
        )

    columns = 2 * NST + 2 * wide + LANES
    weights_arrived = []
    for turn in range(1, ranks):
        weights_arrived.append(shift(for_rank((rank + turn) % ranks), "seq", turn))

    tokens, upstream = block_input[0], cotangent[0]
    span = tokens.shape[0]
    length = span * ranks
    inverse = lax.rsqrt(jnp.mean(tokens * tokens, axis=-1, keepdims=True) + norm_eps)
    hidden_own = (tokens * inverse * norm_float).astype(low)
    weights_arrived = [after(part, hidden_own) for part in weights_arrived]
    weight_rows = jnp.zeros((ranks, rows, columns + wide), low)
    weight_rows = lax.dynamic_update_index_in_dim(weight_rows, for_rank(rank), rank, 0)
    for turn in range(1, ranks):
        weight_rows = lax.dynamic_update_index_in_dim(
            weight_rows, weights_arrived[turn - 1], (rank + ranks - turn) % ranks, 0
        )
    weight_rows = weight_rows.reshape(ranks * rows, columns + wide)
    in_full = lax.all_gather(weight_rows[:, :columns], "dp", axis=0, tiled=True)
    out_full = lax.all_gather(weight_rows[:, columns:], "dp", axis=0, tiled=True)

    hidden = gather_near(hidden_own, "seq").reshape(length, width)
    upstream_low = gather_near(after(upstream.astype(low), hidden), "seq").reshape(length, width)

    projected = dot(hidden, in_full)
    none = jnp.zeros((1, wide), jnp.float32)
    chan = jnp.concatenate(
        [kernel_own, offset_own[None], jnp.repeat(skip_own, HDIM)[None], gated_own[None], none], axis=0
    )
    shared_chan = jnp.concatenate(
        [kernel_float[:, E:], offset_float[None, E:], jnp.zeros((3, 2 * NST), jnp.float32)], axis=0
    )
    head_rows = jnp.pad(jnp.stack([step_bias, decay_log]), ((0, 6), (0, LANES - NHEADS)))
    pairs, chunks = wide // LANES, length // SPAN
    per_rank = span // SPAN
    order = jnp.arange(chunks, dtype=jnp.int32)
    order = (rank + ranks - order // per_rank) % ranks * per_rank + order % per_rank
    table = jnp.concatenate([order, jnp.reshape(rank * heads, (1,))]).astype(jnp.int32)
    zeros = functools.partial(jnp.zeros, dtype=jnp.float32)
    gated, mixed, states, squares = run_forward(table, projected, chan, shared_chan, head_rows)
    packed_length = (ranks, span // LANES, LANES)
    square_sum = sum_near(jnp.sum(squares, axis=1).reshape(packed_length), "seq").reshape(length)
    scale = lax.rsqrt(square_sum / E + norm_eps)
    normed_low = (gated * scale[:, None] * gated_own).astype(low)
    branch_factor = 2.0 ** (14 - math.ceil(math.log2(0.17 * math.sqrt(E * wide))))
    out_half = (dot(normed_low, out_full.T) * branch_factor).astype(half).reshape(ranks, span, width)
    branch = tokens + dot(normed_low[:span], out_full.T)

    normed_grad = dot(upstream_low, out_full)
    pull_sum = jnp.sum(normed_grad * gated_own * gated, axis=1).reshape(packed_length)
    pull_sum = sum_near(pull_sum, "seq").reshape(length)
    stats = jnp.stack([scale, scale * scale * scale * (pull_sum / E)])
    stats = jnp.pad(stats, ((0, 6), (0, 0)))
    gate_low, mix_grad, gate_square, gain_rows = run_gate(projected, gated, mixed, normed_grad, chan, stats)
    gated_grad = gain_rows[0]

    branch_parts = send_near(after(out_half, pull_sum), "seq")

    early = Scatter([dot(upstream_low.T, normed_low), dot(hidden.T, gate_low)], "dp")
    carried = (
        zeros((pairs, NST, LANES)), zeros((pairs, 8, LANES)), zeros((8, 2 * NST)),
        zeros((pairs, 8, LANES)), zeros((8, 2 * NST)), zeros((8, LANES)),
    )
    outputs = ()
    ready = (branch,)
    for turn in range(chunks):
        if early.done < early.steps and turn != 2:
            early.step()
        mix_grad = after(mix_grad, *ready)
        result = run_backward(
            chunks - 1 - turn, table, projected, chan, shared_chan, head_rows, mixed, mix_grad, states, carried, outputs
        )
        outputs, carried = tuple(result[:3]), tuple(result[3:])
        ready = tuple(early.blocks) if turn != 1 else ()
    conv_low, conv_square, shared_grad = outputs
    _, _, _, chan_grad, shared_chan_grad, head_grad = carried
    early.finish()

    shared_parts = shared_grad.reshape(ranks, span, 2 * NST)
    shared_sent = send_near(shared_parts, "seq")

    hidden_part = dot(gate_low, in_full[:, :wide].T) + dot(conv_low, in_full[:, wide + 2 * NST :].T)
    row_bound = 0.1565 * math.sqrt(2 * wide + NHEADS) * jnp.sqrt(gate_square + jnp.sum(conv_square, axis=1, keepdims=True))
    hidden_part = hidden_part.reshape(ranks, span, width)
    hidden_half = pack_half(hidden_part, row_bound.reshape(ranks, span, 1))
    hidden_parts = send_near(hidden_half, "seq")

    split = 4 * LANES
    conv_parts = [dot(hidden.T, conv_low[:, :split]), dot(hidden.T, conv_low[:, split:])]
    for part in branch_parts:
        branch = branch + part.astype(jnp.float32) * (1.0 / branch_factor)
    block_output = branch[None]

    shared_own = shared_parts[0]
    for part in shared_sent:
        shared_own = shared_own + part
    shared_own = shared_own.astype(low)
    late = Scatter(conv_parts + [dot(hidden_own.T, shared_own)], "dp")
    late.finish()

    chan_grad = chan_grad.transpose(1, 0, 2).reshape(8, wide)
    kernel_grad, offset_grad = chan_grad[:CONVW], chan_grad[4]
    skip_grad = jnp.sum(chan_grad[5].reshape(heads, HDIM), axis=1)
    kernel_shared_grad, offset_shared_grad = shared_chan_grad[:CONVW], shared_chan_grad[4]

    sums_all = jnp.concatenate(
        [block.reshape(ranks, rows, -1) for block in (late.blocks + early.blocks)], axis=2
    )
    conv_wide = wide + LANES
    packed_sums = pack_half(sums_all, jnp.max(jnp.abs(sums_all), axis=-1, keepdims=True))
    hidden_parts = [after(part, packed_sums) for part in hidden_parts]
    collected = sums_all
    for turn in range(1, ranks):
        arrived = shift(pick(packed_sums, (rank + turn) % ranks), "seq", turn)
        collected = lax.dynamic_update_index_in_dim(
            collected, unpack_half(arrived), (rank + ranks - turn) % ranks, 0
        )
    at = conv_wide + 2 * NST
    shared_sum = sum(collected[j, :, wide:at] for j in range(ranks))
    grad_in_weight = jnp.concatenate(
        [collected[j, :, at + wide :] for j in range(ranks)]
        + [collected[j, :, :wide] for j in range(ranks)]
        + [shared_sum[:, LANES:], shared_sum[:, : LANES - spare]],
        axis=1,
    )
    grad_out_weight = jnp.concatenate([collected[j, :, at : at + wide] for j in range(ranks)], axis=1)

    hidden_grad = hidden_part[0] + dot(shared_own, in_full[:, wide : wide + 2 * NST].T)
    for part in hidden_parts:
        hidden_grad = hidden_grad + unpack_half(part)
    scaled = tokens * inverse
    gain_grad = jnp.sum(hidden_grad * scaled, axis=0)
    inner = hidden_grad * norm_float
    token_grad = inverse * (inner - scaled * jnp.mean(inner * scaled, axis=-1, keepdims=True))
    input_grad = (upstream + token_grad)[None]

    def placed(own, shared):
        full = jnp.zeros(own.shape[:-1] + (E,), jnp.float32)
        full = lax.dynamic_update_slice_in_dim(full, own, rank * wide, own.ndim - 1)
        return jnp.concatenate([full, shared], axis=-1)

    kernel_all = placed(kernel_grad, kernel_shared_grad).reshape(CONVW, devices, taps)
    kernel_all = kernel_all.transpose(1, 0, 2).reshape(devices, CONVW * taps)
    offset_all = placed(offset_grad, offset_shared_grad).reshape(devices, taps)
    gated_all = lax.dynamic_update_slice_in_dim(jnp.zeros((E,), jnp.float32), gated_grad, rank * wide, 0)
    skip_all = lax.dynamic_update_slice_in_dim(jnp.zeros((NHEADS,), jnp.float32), skip_grad, rank * heads, 0)
    head_all = jnp.concatenate([head_grad[0, :NHEADS], head_grad[1, :NHEADS], skip_all])
    terms = jnp.concatenate(
        [
            gain_grad.reshape(devices, rows),
            kernel_all,
            offset_all,
            gated_all.reshape(devices, gains),
            jnp.broadcast_to(head_all[None], (devices, 3 * NHEADS)),
        ],
        axis=1,
    )
    used = terms.shape[1]
    term_lines = -(-used // LANES)
    terms = jnp.pad(terms, ((0, 0), (0, term_lines * LANES - used)))
    terms = terms.reshape(groups, ranks * term_lines, LANES)
    summed = scatter_bits(terms, "dp").reshape(ranks, term_lines, LANES)
    summed = exchange_sum(summed, "seq").reshape(-1)
    grad_norm_gain = summed[:rows]
    at = rows
    grad_conv_weight = summed[at : at + CONVW * taps].reshape(CONVW, taps)
    at += CONVW * taps
    grad_conv_bias = summed[at : at + taps]
    at += taps
    grad_gated_gain = summed[at : at + gains]
    at += gains
    grad_step_bias, grad_decay_log, grad_skip_gain = (
        summed[at + k * NHEADS : at + (k + 1) * NHEADS] for k in range(3)
    )
    new_norm_gain, new_first_norm_gain, new_second_norm_gain = adamw_update(
        norm_gain, grad_norm_gain, first_norm_gain, second_norm_gain, rate_vector, 0.0
    )
    new_in_weight, new_first_in_weight, new_second_in_weight = adamw_update(
        in_weight, grad_in_weight, first_in_weight, second_in_weight, rate_matrix, weight_decay
    )
    new_conv_weight, new_first_conv_weight, new_second_conv_weight = adamw_update(
        conv_weight, grad_conv_weight, first_conv_weight, second_conv_weight, rate_vector, 0.0
    )
    new_conv_bias, new_first_conv_bias, new_second_conv_bias = adamw_update(
        conv_bias, grad_conv_bias, first_conv_bias, second_conv_bias, rate_vector, 0.0
    )
    new_step_bias, new_first_step_bias, new_second_step_bias = adamw_update(
        step_bias, grad_step_bias, first_step_bias, second_step_bias, rate_vector, 0.0
    )
    new_decay_log, new_first_decay_log, new_second_decay_log = adamw_update(
        decay_log, grad_decay_log, first_decay_log, second_decay_log, rate_vector, 0.0
    )
    new_skip_gain, new_first_skip_gain, new_second_skip_gain = adamw_update(
        skip_gain, grad_skip_gain, first_skip_gain, second_skip_gain, rate_vector, 0.0
    )
    new_gated_gain, new_first_gated_gain, new_second_gated_gain = adamw_update(
        gated_gain, grad_gated_gain, first_gated_gain, second_gated_gain, rate_vector, 0.0
    )
    new_out_weight, new_first_out_weight, new_second_out_weight = adamw_update(
        out_weight, grad_out_weight, first_out_weight, second_out_weight, rate_matrix, weight_decay
    )
    return (
        block_output,
        input_grad,
        grad_norm_gain,
        grad_in_weight,
        grad_conv_weight,
        grad_conv_bias,
        grad_step_bias,
        grad_decay_log,
        grad_skip_gain,
        grad_gated_gain,
        grad_out_weight,
        new_norm_gain,
        new_first_norm_gain,
        new_second_norm_gain,
        new_in_weight,
        new_first_in_weight,
        new_second_in_weight,
        new_conv_weight,
        new_first_conv_weight,
        new_second_conv_weight,
        new_conv_bias,
        new_first_conv_bias,
        new_second_conv_bias,
        new_step_bias,
        new_first_step_bias,
        new_second_step_bias,
        new_decay_log,
        new_first_decay_log,
        new_second_decay_log,
        new_skip_gain,
        new_first_skip_gain,
        new_second_skip_gain,
        new_gated_gain,
        new_first_gated_gain,
        new_second_gated_gain,
        new_out_weight,
        new_first_out_weight,
        new_second_out_weight,
    )


def solution(mesh):
    in_specs = (
        P("dp", "seq", None),
        P("dp", "seq", None),
        P(("dp", "seq")),
        P(("dp", "seq"), None),
        P(None, ("dp", "seq")),
        P(("dp", "seq")),
        P(),
        P(),
        P(),
        P(("dp", "seq")),
        P(("dp", "seq"), None),
        P(("dp", "seq")),
        P(("dp", "seq")),
        P(("dp", "seq"), None),
        P(("dp", "seq"), None),
        P(None, ("dp", "seq")),
        P(None, ("dp", "seq")),
        P(("dp", "seq")),
        P(("dp", "seq")),
        P(),
        P(),
        P(),
        P(),
        P(),
        P(),
        P(("dp", "seq")),
        P(("dp", "seq")),
        P(("dp", "seq"), None),
        P(("dp", "seq"), None),
    )
    out_specs = (
        P("dp", "seq", None),
        P("dp", "seq", None),
        P(("dp", "seq")),
        P(("dp", "seq"), None),
        P(None, ("dp", "seq")),
        P(("dp", "seq")),
        P(),
        P(),
        P(),
        P(("dp", "seq")),
        P(("dp", "seq"), None),
        P(("dp", "seq")),
        P(("dp", "seq")),
        P(("dp", "seq")),
        P(("dp", "seq"), None),
        P(("dp", "seq"), None),
        P(("dp", "seq"), None),
        P(None, ("dp", "seq")),
        P(None, ("dp", "seq")),
        P(None, ("dp", "seq")),
        P(("dp", "seq")),
        P(("dp", "seq")),
        P(("dp", "seq")),
        P(),
        P(),
        P(),
        P(),
        P(),
        P(),
        P(),
        P(),
        P(),
        P(("dp", "seq")),
        P(("dp", "seq")),
        P(("dp", "seq")),
        P(("dp", "seq"), None),
        P(("dp", "seq"), None),
        P(("dp", "seq"), None),
    )

    return jax.shard_map(body, mesh=mesh, in_specs=in_specs, out_specs=out_specs, check_vma=False)
```

profile of v0, /device:TPU:0, one launch (start us, length us, event | category | flops | bytes accessed | tf_op | source)
XLA Modules:
  0.0 586.8 jit_solution(13881100052340234544)
XLA Ops:
  10.2 5.1 collective-permute-start.2
  37.8 10.2 %collective-permute-done.10 = bf16[48,2688]{1,0:T(8,128)(2,1)S(1)} collective-permute-done((bf16[48,2688]{1,0:T(8,128)(2,1)}, bf16[48,2688]{1,0:T(8,128)(2,1)S(1)}, u32[]{:S(2)}, u32[]{:S(2)}) %collective-permute-start.10) | collective-permute-done | bytes 258080 | tf_op jit(solution)/shard_map/ppermute | solution.py:36
  56.4 5.7 collective-permute-start.8
  67.1 13.3 %collective-permute-done.8 = bf16[256,1536]{1,0:T(8,128)(2,1)S(1)} collective-permute-done((bf16[256,1536]{1,0:T(8,128)(2,1)}, bf16[256,1536]{1,0:T(8,128)(2,1)S(1)}, u32[]{:S(2)}, u32[]{:S(2)}) %collective-permute-start.8) | collective-permute-done | bytes 786464 | tf_op jit(solution)/shard_map/ppermute | solution.py:36
  80.4 50.1 %collective-permute-done.7 = bf16[256,1536]{1,0:T(8,128)(2,1)S(1)} collective-permute-done((bf16[256,1536]{1,0:T(8,128)(2,1)}, bf16[256,1536]{1,0:T(8,128)(2,1)S(1)}, u32[]{:S(2)}, u32[]{:S(2)}) %collective-permute-start.7) | collective-permute-done | bytes 786464 | tf_op jit(solution)/shard_map/ppermute | solution.py:36
  141.6 11.9 %fusion.81.z_ref.x_ref.shared_ref.step_ref.x_before_ref.shared_before_ref = f32[1024,1920]{1,0:T(8,128)} fusion(bf16[1024,1536]{1,0:T(8,128)(2,1)} %bitcast.304, bf16[1536,1920]{1,0:T(8,128)(2,1)} %all-gather.3.cloned.1.call-done), kind=kOutput, calls=%fused_computation.293 | convolution fusion | flops 6039797760 | bytes 16908288 | tf_op jit(solution)/shard_map/dot_general | solution.py:604
  153.6 32.1 %mixer_forward.1 = (f32[1024,768]{1,0:T(8,128)}, f32[1024,768]{1,0:T(8,128)}, f32[4,6,128,128]{3,2,1,0:T(8,128)}, f32[1024,128]{1,0:T(8,128)}) custom-call(s32[5]{0:T(128)} %pad_add_fusion.table_ref, f32[1024,1920]{1,0:T(8,128)} %fusion.81.z_ref.x_ref.shared_ref.step_ref.x_before_ref.shared_before_ref, ...), custom_call_target="tpu_custom_call" | custom-call | tf_op jit(solution)/shard_map/mixer_forward/pallas_call | solution.py:405
  188.9 13.6 %collective-permute-done.19 = bf16[256,1536]{1,0:T(8,128)(2,1)} collective-permute-done((bf16[256,1536]{1,0:T(8,128)(2,1)S(1)}, bf16[256,1536]{1,0:T(8,128)(2,1)}, u32[]{:S(2)}, u32[]{:S(2)}) %collective-permute-start.19) | collective-permute-done | bytes 786464 | tf_op jit(solution)/shard_map/ppermute | solution.py:36
  212.0 5.4 collective-permute-done.12
  217.4 8.2 %multiply_reduce_fusion = (f32[1024]{0:T(1024)S(1)}, bf16[1024,768]{1,0:T(8,128)(2,1)S(1)}, f32[1024,768]{1,0:T(8,128)}) fusion(f32[1024,768]{1,0:T(8,128)} %get-tuple-element.96.gated_ref, f32[768]{0:T(1024)S(1)} %dynamic_slice.206, f32[1024]{0:T(1024)S(1)} %add_rsqrt_fusion.1, bf16[1024,1536]{1,0:T(8,128)(2,1)} %bitcast.302, ...), kind=kOutput, calls=%fused_computation.6 | convolution fusion | flops 2420636672 | bytes 13380608 | tf_op jit(solution)/shard_map/dot_general | solution.py:604
  234.2 9.8 %gate_backward.1 = (bf16[1024,768]{1,0:T(8,128)(2,1)}, f32[1024,768]{1,0:T(8,128)}, f32[1024,1]{1,0:T(8,128)}, f32[8,768]{1,0:T(8,128)}) custom-call(f32[1024,1920]{1,0:T(8,128)} %fusion.81.z_ref.x_ref.shared_ref.step_ref.x_before_ref.shared_before_ref, f32[1024,768]{1,0:T(8,128)} %get-tuple-element.96.gated_ref, f32[1024,768]{1,0:T(8,128)} %get-tuple-element.98.mixed_ref, ...), custom_call_target="tpu_custom_call" | custom-call | tf_op jit(solution)/shard_map/gate_backward/pallas_call | solution.py:457
  244.0 5.0 fusion.6
  277.7 15.4 %mixer_backward.4 = (bf16[1024,896]{1,0:T(8,128)(2,1)}, f32[1024,128]{1,0:T(8,128)}, f32[1024,256]{1,0:T(8,128)}, f32[6,128,128]{2,1,0:T(8,128)}, f32[6,8,128]{2...) custom-call(s32[5]{0:T(128)} %pad_add_fusion.table_ref, ...), custom_call_target="tpu_custom_call" | custom-call | tf_op jit(solution)/shard_map/mixer_backward/pallas_call | solution.py:490
  293.1 15.4 %mixer_backward.5 = (bf16[1024,896]{1,0:T(8,128)(2,1)}, f32[1024,128]{1,0:T(8,128)}, f32[1024,256]{1,0:T(8,128)}, f32[6,128,128]{2,1,0:T(8,128)}, f32[6,8,128]{2...) custom-call(s32[5]{0:T(128)} %pad_add_fusion.table_ref, ...), custom_call_target="tpu_custom_call", output_to_operand_aliasing={{0}: (19, {}), {1}: (20, {}), {2}: (21, {})} | custom-call | tf_op jit(solution)/shard_map/mixer_backward/pallas_call | solution.py:490
  308.6 15.4 %mixer_backward.6 = (bf16[1024,896]{1,0:T(8,128)(2,1)}, f32[1024,128]{1,0:T(8,128)}, f32[1024,256]{1,0:T(8,128)}, f32[6,128,128]{2,1,0:T(8,128)}, f32[6,8,128]{2...) custom-call(s32[5]{0:T(128)} %pad_add_fusion.table_ref, ...), custom_call_target="tpu_custom_call", output_to_operand_aliasing={{0}: (19, {}), {1}: (20, {}), {2}: (21, {})} | custom-call | tf_op jit(solution)/shard_map/mixer_backward/pallas_call | solution.py:490
  329.9 15.6 %mixer_backward.7 = (bf16[1024,896]{1,0:T(8,128)(2,1)}, f32[1024,128]{1,0:T(8,128)}, f32[1024,256]{1,0:T(8,128)}, f32[6,128,128]{2,1,0:T(8,128)}, f32[6,8,128]{2...) custom-call(s32[5]{0:T(128)} %pad_add_fusion.table_ref, ...), custom_call_target="tpu_custom_call", output_to_operand_aliasing={{0}: (19, {}), {1}: (20, {}), {2}: (21, {})} | custom-call | tf_op jit(solution)/shard_map/mixer_backward/pallas_call | solution.py:490
  351.7 5.5 fusion.13
  371.2 5.3 fusion.3
  402.3 11.6 %collective-permute-done.42 = f32[192,768]{1,0:T(8,128)S(1)} collective-permute-done((f32[192,768]{1,0:T(8,128)S(1)}, f32[192,768]{1,0:T(8,128)S(1)}, u32[]{:S(2)}, u32[]{:S(2)}) %collective-permute-start.42) | collective-permute-done | bytes 589856 | tf_op jit(solution)/shard_map/ppermute | solution.py:40
  415.1 7.3 %collective-permute-done.39 = f32[2,192,256]{2,1,0:T(8,128)S(1)} collective-permute-done((f32[2,192,256]{2,1,0:T(8,128)S(1)}, f32[2,192,256]{2,1,0:T(8,128)S(1)}, u32[]{:S(2)}, u32[]{:S(2)}) %collective-permute-start.39) | collective-permute-done | bytes 393248 | tf_op jit(solution)/shard_map/ppermute | solution.py:40
  426.1 11.9 %collective-permute-done.33 = f32[2,192,512]{2,1,0:T(8,128)S(1)} collective-permute-done((f32[2,192,512]{2,1,0:T(8,128)S(1)}, f32[2,192,512]{2,1,0:T(8,128)S(1)}, u32[]{:S(2)}, u32[]{:S(2)}) %collective-permute-start.33) | collective-permute-done | bytes 786464 | tf_op jit(solution)/shard_map/ppermute | solution.py:40
  454.3 32.3 %collective-permute-done.31 = f16[256,1664]{1,0:T(8,128)(2,1)S(1)} collective-permute-done((f16[256,1664]{1,0:T(8,128)(2,1)S(1)}, f16[256,1664]{1,0:T(8,128)(2,1)S(1)}, u32[]{:S(2)}, u32[]{:S(2)}) %collective-permute-start.31) | collective-permute-done | bytes 852000 | tf_op jit(solution)/shard_map/ppermute | solution.py:36
  491.9 30.7 %collective-permute-done.15 = f16[256,1536]{1,0:T(8,128)(2,1)} collective-permute-done((f16[256,1536]{1,0:T(8,128)(2,1)}, f16[256,1536]{1,0:T(8,128)(2,1)}, u32[]{:S(2)}, u32[]{:S(2)}) %collective-permute-start.15) | collective-permute-done | bytes 786464 | tf_op jit(solution)/shard_map/ppermute | solution.py:36
  551.1 5.2 collective-permute-done.49
  (473 shorter events, 228.5 us)
Async XLA Ops:
  7.2 134.4 %all-gather.3.cloned.1.call-start = ((), (), s32[]{:S(2)}) async-start(), calls=%async_computation | async-start | bytes 6635520 | tf_op jit(solution)/shard_map/all_gather | solution.py:702
  53.8 163.6 %all-gather.5.cloned.1.call-start = ((), (), s32[]{:S(2)}) async-start(), calls=%async_computation.1 | async-start | bytes 2654208 | tf_op jit(solution)/shard_map/all_gather | solution.py:703
  56.4 24.0 %collective-permute-start.8 = (bf16[256,1536]{1,0:T(8,128)(2,1)}, bf16[256,1536]{1,0:T(8,128)(2,1)S(1)}, u32[]{:S(2)}, u32[]{:S(2)}) collective-permute-start(bf16[256,1536]{1,0:T(8,128)(2,1)} %multiply_convert_fusion.4), channel_id=1, source_target_pairs={{0,3},{1,0},{2,1},{3,2},{4,7},{5,4},{6,5},{7,6},{8,11},{9,8},{10,9... | collective-permute-start | bytes 2359304 | tf_op jit(solution)/shard_map/ppermute | solution.py:36
  62.1 68.4 %collective-permute-start.7 = (bf16[256,1536]{1,0:T(8,128)(2,1)}, bf16[256,1536]{1,0:T(8,128)(2,1)S(1)}, u32[]{:S(2)}, u32[]{:S(2)}) collective-permute-start(bf16[256,1536]{1,0:T(8,128)(2,1)} %multiply_convert_fusion.4), channel_id=1, source_target_pairs={{0,2},{1,3},{2,0},{3,1},{4,6},{5,7},{6,4},{7,5},{8,10},{9,11},{10,... | collective-permute-start | bytes 2359304 | tf_op jit(solution)/shard_map/ppermute | solution.py:36
  63.0 67.4 %collective-permute-start.6 = (bf16[256,1536]{1,0:T(8,128)(2,1)}, bf16[256,1536]{1,0:T(8,128)(2,1)}, u32[]{:S(2)}, u32[]{:S(2)}) collective-permute-start(bf16[256,1536]{1,0:T(8,128)(2,1)} %multiply_convert_fusion.4), channel_id=1, source_target_pairs={{0,1},{1,2},{2,3},{3,0},{4,5},{5,6},{6,7},{7,4},{8,9},{9,10},{10,1... | collective-permute-start | bytes 2359304 | tf_op jit(solution)/shard_map/ppermute | solution.py:36
  134.4 54.4 %collective-permute-start.20 = (bf16[256,1536]{1,0:T(8,128)(2,1)S(1)}, bf16[256,1536]{1,0:T(8,128)(2,1)S(1)}, u32[]{:S(2)}, u32[]{:S(2)}) collective-permute-start(bf16[256,1536]{1,0:T(8,128)(2,1)S(1)} %copy-done.25), channel_id=1, source_target_pairs={{0,3},{1,0},{2,1},{3,2},{4,7},{5,4},{6,5},{7,6},{8,11},{9,8},{10,9... | collective-permute-start | bytes 2359304 | tf_op jit(solution)/shard_map/ppermute | solution.py:36
  134.5 68.0 %collective-permute-start.19 = (bf16[256,1536]{1,0:T(8,128)(2,1)S(1)}, bf16[256,1536]{1,0:T(8,128)(2,1)}, u32[]{:S(2)}, u32[]{:S(2)}) collective-permute-start(bf16[256,1536]{1,0:T(8,128)(2,1)S(1)} %copy-done.25), channel_id=1, source_target_pairs={{0,2},{1,3},{2,0},{3,1},{4,6},{5,7},{6,4},{7,5},{8,10},{9,11},{10,... | collective-permute-start | bytes 2359304 | tf_op jit(solution)/shard_map/ppermute | solution.py:36
  135.0 67.5 %collective-permute-start.18 = (bf16[256,1536]{1,0:T(8,128)(2,1)S(1)}, bf16[256,1536]{1,0:T(8,128)(2,1)}, u32[]{:S(2)}, u32[]{:S(2)}) collective-permute-start(bf16[256,1536]{1,0:T(8,128)(2,1)S(1)} %copy-done.25), channel_id=1, source_target_pairs={{0,1},{1,2},{2,3},{3,0},{4,5},{5,6},{6,7},{7,4},{8,9},{9,10},{10,1... | collective-permute-start | bytes 2359304 | tf_op jit(solution)/shard_map/ppermute | solution.py:36
  186.9 25.0 %collective-permute-start.14 = (f32[4,2,128]{2,1,0:T(2,128)S(1)}, f32[4,2,128]{2,1,0:T(2,128)S(1)}, u32[]{:S(2)}, u32[]{:S(2)}) collective-permute-start(f32[4,2,128]{2,1,0:T(2,128)S(1)} %bitcast.333), channel_id=1, source_target_pairs={{0,3},{1,0},{2,1},{3,2},{4,7},{5,4},{6,5},{7,6},{8,11},{9,8},{10,9... | collective-permute-start | bytes 12296 | tf_op jit(solution)/shard_map/ppermute | solution.py:36
  233.4 25.1 %collective-permute-start.24 = (f32[2,2,192,768]{3,2,1,0:T(8,128)}, f32[2,2,192,768]{3,2,1,0:T(8,128)}, u32[]{:S(2)}, u32[]{:S(2)}) collective-permute-start(f32[2,2,192,768]{3,2,1,0:T(8,128)} %dynamic-slice_bitcast_fusion.1), channel_id=1, source_target_pairs={{0,4},{4,0},{8,12},{12,8},{16,20},{20,16},{24,28},{28,24},{1,5},{5... | collective-permute-start | bytes 7077896 | tf_op jit(solution)/shard_map/ppermute | solution.py:40
  261.5 62.6 %collective-permute-start.26 = (f32[2,192,768]{2,1,0:T(8,128)S(1)}, f32[2,192,768]{2,1,0:T(8,128)}, u32[]{:S(2)}, u32[]{:S(2)}) collective-permute-start(f32[2,192,768]{2,1,0:T(8,128)S(1)} %dynamic-slice_bitcast_fusion.5), channel_id=1, source_target_pairs={{0,8},{4,12},{8,0},{12,4},{16,24},{20,28},{24,16},{28,20},{1,9},{5... | collective-permute-start | bytes 3538952 | tf_op jit(solution)/shard_map/ppermute | solution.py:40
  265.4 62.1 %collective-permute-start.27 = (f32[2,192,768]{2,1,0:T(8,128)}, f32[2,192,768]{2,1,0:T(8,128)}, u32[]{:S(2)}, u32[]{:S(2)}) collective-permute-start(f32[2,192,768]{2,1,0:T(8,128)} %dynamic-slice_bitcast_fusion.4), channel_id=1, source_target_pairs={{0,16},{4,20},{8,24},{12,28},{16,0},{20,4},{24,8},{28,12},{1,17},{... | collective-permute-start | bytes 3538952 | tf_op jit(solution)/shard_map/ppermute | solution.py:40
  268.6 223.3 %collective-permute-start.17 = (f16[256,1536]{1,0:T(8,128)(2,1)}, f16[256,1536]{1,0:T(8,128)(2,1)}, u32[]{:S(2)}, u32[]{:S(2)}) collective-permute-start(f16[256,1536]{1,0:T(8,128)(2,1)} %get-tuple-element.190), channel_id=1, source_target_pairs={{0,1},{1,2},{2,3},{3,0},{4,5},{5,6},{6,7},{7,4},{8,9},{9,10},{10,1... | collective-permute-start | bytes 2359304 | tf_op jit(solution)/shard_map/ppermute | solution.py:36
  327.0 66.5 %collective-permute-start.41 = (f32[192,768]{1,0:T(8,128)}, f32[192,768]{1,0:T(8,128)}, u32[]{:S(2)}, u32[]{:S(2)}) collective-permute-start(f32[192,768]{1,0:T(8,128)} %dynamic-slice_bitcast_fusion.9), channel_id=1, source_target_pairs={{0,16},{4,20},{8,24},{12,28},{16,0},{20,4},{24,8},{28,12},{1,17},{... | collective-permute-start | bytes 1769480 | tf_op jit(solution)/shard_map/ppermute | solution.py:40
  393.4 98.4 %collective-permute-start.16 = (f16[256,1536]{1,0:T(8,128)(2,1)}, f16[256,1536]{1,0:T(8,128)(2,1)}, u32[]{:S(2)}, u32[]{:S(2)}) collective-permute-start(f16[256,1536]{1,0:T(8,128)(2,1)} %get-tuple-element.191), channel_id=1, source_target_pairs={{0,2},{1,3},{2,0},{3,1},{4,6},{5,7},{6,4},{7,5},{8,10},{9,11},{10,... | collective-permute-start | bytes 2359304 | tf_op jit(solution)/shard_map/ppermute | solution.py:36
  400.2 24.7 %collective-permute-start.36 = (f32[2,192,384]{2,1,0:T(8,128)S(1)}, f32[2,192,384]{2,1,0:T(8,128)S(1)}, u32[]{:S(2)}, u32[]{:S(2)}) collective-permute-start(f32[2,192,384]{2,1,0:T(8,128)S(1)} %dynamic-slice_bitcast_fusion.10), channel_id=1, source_target_pairs={{0,16},{4,20},{8,24},{12,28},{16,0},{20,4},{24,8},{28,12},{1,17},{... | collective-permute-start | bytes 1769480 | tf_op jit(solution)/shard_map/ppermute | solution.py:40
  413.9 24.1 %collective-permute-start.33 = (f32[2,192,512]{2,1,0:T(8,128)S(1)}, f32[2,192,512]{2,1,0:T(8,128)S(1)}, u32[]{:S(2)}, u32[]{:S(2)}) collective-permute-start(f32[2,192,512]{2,1,0:T(8,128)S(1)} %dynamic-slice_bitcast_fusion.7), channel_id=1, source_target_pairs={{0,8},{4,12},{8,0},{12,4},{16,24},{20,28},{24,16},{28,20},{1,9},{5... | collective-permute-start | bytes 2359304 | tf_op jit(solution)/shard_map/ppermute | solution.py:40
  422.3 64.8 %collective-permute-start.44 = (f16[256,1664]{1,0:T(8,128)(2,1)S(1)}, f16[256,1664]{1,0:T(8,128)(2,1)S(1)}, u32[]{:S(2)}, u32[]{:S(2)}) collective-permute-start(f16[256,1664]{1,0:T(8,128)(2,1)S(1)} %get-tuple-element.186), channel_id=1, source_target_pairs={{0,1},{1,2},{2,3},{3,0},{4,5},{5,6},{6,7},{7,4},{8,9},{9,10},{10,1... | collective-permute-start | bytes 2555912 | tf_op jit(solution)/shard_map/ppermute | solution.py:36
  445.9 41.3 %collective-permute-start.43 = (f16[256,1664]{1,0:T(8,128)(2,1)S(1)}, f16[256,1664]{1,0:T(8,128)(2,1)S(1)}, u32[]{:S(2)}, u32[]{:S(2)}) collective-permute-start(f16[256,1664]{1,0:T(8,128)(2,1)S(1)} %get-tuple-element.185), channel_id=1, source_target_pairs={{0,2},{1,3},{2,0},{3,1},{4,6},{5,7},{6,4},{7,5},{8,10},{9,11},{10,... | collective-permute-start | bytes 2555912 | tf_op jit(solution)/shard_map/ppermute | solution.py:36
  449.0 37.6 %collective-permute-start.31 = (f16[256,1664]{1,0:T(8,128)(2,1)S(1)}, f16[256,1664]{1,0:T(8,128)(2,1)S(1)}, u32[]{:S(2)}, u32[]{:S(2)}) collective-permute-start(f16[256,1664]{1,0:T(8,128)(2,1)S(1)} %get-tuple-element.184), channel_id=1, source_target_pairs={{0,3},{1,0},{2,1},{3,2},{4,7},{5,4},{6,5},{7,6},{8,11},{9,8},{10,9... | collective-permute-start | bytes 2555912 | tf_op jit(solution)/shard_map/ppermute | solution.py:36
  486.6 35.9 %collective-permute-start.15 = (f16[256,1536]{1,0:T(8,128)(2,1)}, f16[256,1536]{1,0:T(8,128)(2,1)}, u32[]{:S(2)}, u32[]{:S(2)}) collective-permute-start(f16[256,1536]{1,0:T(8,128)(2,1)} %get-tuple-element.189), channel_id=1, source_target_pairs={{0,3},{1,0},{2,1},{3,2},{4,7},{5,4},{6,5},{7,6},{8,11},{9,8},{10,9... | collective-permute-start | bytes 2359304 | tf_op jit(solution)/shard_map/ppermute | solution.py:36
  491.8 34.0 %collective-permute-start.45 = (f32[4,28,128]{2,0,1:T(4,128)S(1)}, f32[4,28,128]{2,0,1:T(4,128)S(1)}, u32[]{:S(2)}, u32[]{:S(2)}) collective-permute-start(f32[4,28,128]{2,0,1:T(4,128)S(1)} %bitcast.332), channel_id=1, source_target_pairs={{0,4},{4,0},{8,12},{12,8},{16,20},{20,16},{24,28},{28,24},{1,5},{5... | collective-permute-start | bytes 172040 | tf_op jit(solution)/shard_map/ppermute | solution.py:40
  531.6 28.1 %collective-permute-start.51 = (f16[48,2816]{1,0:T(8,128)(2,1)}, f16[48,2816]{1,0:T(8,128)(2,1)}, u32[]{:S(2)}, u32[]{:S(2)}) collective-permute-start(f16[48,2816]{1,0:T(8,128)(2,1)} %get-tuple-element.197), channel_id=1, source_target_pairs={{0,1},{1,2},{2,3},{3,0},{4,5},{5,6},{6,7},{7,4},{8,9},{9,10},{10,1... | collective-permute-start | bytes 811016 | tf_op jit(solution)/shard_map/ppermute | solution.py:36
  535.8 26.7 %collective-permute-start.52 = (f16[48,2816]{1,0:T(8,128)(2,1)}, f16[48,2816]{1,0:T(8,128)(2,1)S(1)}, u32[]{:S(2)}, u32[]{:S(2)}) collective-permute-start(f16[48,2816]{1,0:T(8,128)(2,1)} %get-tuple-element.198), channel_id=1, source_target_pairs={{0,2},{1,3},{2,0},{3,1},{4,6},{5,7},{6,4},{7,5},{8,10},{9,11},{10,... | collective-permute-start | bytes 811016 | tf_op jit(solution)/shard_map/ppermute | solution.py:36
  (105 other events, 1004.4 us)
Sparse Core Ops, SparseCore 0:
  53.9 46.1 all-gather.2
  102.6 28.8 all-gather.4
where the time goes:
time: 597 us; the launch traced here: 587 us
  waiting for transfers between devices  209 us (35%)
  Pallas kernels  104 us (17%)
  starting transfers between devices  74 us (12%)
  local copies, waits for them, and re-layouts  64.5 us (11%)
  other arithmetic  61.1 us (10%)
  matrix products  58.5 us (10%)
  between operations  16.3 us (3%)
    ppermute x33, waiting for transfers between devices, shift(): lax.ppermute(block, axis, [(i, (i + distance) % size) for i in range(size)])  168 us
    pallas_call x4, Pallas kernels, run_backward(): pl.pallas_call(functools.partial(backward_kernel, chunk == 0, chunks), gr...  61.8 us
    dot_general x12, matrix products, dot(): return jnp.dot(left, right, preferred_element_type=jnp.float32)  58.5 us
    ppermute x33, starting transfers between devices, shift(): lax.ppermute(block, axis, [(i, (i + distance) % size) for i in range(size)])  55.5 us
    ppermute x21, waiting for transfers between devices, swap(): lax.ppermute(block, axis, [(i, i ^ bit) for i in range(lax.axis_size(axis...  40.8 us
    pallas_call x1, Pallas kernels, run_forward(): pl.pallas_call(forward_kernel, grid_spec=pltpu.PrefetchScalarGridSpec(num...  32.1 us
    ppermute x21, starting transfers between devices, swap(): lax.ppermute(block, axis, [(i, i ^ bit) for i in range(lax.axis_size(axis...  18.4 us
    unnamed x164, local copies, waits for them, and re-layouts  17.9 us
  transfers between devices with their start and end apart: 56, of which 20 were waited for; matrix products, arithmetic and copies ran while one was open for 25% of the time, Pallas kernels for 18%

commit v1 on v0

--- a/solution.py
+++ b/solution.py
@@ -36,6 +36,12 @@
     return lax.ppermute(block, axis, [(i, (i + distance) % size) for i in range(size)])
 
 
+def step_to(block, axis, distance):
+    size = lax.axis_size(axis)
+    route = [(i, i + distance) for i in range(size) if 0 <= i + distance < size]
+    return lax.ppermute(block, axis, route)
+
+
 def swap(block, axis, bit):
     return lax.ppermute(block, axis, [(i, i ^ bit) for i in range(lax.axis_size(axis))])
 
@@ -68,8 +74,14 @@
     return message[..., :width].astype(jnp.float32) * jnp.exp2(message[..., width : width + 1].astype(jnp.float32))
 
 
-def gather_near(block, axis):
-    return jnp.stack([block] + [shift(block, axis, turn) for turn in range(1, lax.axis_size(axis))])
+def near_parts(block, axis):
+    size, here = lax.axis_size(axis), lax.axis_index(axis)
+    if size != 4:
+        return [block] + [shift(block, axis, turn) for turn in range(1, size)]
+    below, above = step_to(block, axis, 1), step_to(block, axis, -1)
+    across = shift(block, axis, 2)
+    far = lax.ppermute(across, axis, [(2, 3), (1, 0)])
+    return [block, jnp.where(here == 0, far, below), across, jnp.where(here == size - 1, far, above)]
 
 
 def send_near(stacked, axis):
@@ -101,6 +113,30 @@
         )
         bit *= 2
     return result
+
+
+def gather_rows(blocks, axis):
+    size, here = lax.axis_size(axis), lax.axis_index(axis)
+    bits = [1 << k for k in range(size.bit_length() - 1)]
+    upper = bits[1:]
+    turned = upper[len(upper) // 2 :] + upper[: len(upper) // 2]
+    parts, paths = [], []
+    for block in blocks:
+        rows = block.shape[0] // 2
+        parts += [p.reshape((1,) * len(bits) + p.shape) for p in (block[:rows], block[rows:])]
+        paths += [upper + bits[:1], turned + bits[:1]]
+    for step in range(len(bits)):
+        arrived = [swap(p, axis, path[step]) for p, path in zip(parts, paths)]
+        for k, path in enumerate(paths):
+            place = bits[::-1].index(path[step])
+            up = (here & path[step]) > 0
+            parts[k] = jnp.concatenate(
+                [jnp.where(up, arrived[k], parts[k]), jnp.where(up, parts[k], arrived[k])], axis=place
+            )
+    return [
+        jnp.concatenate(parts[2 * k : 2 * k + 2], axis=len(bits)).reshape(-1, block.shape[1])
+        for k, block in enumerate(blocks)
+    ]
 
 
 def scatter_bits(stacked, axis):
@@ -123,12 +159,23 @@
 
 
 def product(left, right, right_dim=0):
+    joined_left = jnp.concatenate([left[0], left[0], left[1]], axis=1)
+    joined_right = jnp.concatenate([right[0], right[1], right[0]], axis=right_dim)
     dims = (((1,), (right_dim,)), ((), ()))
-
-    def one(a, b):
-        return lax.dot_general(a, b, dims, preferred_element_type=jnp.float32)
-
-    return one(left[0], right[0]) + (one(left[0], right[1]) + one(left[1], right[0]))
+    return lax.dot_general(joined_left, joined_right, dims, preferred_element_type=jnp.float32)
+
+
+def thirds(value):
+    high, rest = value.astype(low), value
+    rest = value - high.astype(jnp.float32)
+    middle = rest.astype(low)
+    return high, middle, (rest - middle.astype(jnp.float32)).astype(low)
+
+
+def spread(parts, chosen):
+    return jnp.dot(
+        jnp.concatenate(parts, axis=1), jnp.concatenate([chosen] * len(parts), axis=0), preferred_element_type=jnp.float32
+    )
 
 
 def exact_dot(left, right):
@@ -149,7 +196,29 @@
     shape = (LANES, LANES)
     head = lax.broadcasted_iota(jnp.int32, shape, 1 if transposed else 0)
     lane = lax.broadcasted_iota(jnp.int32, shape, 0 if transposed else 1)
-    return (head == base + 2 * pair + lane // HDIM).astype(jnp.float32)
+    return jnp.where(head == base + 2 * pair + lane // HDIM, 1.0, 0.0).astype(low)
+
+
+def own_lanes(parts, side):
+    lane = lax.broadcasted_iota(jnp.int32, parts[0].shape, 1)
+    return tuple(jnp.where(lane // HDIM == side, p, jnp.zeros_like(p)) for p in parts)
+
+
+def decays(column, row, after_row):
+    mid = column.shape[0] // 2
+    shape = (mid, mid)
+    down = lax.broadcasted_iota(jnp.int32, shape, 0)
+    across = lax.broadcasted_iota(jnp.int32, shape, 1)
+    keep = (down <= across) if after_row else (down >= across)
+
+    def block(rows, cols, masked):
+        gap = column[rows] - row[:, cols]
+        gap = -gap if after_row else gap
+        return jnp.exp(jnp.where(keep, gap, -1e30)) if masked else jnp.exp(gap)
+
+    early, late = slice(0, mid), slice(mid, 2 * mid)
+    side = block(early, late, False) if after_row else block(late, early, False)
+    return block(early, early, True), side, block(late, late, True)
 
 
 def taps_of(extended, size, kernel, offset):
@@ -196,8 +265,9 @@
         read_high[...], read_low[...] = read
         keys_high[...], keys_low[...] = halves(active[:, :NST].T)
         delta, _, running = step_sizes(step_ref[...], head_ref[...])
-        delta_all[...] = delta
-        run_all[...] = running
+        for k, (d, r) in enumerate(zip(thirds(delta), thirds(running))):
+            delta_all[k] = d
+            run_all[k] = r
         run_rows[...] = running.T
         square_ref[...] = jnp.zeros_like(square_ref)
 
@@ -208,21 +278,29 @@
     pre = taps_of(extended, size, chan, chan[4:5])
     values = pre * jax.nn.sigmoid(pre)
     lanes = lane_of_head(pair, base)
-    delta = exact_dot(delta_all[...], lanes)
-    running = exact_dot(run_all[...], lanes)
+    delta = spread([delta_all[k] for k in range(3)], lanes)
+    running = spread([run_all[k] for k in range(3)], lanes)
     stepped = delta * values
-    causal = lax.broadcasted_iota(jnp.int32, (size, size), 0) >= lax.broadcasted_iota(jnp.int32, (size, size), 1)
-    locals_ = []
+    stepped_halves = halves(stepped)
+    mid = size // 2
+    top, bottom, sources = [], [], []
     for side in range(2):
         column = running[:, side * HDIM : side * HDIM + 1]
         row = run_rows[pl.ds(base + 2 * pair + side, 1), :]
-        decay = jnp.exp(jnp.where(causal, column - row, -1e30))
-        mixing = halves(decay * meet[...])
-        locals_.append(product(mixing, halves(stepped[:, side * HDIM : (side + 1) * HDIM])))
+        first, below, second = decays(column, row, False)
+        top.append(halves(first * meet[:mid, :mid]))
+        bottom.append(
+            (halves(below * meet[mid:, :mid]), halves(second * meet[mid:, mid:]))
+        )
+        sources.append(own_lanes(stepped_halves, side))
+    joined = lambda parts, axis: tuple(jnp.concatenate(p, axis=axis) for p in zip(*parts))
+    upper = product(joined(top, 1), joined([tuple(p[:mid] for p in x) for x in sources], 0))
+    lower = product(joined([joined(b, 1) for b in bottom], 1), joined(sources, 0))
+    local = jnp.concatenate([upper, lower], axis=0)
     state = states[pair]
     state_ref[0, 0] = state
     carried = product((read_high[...], read_low[...]), halves(state))
-    scanned = jnp.concatenate(locals_, axis=1) + jnp.exp(running) * carried
+    scanned = local + jnp.exp(running) * carried
     last = running[size - 1 :, :]
     tail = halves(stepped * jnp.exp(last - running))
     states[pair] = jnp.exp(last) * state + product((keys_high[...], keys_low[...]), tail)
@@ -290,9 +368,10 @@
         keys_high[...], keys_low[...] = keys
         read_rows_high[...], read_rows_low[...] = halves(active[:, NST:].T)
         delta, change, running = step_sizes(step_ref[...], head_ref[...])
-        delta_all[...] = delta
+        for k, (d, r) in enumerate(zip(thirds(delta), thirds(running))):
+            delta_all[k] = d
+            run_all[k] = r
         change_all[...] = change
-        run_all[...] = running
         run_rows[...] = running.T
         meet_grad[...] = jnp.zeros_like(meet_grad)
         keys_grad[...] = jnp.zeros_like(keys_grad)
@@ -309,8 +388,8 @@
     gain = jax.nn.sigmoid(pre)
     values = pre * gain
     lanes = lane_of_head(pair, base)
-    delta = exact_dot(delta_all[...], lanes)
-    running = exact_dot(run_all[...], lanes)
+    delta = spread([delta_all[k] for k in range(3)], lanes)
+    running = spread([run_all[k] for k in range(3)], lanes)
     stepped = delta * values
 
     mixed, mix_grad = mixed_ref[...], mix_grad_ref[...]
@@ -327,23 +406,35 @@
     ended = jnp.sum(state_grad * state_after_ref[0, 0], axis=0, keepdims=True)
     state_grads[pair] = jnp.exp(last) * state_grad + product((read_rows_high[...], read_rows_low[...]), risen)
 
-    causal = lax.broadcasted_iota(jnp.int32, (size, size), 0) <= lax.broadcasted_iota(jnp.int32, (size, size), 1)
-    parts = []
+    mid = size // 2
+    grad_halves, stepped_halves = halves(mix_grad), halves(stepped)
+    early, late = slice(0, mid), slice(mid, size)
+    joined = lambda parts, axis: tuple(jnp.concatenate(p, axis=axis) for p in zip(*parts))
+    top, bottom, sources = [], [], []
+    first_grad = side_grad = second_grad = 0.0
     for side in range(2):
-        own = slice(side * HDIM, (side + 1) * HDIM)
         column = running[:, side * HDIM : side * HDIM + 1]
         row = run_rows[pl.ds(base + 2 * pair + side, 1), :]
-        decay = jnp.exp(jnp.where(causal, row - column, -1e30))
-        mixing = halves(decay * meet[...])
-        grad_halves = halves(mix_grad[:, own])
-        parts.append(product(mixing, grad_halves))
-        meet_grad[...] += decay * product(halves(stepped[:, own]), grad_halves, 1)
-    stepped_grad = stepped_grad + jnp.concatenate(parts, axis=1)
+        first, beside, second = decays(column, row, True)
+        top.append((halves(first * meet[early, early]), halves(beside * meet[early, late])))
+        bottom.append(halves(second * meet[late, late]))
+        sources.append(own_lanes(grad_halves, side))
+        mine = own_lanes(stepped_halves, side)
+        wide_grad = product(tuple(p[early] for p in mine), grad_halves, 1)
+        first_grad += first * wide_grad[:, early]
+        side_grad += beside * wide_grad[:, late]
+        second_grad += second * product(tuple(p[late] for p in mine), tuple(p[late] for p in grad_halves), 1)
+    meet_grad[early, early] += first_grad
+    meet_grad[early, late] += side_grad
+    meet_grad[late, late] += second_grad
+    upper = product(joined([joined(t, 1) for t in top], 1), joined(sources, 0))
+    lower = product(joined(bottom, 1), joined([tuple(p[late] for p in x) for x in sources], 0))
+    stepped_grad = stepped_grad + jnp.concatenate([upper, lower], axis=0)
     to_head = lane_of_head(pair, base, transposed=True)
     scanned = mixed - chan[5:6] * values
-    run_grad[...] += exact_dot(mix_grad * scanned - stepped * stepped_grad, to_head)
-    delta_grad[...] += exact_dot(values * stepped_grad, to_head)
-    last_grad[0:1, :] += exact_dot(jnp.broadcast_to(ended, (8, LANES)), to_head)[0:1]
+    run_grad[...] += spread(halves(mix_grad * scanned - stepped * stepped_grad), to_head)
+    delta_grad[...] += spread(halves(values * stepped_grad), to_head)
+    last_grad[...] += spread(thirds(jnp.broadcast_to(ended, (8, LANES))), to_head)
 
     values_grad = chan[5:6] * mix_grad + delta * stepped_grad
     pre_grad = values_grad * (gain * (1.0 + pre * (1.0 - gain)))
@@ -433,8 +524,8 @@
                 pltpu.VMEM((SPAN, NST), low),
                 pltpu.VMEM((NST, SPAN), low),
                 pltpu.VMEM((NST, SPAN), low),
-                pltpu.VMEM((SPAN, LANES), f32),
-                pltpu.VMEM((SPAN, LANES), f32),
+                pltpu.VMEM((3, SPAN, LANES), low),
+                pltpu.VMEM((3, SPAN, LANES), low),
                 pltpu.VMEM((LANES, SPAN), f32),
             ],
         ),
@@ -527,9 +618,9 @@
                 pltpu.VMEM((SPAN, NST), low),
                 pltpu.VMEM((NST, SPAN), low),
                 pltpu.VMEM((NST, SPAN), low),
+                pltpu.VMEM((3, SPAN, LANES), low),
                 pltpu.VMEM((SPAN, LANES), f32),
-                pltpu.VMEM((SPAN, LANES), f32),
-                pltpu.VMEM((SPAN, LANES), f32),
+                pltpu.VMEM((3, SPAN, LANES), low),
                 pltpu.VMEM((LANES, SPAN), f32),
                 pltpu.VMEM((SPAN, SPAN), f32),
                 pltpu.VMEM((SPAN, NST), f32),
@@ -666,8 +757,8 @@
     gated_own = lax.dynamic_slice_in_dim(gated_float, rank * wide, wide, 0)
     skip_own = lax.dynamic_slice_in_dim(skip_gain, rank * heads, heads, 0)
 
-    in_low = after(in_weight.astype(low), small_line)
-    out_low = after(out_weight.astype(low), small_line)
+    in_low = in_weight.astype(low)
+    out_low = out_weight.astype(low)
 
     def for_rank(j):
         return jnp.concatenate(
@@ -699,11 +790,12 @@
             weight_rows, weights_arrived[turn - 1], (rank + ranks - turn) % ranks, 0
         )
     weight_rows = weight_rows.reshape(ranks * rows, columns + wide)
-    in_full = lax.all_gather(weight_rows[:, :columns], "dp", axis=0, tiled=True)
-    out_full = lax.all_gather(weight_rows[:, columns:], "dp", axis=0, tiled=True)
-
-    hidden = gather_near(hidden_own, "seq").reshape(length, width)
-    upstream_low = gather_near(after(upstream.astype(low), hidden), "seq").reshape(length, width)
+    in_full, out_full = gather_rows([weight_rows[:, :columns], weight_rows[:, columns:]], "dp")
+
+    line_parts = near_parts(hidden_own, "seq")
+    line_parts = [after(part, in_full, out_full) for part in line_parts]
+    up_parts = near_parts(after(upstream.astype(low), *line_parts), "seq")
+    hidden = jnp.stack(line_parts).reshape(length, width)
 
     projected = dot(hidden, in_full)
     none = jnp.zeros((1, wide), jnp.float32)
@@ -727,8 +819,8 @@
     normed_low = (gated * scale[:, None] * gated_own).astype(low)
     branch_factor = 2.0 ** (14 - math.ceil(math.log2(0.17 * math.sqrt(E * wide))))
     out_half = (dot(normed_low, out_full.T) * branch_factor).astype(half).reshape(ranks, span, width)
-    branch = tokens + dot(normed_low[:span], out_full.T)
-
+
+    upstream_low = jnp.stack([after(part, out_half) for part in up_parts]).reshape(length, width)
     normed_grad = dot(upstream_low, out_full)
     pull_sum = jnp.sum(normed_grad * gated_own * gated, axis=1).reshape(packed_length)
     pull_sum = sum_near(pull_sum, "seq").reshape(length)
@@ -737,15 +829,16 @@
     gate_low, mix_grad, gate_square, gain_rows = run_gate(projected, gated, mixed, normed_grad, chan, stats)
     gated_grad = gain_rows[0]
 
-    branch_parts = send_near(after(out_half, pull_sum), "seq")
-
-    early = Scatter([dot(upstream_low.T, normed_low), dot(hidden.T, gate_low)], "dp")
+    branch_parts = send_near(out_half, "seq")
+
+    out_grad_part = dot(upstream_low.T, normed_low)
+    early = Scatter([out_grad_part, dot(hidden.T, gate_low)], "dp")
     carried = (
         zeros((pairs, NST, LANES)), zeros((pairs, 8, LANES)), zeros((8, 2 * NST)),
         zeros((pairs, 8, LANES)), zeros((8, 2 * NST)), zeros((8, LANES)),
     )
     outputs = ()
-    ready = (branch,)
+    ready = (gate_low,)
     for turn in range(chunks):
         if early.done < early.steps and turn != 2:
             early.step()
@@ -759,27 +852,40 @@
     _, _, _, chan_grad, shared_chan_grad, head_grad = carried
     early.finish()
 
+    largest = jnp.max(gate_square.reshape(ranks, span) + jnp.sum(conv_square.reshape(ranks, span, LANES), axis=2), axis=1)
+    bound = 0.1565 * math.sqrt(2 * wide + NHEADS) * jnp.sqrt(largest)
+    power = jnp.clip(jnp.ceil(jnp.log2(bound)) - 14.0, -120.0, 120.0)
     shared_parts = shared_grad.reshape(ranks, span, 2 * NST)
-    shared_sent = send_near(shared_parts, "seq")
-
-    hidden_part = dot(gate_low, in_full[:, :wide].T) + dot(conv_low, in_full[:, wide + 2 * NST :].T)
-    row_bound = 0.1565 * math.sqrt(2 * wide + NHEADS) * jnp.sqrt(gate_square + jnp.sum(conv_square, axis=1, keepdims=True))
-    hidden_part = hidden_part.reshape(ranks, span, width)
-    hidden_half = pack_half(hidden_part, row_bound.reshape(ranks, span, 1))
-    hidden_parts = send_near(hidden_half, "seq")
-
+    lines_of_power = jnp.broadcast_to(power[:, None, None], (ranks, 8, 2 * NST))
+    shared_sent = send_near(jnp.concatenate([shared_parts, lines_of_power], axis=1), "seq")
+
+    def hidden_rows(turn):
+        own = slice(turn * span, (turn + 1) * span)
+        return dot(gate_low[own], in_full[:, :wide].T) + dot(conv_low[own], in_full[:, wide + 2 * NST :].T)
+
+    hidden_parts, hidden_halves = [], []
+    for turn in range(1, ranks):
+        hidden_halves.append((hidden_rows(turn) * jnp.exp2(-power[turn])).astype(half))
+        hidden_parts.append(shift(hidden_halves[-1], "seq", ranks - turn))
     split = 4 * LANES
     conv_parts = [dot(hidden.T, conv_low[:, :split]), dot(hidden.T, conv_low[:, split:])]
+    late = Scatter(conv_parts, "dp")
+    conv_own, normed_own = conv_low[:span], normed_low[:span]
+    for turn in range(late.steps):
+        if turn == 1:
+            conv_own, normed_own = after(conv_own, *late.blocks), after(normed_own, *late.blocks)
+        late.step()
+    shared_own = shared_parts[0]
+    for part in shared_sent:
+        shared_own = shared_own + part[:span]
+    shared_own = shared_own.astype(low)
+    hidden_grad = dot(gate_low[:span], in_full[:, :wide].T) + dot(conv_own, in_full[:, wide + 2 * NST :].T)
+    branch = tokens + dot(normed_own, out_full.T)
     for part in branch_parts:
         branch = branch + part.astype(jnp.float32) * (1.0 / branch_factor)
     block_output = branch[None]
-
-    shared_own = shared_parts[0]
-    for part in shared_sent:
-        shared_own = shared_own + part
-    shared_own = shared_own.astype(low)
-    late = Scatter(conv_parts + [dot(hidden_own.T, shared_own)], "dp")
-    late.finish()
+    last = Scatter([dot(hidden_own.T, shared_own)], "dp")
+    last.finish()
 
     chan_grad = chan_grad.transpose(1, 0, 2).reshape(8, wide)
     kernel_grad, offset_grad = chan_grad[:CONVW], chan_grad[4]
@@ -787,11 +893,12 @@
     kernel_shared_grad, offset_shared_grad = shared_chan_grad[:CONVW], shared_chan_grad[4]
 
     sums_all = jnp.concatenate(
-        [block.reshape(ranks, rows, -1) for block in (late.blocks + early.blocks)], axis=2
+        [block.reshape(ranks, rows, -1) for block in (late.blocks + last.blocks + early.blocks)], axis=2
     )
     conv_wide = wide + LANES
     packed_sums = pack_half(sums_all, jnp.max(jnp.abs(sums_all), axis=-1, keepdims=True))
-    hidden_parts = [after(part, packed_sums) for part in hidden_parts]
+    hidden_parts = [after(part, packed_sums, block_output) for part in hidden_parts]
+    power_parts = [after(part, packed_sums)[span, 0] for part in shared_sent]
     collected = sums_all
     for turn in range(1, ranks):
         arrived = shift(pick(packed_sums, (rank + turn) % ranks), "seq", turn)
@@ -808,9 +915,9 @@
     )
     grad_out_weight = jnp.concatenate([collected[j, :, at : at + wide] for j in range(ranks)], axis=1)
 
-    hidden_grad = hidden_part[0] + dot(shared_own, in_full[:, wide : wide + 2 * NST].T)
-    for part in hidden_parts:
-        hidden_grad = hidden_grad + unpack_half(part)
+    hidden_grad = hidden_grad + dot(shared_own, in_full[:, wide : wide + 2 * NST].T)
+    for part, exponent in zip(hidden_parts, power_parts):
+        hidden_grad = hidden_grad + part.astype(jnp.float32) * jnp.exp2(exponent)
     scaled = tokens * inverse
     gain_grad = jnp.sum(hidden_grad * scaled, axis=0)
     inner = hidden_grad * norm_float
@@ -830,7 +937,6 @@
     head_all = jnp.concatenate([head_grad[0, :NHEADS], head_grad[1, :NHEADS], skip_all])
     terms = jnp.concatenate(
         [
-            gain_grad.reshape(devices, rows),
             kernel_all,
             offset_all,
             gated_all.reshape(devices, gains),
@@ -841,11 +947,16 @@
     used = terms.shape[1]
     term_lines = -(-used // LANES)
     terms = jnp.pad(terms, ((0, 0), (0, term_lines * LANES - used)))
-    terms = terms.reshape(groups, ranks * term_lines, LANES)
+    terms = terms.reshape(groups, ranks, term_lines, LANES)
+    norm_lines = -(-rows // LANES)
+    norm_terms = jnp.pad(gain_grad.reshape(devices, rows), ((0, 0), (0, norm_lines * LANES - rows)))
+    norm_terms = norm_terms.reshape(groups, ranks, norm_lines, LANES)
+    term_lines += norm_lines
+    terms = jnp.concatenate([norm_terms, terms], axis=2).reshape(groups, ranks * term_lines, LANES)
     summed = scatter_bits(terms, "dp").reshape(ranks, term_lines, LANES)
     summed = exchange_sum(summed, "seq").reshape(-1)
     grad_norm_gain = summed[:rows]
-    at = rows
+    at = norm_lines * LANES
     grad_conv_weight = summed[at : at + CONVW * taps].reshape(CONVW, taps)
     at += CONVW * taps
     grad_conv_bias = summed[at : at + taps]

time: 597 us -> 601 us (level)
  the two profiles are of different devices: /device:TPU:0 before, /device:TPU:16 now
where the time goes in v1:
time: 601 us; the launch traced here: 590 us
  waiting for transfers between devices  180 us (30%)
  starting transfers between devices  123 us (20%)
  Pallas kernels  91.2 us (15%)
  local copies, waits for them, and re-layouts  66.9 us (11%)
  matrix products  61.1 us (10%)
  other arithmetic  60.5 us (10%)
  between operations  7.17 us (1%)
    ppermute x29, waiting for transfers between devices, shift(): lax.ppermute(block, axis, [(i, (i + distance) % size) for i in range(size)])  101 us
    ppermute x29, starting transfers between devices, shift(): lax.ppermute(block, axis, [(i, (i + distance) % size) for i in range(size)])  69.7 us
    ppermute x33, waiting for transfers between devices, swap(): lax.ppermute(block, axis, [(i, i ^ bit) for i in range(lax.axis_size(axis...  64.4 us
    dot_general x18, matrix products, dot(): return jnp.dot(left, right, preferred_element_type=jnp.float32)  61.1 us
    pallas_call x4, Pallas kernels, run_backward(): pl.pallas_call(functools.partial(backward_kernel, chunk == 0, chunks), gr...  53.6 us
    ppermute x33, starting transfers between devices, swap(): lax.ppermute(block, axis, [(i, i ^ bit) for i in range(lax.axis_size(axis...  33.1 us
    pallas_call x1, Pallas kernels, run_forward(): pl.pallas_call(forward_kernel, grid_spec=pltpu.PrefetchScalarGridSpec(num...  27.8 us
    unnamed x180, local copies, waits for them, and re-layouts  16.8 us
  transfers between devices with their start and end apart: 68, of which 28 were waited for; matrix products, arithmetic and copies ran while one was open for 24% of the time, Pallas kernels for 11%

profile of v1, /device:TPU:16, one launch (start us, length us, event | category | flops | bytes accessed | tf_op | source)
XLA Modules:
  0.0 589.6 jit_solution(12708433427273623242)
XLA Ops:
  41.1 7.3 %collective-permute-done.6 = bf16[48,2688]{1,0:T(8,128)(2,1)} collective-permute-done((bf16[48,2688]{1,0:T(8,128)(2,1)}, bf16[48,2688]{1,0:T(8,128)(2,1)}, u32[]{:S(2)}, u32[]{:S(2)}) %collective-permute-start.6) | collective-permute-done | bytes 258080 | tf_op jit(solution)/shard_map/ppermute | solution.py:36
  83.9 7.8 %collective-permute-done.13 = bf16[2,1,1,96,1920]{4,3,2,1,0:T(8,128)(2,1)S(1)} collective-permute-done((bf16[2,1,1,96,1920]{4,3,2,1,0:T(8,128)(2,1)S(1)}, bf16[2,1,1,96,1920]{4,3,2,1,0:T(8,128)(2,1)S(1)}, u32[]{:S(2)}, u32[]{:S(2)}) %collective-permute-start.13) | collective-permute-done | bytes 737312 | tf_op jit(solution)/shard_map/ppermute | solution.py:46
  103.0 6.6 %collective-permute-done.22 = bf16[256,1536]{1,0:T(8,128)(2,1)S(1)} collective-permute-done((bf16[256,1536]{1,0:T(8,128)(2,1)}, bf16[256,1536]{1,0:T(8,128)(2,1)S(1)}, u32[]{:S(2)}, u32[]{:S(2)}) %collective-permute-start.22) | collective-permute-done | bytes 786464 | tf_op jit(solution)/shard_map/ppermute | solution.py:83
  116.0 8.8 %fusion.109.z_ref.x_ref.shared_ref.step_ref.x_before_ref.shared_before_ref = f32[1024,1920]{1,0:T(8,128)} fusion(bf16[1024,1536]{1,0:T(8,128)(2,1)S(1)} %bitcast.327, bf16[1536,1920]{1,0:T(8,128)(2,1)S(1)} %bitcast.338), kind=kOutput, calls=%fused_computation.357 | convolution fusion | flops 6039797760 | bytes 16908288 | tf_op jit(solution)/shard_map/dot_general | solution.py:695
  124.8 27.8 %mixer_forward.1 = (f32[1024,768]{1,0:T(8,128)}, f32[1024,768]{1,0:T(8,128)}, f32[4,6,128,128]{3,2,1,0:T(8,128)}, f32[1024,128]{1,0:T(8,128)}) custom-call(s32[5]{0:T(128)} %pad_add_fusion.table_ref, f32[1024,1920]{1,0:T(8,128)} %fusion.109.z_ref.x_ref.shared_ref.step_ref.x_before_ref.shared_before_ref, ...), custom_call_target="tpu_custom_call" | custom-call | tf_op jit(solution)/shard_map/mixer_forward/pallas_call | solution.py:496
  153.8 6.7 %collective-permute-start.27 = (f32[4,2,128]{2,1,0:T(2,128)S(1)}, f32[4,2,128]{2,1,0:T(2,128)S(1)}, u32[]{:S(2)}, u32[]{:S(2)}) collective-permute-start(f32[4,2,128]{2,1,0:T(2,128)S(1)} %bitcast.380), channel_id=1, source_target_pairs={{0,3},{1,0},{2,1},{3,2},{4,7},{5,4},{6,5},{7,6},{8,11},{9,8},{10,9... | collective-permute-start | bytes 12296 | tf_op jit(solution)/shard_map/ppermute | solution.py:36
  175.3 23.2 %collective-permute-done.25 = f32[4,2,128]{2,1,0:T(2,128)S(1)} collective-permute-done((f32[4,2,128]{2,1,0:T(2,128)S(1)}, f32[4,2,128]{2,1,0:T(2,128)S(1)}, u32[]{:S(2)}, u32[]{:S(2)}) %collective-permute-start.25) | collective-permute-done | bytes 4128 | tf_op jit(solution)/shard_map/ppermute | solution.py:36
  208.6 5.4 collective-permute-done.30
  224.7 9.1 %collective-permute-start.34 = (f32[4,2,128]{2,1,0:T(2,128)S(1)}, f32[4,2,128]{2,1,0:T(2,128)S(1)}, u32[]{:S(2)}, u32[]{:S(2)}) collective-permute-start(f32[4,2,128]{2,1,0:T(2,128)S(1)} %bitcast.396), channel_id=1, source_target_pairs={{0,3},{1,0},{2,1},{3,2},{4,7},{5,4},{6,5},{7,6},{8,11},{9,8},{10,9... | collective-permute-start | bytes 12296 | tf_op jit(solution)/shard_map/ppermute | solution.py:36
  249.3 9.8 %gate_backward.1 = (bf16[1024,768]{1,0:T(8,128)(2,1)}, f32[1024,768]{1,0:T(8,128)}, f32[1024,1]{1,0:T(8,128)}, f32[8,768]{1,0:T(8,128)}) custom-call(f32[1024,1920]{1,0:T(8,128)} %fusion.109.z_ref.x_ref.shared_ref.step_ref.x_before_ref.shared_before_ref, f32[1024,768]{1,0:T(8,128)} %get-tuple-element.109.gated_ref, ...), custom_call_target="tpu_custom_call" | custom-call | tf_op jit(solution)/shard_map/gate_backward/pallas_call | solution.py:548
  259.1 5.0 fusion.21
  286.3 13.3 %mixer_backward.4 = (bf16[1024,896]{1,0:T(8,128)(2,1)}, f32[1024,128]{1,0:T(8,128)}, f32[1024,256]{1,0:T(8,128)}, f32[6,128,128]{2,1,0:T(8,128)}, f32[6,8,128]{2...) custom-call(s32[5]{0:T(128)} %pad_add_fusion.table_ref, ...), custom_call_target="tpu_custom_call" | custom-call | tf_op jit(solution)/shard_map/mixer_backward/pallas_call | solution.py:581
  303.4 13.3 %mixer_backward.5 = (bf16[1024,896]{1,0:T(8,128)(2,1)}, f32[1024,128]{1,0:T(8,128)}, f32[1024,256]{1,0:T(8,128)}, f32[6,128,128]{2,1,0:T(8,128)}, f32[6,8,128]{2...) custom-call(s32[5]{0:T(128)} %pad_add_fusion.table_ref, ...), custom_call_target="tpu_custom_call", output_to_operand_aliasing={{0}: (19, {}), {1}: (20, {}), {2}: (21, {})} | custom-call | tf_op jit(solution)/shard_map/mixer_backward/pallas_call | solution.py:581
  316.7 13.3 %mixer_backward.6 = (bf16[1024,896]{1,0:T(8,128)(2,1)}, f32[1024,128]{1,0:T(8,128)}, f32[1024,256]{1,0:T(8,128)}, f32[6,128,128]{2,1,0:T(8,128)}, f32[6,8,128]{2...) custom-call(s32[5]{0:T(128)} %pad_add_fusion.table_ref, ...), custom_call_target="tpu_custom_call", output_to_operand_aliasing={{0}: (19, {}), {1}: (20, {}), {2}: (21, {})} | custom-call | tf_op jit(solution)/shard_map/mixer_backward/pallas_call | solution.py:581
  335.8 13.7 %mixer_backward.7 = (bf16[1024,896]{1,0:T(8,128)(2,1)}, f32[1024,128]{1,0:T(8,128)}, f32[1024,256]{1,0:T(8,128)}, f32[6,128,128]{2,1,0:T(8,128)}, f32[6,8,128]{2...) custom-call(s32[5]{0:T(128)} %pad_add_fusion.table_ref, ...), custom_call_target="tpu_custom_call", output_to_operand_aliasing={{0}: (19, {}), {1}: (20, {}), {2}: (21, {})} | custom-call | tf_op jit(solution)/shard_map/mixer_backward/pallas_call | solution.py:581
  400.1 9.0 %collective-permute-done.56 = f32[192,768]{1,0:T(8,128)S(1)} collective-permute-done((f32[192,768]{1,0:T(8,128)S(1)}, f32[192,768]{1,0:T(8,128)S(1)}, u32[]{:S(2)}, u32[]{:S(2)}) %collective-permute-start.56) | collective-permute-done | bytes 589856 | tf_op jit(solution)/shard_map/ppermute | solution.py:46
  415.2 6.3 %collective-permute-done.53 = f32[2,192,256]{2,1,0:T(8,128)S(1)} collective-permute-done((f32[2,192,256]{2,1,0:T(8,128)S(1)}, f32[2,192,256]{2,1,0:T(8,128)S(1)}, u32[]{:S(2)}, u32[]{:S(2)}) %collective-permute-start.53) | collective-permute-done | bytes 393248 | tf_op jit(solution)/shard_map/ppermute | solution.py:46
  427.8 18.2 %collective-permute-done.42 = f16[256,1536]{1,0:T(8,128)(2,1)S(1)} collective-permute-done((f16[256,1536]{1,0:T(8,128)(2,1)S(1)}, f16[256,1536]{1,0:T(8,128)(2,1)S(1)}, u32[]{:S(2)}, u32[]{:S(2)}) %collective-permute-start.42) | collective-permute-done | bytes 786464 | tf_op jit(solution)/shard_map/ppermute | solution.py:36
  445.9 17.4 %collective-permute-start.47 = (f16[256,1536]{1,0:T(8,128)(2,1)S(1)}, f16[256,1536]{1,0:T(8,128)(2,1)S(1)}, u32[]{:S(2)}, u32[]{:S(2)}) collective-permute-start(f16[256,1536]{1,0:T(8,128)(2,1)S(1)} %fusion.10), channel_id=1, source_target_pairs={{0,3},{1,0},{2,1},{3,2},{4,7},{5,4},{6,5},{7,6},{8,11},{9,8},{10,9... | collective-permute-start | bytes 2359304 | tf_op jit(solution)/shard_map/ppermute | solution.py:36
  463.4 29.9 %collective-permute-done.41 = f16[256,1536]{1,0:T(8,128)(2,1)S(1)} collective-permute-done((f16[256,1536]{1,0:T(8,128)(2,1)S(1)}, f16[256,1536]{1,0:T(8,128)(2,1)S(1)}, u32[]{:S(2)}, u32[]{:S(2)}) %collective-permute-start.41) | collective-permute-done | bytes 786464 | tf_op jit(solution)/shard_map/ppermute | solution.py:36
  499.7 12.9 %collective-permute-done.48 = f32[2,192,512]{2,1,0:T(8,128)S(1)} collective-permute-done((f32[2,192,512]{2,1,0:T(8,128)S(1)}, f32[2,192,512]{2,1,0:T(8,128)S(1)}, u32[]{:S(2)}, u32[]{:S(2)}) %collective-permute-start.48) | collective-permute-done | bytes 786464 | tf_op jit(solution)/shard_map/ppermute | solution.py:46
  515.6 5.0 collective-permute-done.51
  550.6 8.7 %collective-permute-done.64 = f32[7,128]{1,0:T(8,128)S(1)} collective-permute-done((f32[7,128]{1,0:T(8,128)S(1)}, f32[7,128]{1,0:T(8,128)S(1)}, u32[]{:S(2)}, u32[]{:S(2)}) %collective-permute-start.64) | collective-permute-done | bytes 3616 | tf_op jit(solution)/shard_map/ppermute | solution.py:36
  561.9 5.1 collective-permute-done.62
  (543 shorter events, 298.9 us)
Async XLA Ops:
  12.5 35.8 %collective-permute-start.6 = (bf16[48,2688]{1,0:T(8,128)(2,1)}, bf16[48,2688]{1,0:T(8,128)(2,1)}, u32[]{:S(2)}, u32[]{:S(2)}) collective-permute-start(bf16[48,2688]{1,0:T(8,128)(2,1)} %get-tuple-element.269), channel_id=1, source_target_pairs={{0,1},{1,2},{2,3},{3,0},{4,5},{5,6},{6,7},{7,4},{8,9},{9,10},{10,1... | collective-permute-start | bytes 774152 | tf_op jit(solution)/shard_map/ppermute | solution.py:36
  14.0 34.4 %collective-permute-start.7 = (bf16[48,2688]{1,0:T(8,128)(2,1)}, bf16[48,2688]{1,0:T(8,128)(2,1)}, u32[]{:S(2)}, u32[]{:S(2)}) collective-permute-start(bf16[48,2688]{1,0:T(8,128)(2,1)} %get-tuple-element.268), channel_id=1, source_target_pairs={{0,2},{1,3},{2,0},{3,1},{4,6},{5,7},{6,4},{7,5},{8,10},{9,11},{10,... | collective-permute-start | bytes 774152 | tf_op jit(solution)/shard_map/ppermute | solution.py:36
  16.5 36.5 %collective-permute-start.8 = (bf16[48,2688]{1,0:T(8,128)(2,1)}, bf16[48,2688]{1,0:T(8,128)(2,1)}, u32[]{:S(2)}, u32[]{:S(2)}) collective-permute-start(bf16[48,2688]{1,0:T(8,128)(2,1)} %copy-done.48), channel_id=1, source_target_pairs={{0,3},{1,0},{2,1},{3,2},{4,7},{5,4},{6,5},{7,6},{8,11},{9,8},{10,9... | collective-permute-start | bytes 774152 | tf_op jit(solution)/shard_map/ppermute | solution.py:36
  27.6 56.3 %collective-permute-start.21 = (bf16[256,1536]{1,0:T(8,128)(2,1)S(1)}, bf16[256,1536]{1,0:T(8,128)(2,1)}, u32[]{:S(2)}, u32[]{:S(2)}) collective-permute-start(bf16[256,1536]{1,0:T(8,128)(2,1)S(1)} %multiply_convert_fusion.3), channel_id=1, source_target_pairs={{0,2},{1,3},{2,0},{3,1},{4,6},{5,7},{6,4},{7,5},{8,10},{9,11},{10,... | collective-permute-start | bytes 2359304 | tf_op jit(solution)/shard_map/ppermute | solution.py:36
  29.6 73.4 %collective-permute-start.23 = (bf16[256,1536]{1,0:T(8,128)(2,1)S(1)}, bf16[256,1536]{1,0:T(8,128)(2,1)}, u32[]{:S(2)}, u32[]{:S(2)}) collective-permute-start(bf16[256,1536]{1,0:T(8,128)(2,1)S(1)} %multiply_convert_fusion.3), channel_id=1, source_target_pairs={{0,1},{1,2},{2,3},{4,5},{5,6},{6,7},{8,9},{9,10},{10,11},{12,13},{... | collective-permute-start | bytes 2359304 | tf_op jit(solution)/shard_map/ppermute | solution.py:42
  77.6 25.4 %collective-permute-start.24 = (bf16[256,1536]{1,0:T(8,128)(2,1)S(1)}, bf16[256,1536]{1,0:T(8,128)(2,1)S(1)}, u32[]{:S(2)}, u32[]{:S(2)}) collective-permute-start(bf16[256,1536]{1,0:T(8,128)(2,1)S(1)} %multiply_convert_fusion.3), channel_id=1, source_target_pairs={{1,0},{2,1},{3,2},{5,4},{6,5},{7,6},{9,8},{10,9},{11,10},{13,12},{... | collective-permute-start | bytes 2359304 | tf_op jit(solution)/shard_map/ppermute | solution.py:42
  161.5 37.1 %collective-permute-start.28 = (bf16[256,1536]{1,0:T(8,128)(2,1)}, bf16[256,1536]{1,0:T(8,128)(2,1)}, u32[]{:S(2)}, u32[]{:S(2)}) collective-permute-start(bf16[256,1536]{1,0:T(8,128)(2,1)} %bitcast_convert_fusion), channel_id=1, source_target_pairs={{0,2},{1,3},{2,0},{3,1},{4,6},{5,7},{6,4},{7,5},{8,10},{9,11},{10,... | collective-permute-start | bytes 2359304 | tf_op jit(solution)/shard_map/ppermute | solution.py:36
  162.2 36.3 %collective-permute-start.26 = (f32[4,2,128]{2,1,0:T(2,128)S(1)}, f32[4,2,128]{2,1,0:T(2,128)S(1)}, u32[]{:S(2)}, u32[]{:S(2)}) collective-permute-start(f32[4,2,128]{2,1,0:T(2,128)S(1)} %bitcast.381), channel_id=1, source_target_pairs={{0,2},{1,3},{2,0},{3,1},{4,6},{5,7},{6,4},{7,5},{8,10},{9,11},{10,... | collective-permute-start | bytes 12296 | tf_op jit(solution)/shard_map/ppermute | solution.py:36
  164.4 34.1 %collective-permute-start.25 = (f32[4,2,128]{2,1,0:T(2,128)S(1)}, f32[4,2,128]{2,1,0:T(2,128)S(1)}, u32[]{:S(2)}, u32[]{:S(2)}) collective-permute-start(f32[4,2,128]{2,1,0:T(2,128)S(1)} %bitcast.382), channel_id=1, source_target_pairs={{0,1},{1,2},{2,3},{3,0},{4,5},{5,6},{6,7},{7,4},{8,9},{9,10},{10,1... | collective-permute-start | bytes 12296 | tf_op jit(solution)/shard_map/ppermute | solution.py:36
  164.4 49.5 %collective-permute-start.30 = (bf16[256,1536]{1,0:T(8,128)(2,1)}, bf16[256,1536]{1,0:T(8,128)(2,1)}, u32[]{:S(2)}, u32[]{:S(2)}) collective-permute-start(bf16[256,1536]{1,0:T(8,128)(2,1)} %bitcast_convert_fusion), channel_id=1, source_target_pairs={{0,1},{1,2},{2,3},{4,5},{5,6},{6,7},{8,9},{9,10},{10,11},{12,13},{... | collective-permute-start | bytes 2359304 | tf_op jit(solution)/shard_map/ppermute | solution.py:42
  173.2 40.8 %collective-permute-start.31 = (bf16[256,1536]{1,0:T(8,128)(2,1)}, bf16[256,1536]{1,0:T(8,128)(2,1)S(1)}, u32[]{:S(2)}, u32[]{:S(2)}) collective-permute-start(bf16[256,1536]{1,0:T(8,128)(2,1)} %bitcast_convert_fusion), channel_id=1, source_target_pairs={{1,0},{2,1},{3,2},{5,4},{6,5},{7,6},{9,8},{10,9},{11,10},{13,12},{... | collective-permute-start | bytes 2359304 | tf_op jit(solution)/shard_map/ppermute | solution.py:42
  224.7 23.9 %collective-permute-start.34 = (f32[4,2,128]{2,1,0:T(2,128)S(1)}, f32[4,2,128]{2,1,0:T(2,128)S(1)}, u32[]{:S(2)}, u32[]{:S(2)}) collective-permute-start(f32[4,2,128]{2,1,0:T(2,128)S(1)} %bitcast.396), channel_id=1, source_target_pairs={{0,3},{1,0},{2,1},{3,2},{4,7},{5,4},{6,5},{7,6},{8,11},{9,8},{10,9... | collective-permute-start | bytes 12296 | tf_op jit(solution)/shard_map/ppermute | solution.py:36
  271.8 58.2 %collective-permute-start.37 = (f32[2,192,768]{2,1,0:T(8,128)S(1)}, f32[2,192,768]{2,1,0:T(8,128)}, u32[]{:S(2)}, u32[]{:S(2)}) collective-permute-start(f32[2,192,768]{2,1,0:T(8,128)S(1)} %dynamic-slice_bitcast_fusion.5), channel_id=1, source_target_pairs={{0,8},{4,12},{8,0},{12,4},{16,24},{20,28},{24,16},{28,20},{1,9},{5... | collective-permute-start | bytes 3538952 | tf_op jit(solution)/shard_map/ppermute | solution.py:46
  276.8 56.6 %collective-permute-start.38 = (f32[2,192,768]{2,1,0:T(8,128)}, f32[2,192,768]{2,1,0:T(8,128)}, u32[]{:S(2)}, u32[]{:S(2)}) collective-permute-start(f32[2,192,768]{2,1,0:T(8,128)} %dynamic-slice_bitcast_fusion.4), channel_id=1, source_target_pairs={{0,16},{4,20},{8,24},{12,28},{16,0},{20,4},{24,8},{28,12},{1,17},{... | collective-permute-start | bytes 3538952 | tf_op jit(solution)/shard_map/ppermute | solution.py:46
  279.9 145.5 %collective-permute-start.43 = (f16[256,1536]{1,0:T(8,128)(2,1)}, f16[256,1536]{1,0:T(8,128)(2,1)}, u32[]{:S(2)}, u32[]{:S(2)}) collective-permute-start(f16[256,1536]{1,0:T(8,128)(2,1)} %get-tuple-element.207), channel_id=1, source_target_pairs={{0,1},{1,2},{2,3},{3,0},{4,5},{5,6},{6,7},{7,4},{8,9},{9,10},{10,1... | collective-permute-start | bytes 2359304 | tf_op jit(solution)/shard_map/ppermute | solution.py:36
  332.9 65.1 %collective-permute-start.55 = (f32[192,768]{1,0:T(8,128)}, f32[192,768]{1,0:T(8,128)}, u32[]{:S(2)}, u32[]{:S(2)}) collective-permute-start(f32[192,768]{1,0:T(8,128)} %dynamic-slice_bitcast_fusion.9), channel_id=1, source_target_pairs={{0,16},{4,20},{8,24},{12,28},{16,0},{20,4},{24,8},{28,12},{1,17},{... | collective-permute-start | bytes 1769480 | tf_op jit(solution)/shard_map/ppermute | solution.py:46
  409.1 36.8 %collective-permute-start.42 = (f16[256,1536]{1,0:T(8,128)(2,1)S(1)}, f16[256,1536]{1,0:T(8,128)(2,1)S(1)}, u32[]{:S(2)}, u32[]{:S(2)}) collective-permute-start(f16[256,1536]{1,0:T(8,128)(2,1)S(1)} %copy-done.38), channel_id=1, source_target_pairs={{0,2},{1,3},{2,0},{3,1},{4,6},{5,7},{6,4},{7,5},{8,10},{9,11},{10,... | collective-permute-start | bytes 2359304 | tf_op jit(solution)/shard_map/ppermute | solution.py:36
  409.9 83.3 %collective-permute-start.41 = (f16[256,1536]{1,0:T(8,128)(2,1)S(1)}, f16[256,1536]{1,0:T(8,128)(2,1)S(1)}, u32[]{:S(2)}, u32[]{:S(2)}) collective-permute-start(f16[256,1536]{1,0:T(8,128)(2,1)S(1)} %copy-done.37), channel_id=1, source_target_pairs={{0,3},{1,0},{2,1},{3,2},{4,7},{5,4},{6,5},{7,6},{8,11},{9,8},{10,9... | collective-permute-start | bytes 2359304 | tf_op jit(solution)/shard_map/ppermute | solution.py:36
  421.5 105.8 %collective-permute-start.58 = (f16[256,1536]{1,0:T(8,128)(2,1)S(1)}, f16[256,1536]{1,0:T(8,128)(2,1)S(1)}, u32[]{:S(2)}, u32[]{:S(2)}) collective-permute-start(f16[256,1536]{1,0:T(8,128)(2,1)S(1)} %fusion.12), channel_id=1, source_target_pairs={{0,1},{1,2},{2,3},{3,0},{4,5},{5,6},{6,7},{7,4},{8,9},{9,10},{10,1... | collective-permute-start | bytes 2359304 | tf_op jit(solution)/shard_map/ppermute | solution.py:36
  422.4 75.8 %collective-permute-start.50 = (f32[2,192,384]{2,1,0:T(8,128)S(1)}, f32[2,192,384]{2,1,0:T(8,128)S(1)}, u32[]{:S(2)}, u32[]{:S(2)}) collective-permute-start(f32[2,192,384]{2,1,0:T(8,128)S(1)} %dynamic-slice_bitcast_fusion.10), channel_id=1, source_target_pairs={{0,16},{4,20},{8,24},{12,28},{16,0},{20,4},{24,8},{28,12},{1,17},{... | collective-permute-start | bytes 1769480 | tf_op jit(solution)/shard_map/ppermute | solution.py:46
  425.4 103.7 %collective-permute-start.57 = (f16[256,1536]{1,0:T(8,128)(2,1)S(1)}, f16[256,1536]{1,0:T(8,128)(2,1)S(1)}, u32[]{:S(2)}, u32[]{:S(2)}) collective-permute-start(f16[256,1536]{1,0:T(8,128)(2,1)S(1)} %fusion.11), channel_id=1, source_target_pairs={{0,2},{1,3},{2,0},{3,1},{4,6},{5,7},{6,4},{7,5},{8,10},{9,11},{10,... | collective-permute-start | bytes 2359304 | tf_op jit(solution)/shard_map/ppermute | solution.py:36
  445.9 85.1 %collective-permute-start.47 = (f16[256,1536]{1,0:T(8,128)(2,1)S(1)}, f16[256,1536]{1,0:T(8,128)(2,1)S(1)}, u32[]{:S(2)}, u32[]{:S(2)}) collective-permute-start(f16[256,1536]{1,0:T(8,128)(2,1)S(1)} %fusion.10), channel_id=1, source_target_pairs={{0,3},{1,0},{2,1},{3,2},{4,7},{5,4},{6,5},{7,6},{8,11},{9,8},{10,9... | collective-permute-start | bytes 2359304 | tf_op jit(solution)/shard_map/ppermute | solution.py:36
  540.9 29.5 %collective-permute-start.65 = (f16[48,2816]{1,0:T(8,128)(2,1)}, f16[48,2816]{1,0:T(8,128)(2,1)}, u32[]{:S(2)}, u32[]{:S(2)}) collective-permute-start(f16[48,2816]{1,0:T(8,128)(2,1)} %get-tuple-element.234), channel_id=1, source_target_pairs={{0,1},{1,2},{2,3},{3,0},{4,5},{5,6},{6,7},{7,4},{8,9},{9,10},{10,1... | collective-permute-start | bytes 811016 | tf_op jit(solution)/shard_map/ppermute | solution.py:36
  542.1 31.0 %collective-permute-start.66 = (f16[48,2816]{1,0:T(8,128)(2,1)}, f16[48,2816]{1,0:T(8,128)(2,1)S(1)}, u32[]{:S(2)}, u32[]{:S(2)}) collective-permute-start(f16[48,2816]{1,0:T(8,128)(2,1)} %get-tuple-element.235), channel_id=1, source_target_pairs={{0,2},{1,3},{2,0},{3,1},{4,6},{5,7},{6,4},{7,5},{8,10},{9,11},{10,... | collective-permute-start | bytes 811016 | tf_op jit(solution)/shard_map/ppermute | solution.py:36
  (126 other events, 1528.3 us)

commit v2 on v1

--- a/solution.py
+++ b/solution.py
@@ -86,6 +86,12 @@
 
 def send_near(stacked, axis):
     return [shift(stacked[turn], axis, lax.axis_size(axis) - turn) for turn in range(1, lax.axis_size(axis))]
+
+
+def slots_of(own_blocks, packed, axis):
+    size, here = lax.axis_size(axis), lax.axis_index(axis)
+    arrived = [shift(pick(packed, (here + turn) % size), axis, turn) for turn in range(1, size)]
+    return [pick(own_blocks, here)] + arrived
 
 
 def gather_direct(block, axis):
@@ -336,7 +342,7 @@
 
 
 def backward_kernel(
-    first, chunks, table_ref, x_ref, x_before_ref, shared_ref, shared_before_ref, step_ref, chan_ref, shared_chan_ref, head_ref,
+    start, chunks, table_ref, x_ref, x_before_ref, shared_ref, shared_before_ref, step_ref, chan_ref, shared_chan_ref, head_ref,
     mixed_ref, mix_grad_ref, state_ref, state_after_ref, carried_in, *refs
 ):
     carried_in = (carried_in,) + refs[:5]
@@ -348,16 +354,19 @@
         delta_all, change_all, run_all, run_rows, meet_grad, keys_grad, read_grad, run_grad, delta_grad, last_grad,
     ) = refs[-31:]
     carried_out = (state_grads, heads_after, shared_after, chan_grad_ref, shared_chan_grad_ref, head_grad_ref)
-    pair, pairs = pl.program_id(0), pl.num_programs(0)
+    turn, pair, pairs = pl.program_id(0), pl.program_id(1), pl.num_programs(1)
+    first = turn == start
     size = x_ref.shape[0]
     base = table_ref[chunks]
 
     @pl.when(pair == 0)
     def _():
-        for new, old in zip(carried_out, carried_in):
-            new[...] = old[...]
-
-        shared_extended[0:8, :] = jnp.zeros(shared_before_ref.shape, jnp.float32) if first else shared_before_ref[...]
+        @pl.when(turn == 0)
+        def _():
+            for new, old in zip(carried_out, carried_in):
+                new[...] = old[...]
+
+        shared_extended[0:8, :] = jnp.where(first, 0.0, shared_before_ref[...])
         shared_extended[8:, :] = shared_ref[...]
         pre = taps_of(shared_extended, size, shared_chan_ref[...], shared_chan_ref[4:5, :])
         shared_pre[...] = pre
@@ -382,7 +391,7 @@
         square_ref[...] = jnp.zeros_like(square_ref)
 
     chan = chan_ref[...]
-    extended[0:8, :] = jnp.zeros(x_before_ref.shape, jnp.float32) if first else x_before_ref[...]
+    extended[0:8, :] = jnp.where(first, 0.0, x_before_ref[...])
     extended[8:, :] = x_ref[...]
     pre = taps_of(extended, size, chan, chan[4:5])
     gain = jax.nn.sigmoid(pre)
@@ -542,7 +551,7 @@
 def run_gate(projected, gated, mixed, up, chan, stats):
     length, wide = gated.shape
     f32 = jnp.float32
-    size = SPAN // 2
+    size = SPAN
     block = pl.BlockSpec((size, wide), lambda c: (c, 0))
     whole = pl.BlockSpec((8, wide), lambda c: (0, 0))
     return pl.pallas_call(
@@ -560,49 +569,50 @@
     )(projected, gated, mixed, up, chan, stats)
 
 
-def run_backward(chunk, table, projected, chan, shared_chan, head_rows, mixed, mix_grad, states, carried, before):
+def run_backward(start, count, table, projected, chan, shared_chan, head_rows, mixed, mix_grad, states, carried, before):
     length, wide = projected.shape[0], chan.shape[1]
     chunks, pairs = length // SPAN, wide // LANES
     f32 = jnp.float32
     lines = SPAN // 8
-    earlier, following = max(chunk - 1, 0), min(chunk + 1, chunks - 1)
-    block = pl.BlockSpec((SPAN, LANES), lambda p, t: (t[chunk], p))
-    flat = pl.BlockSpec((8, 2 * NST), lambda p, t: (0, 0))
-    head = pl.BlockSpec((8, LANES), lambda p, t: (0, 0))
+    earlier = lambda c: jnp.maximum(start - c - 1, 0)
+    following = lambda c: jnp.minimum(start - c + 1, chunks - 1)
+    block = pl.BlockSpec((SPAN, LANES), lambda c, p, t: (t[start - c], p))
+    flat = pl.BlockSpec((8, 2 * NST), lambda c, p, t: (0, 0))
+    head = pl.BlockSpec((8, LANES), lambda c, p, t: (0, 0))
     carries = [
-        pl.BlockSpec((pairs, NST, LANES), lambda p, t: (0, 0, 0)),
-        pl.BlockSpec((pairs, 8, LANES), lambda p, t: (0, 0, 0)),
+        pl.BlockSpec((pairs, NST, LANES), lambda c, p, t: (0, 0, 0)),
+        pl.BlockSpec((pairs, 8, LANES), lambda c, p, t: (0, 0, 0)),
         flat,
-        pl.BlockSpec((pairs, 8, LANES), lambda p, t: (0, 0, 0)),
+        pl.BlockSpec((pairs, 8, LANES), lambda c, p, t: (0, 0, 0)),
         flat,
         head,
     ]
     carried_shapes = [jax.ShapeDtypeStruct(c.shape, f32) for c in carried]
     return pl.pallas_call(
-        functools.partial(backward_kernel, chunk == 0, chunks),
+        functools.partial(backward_kernel, start, chunks),
         grid_spec=pltpu.PrefetchScalarGridSpec(
             num_scalar_prefetch=1,
-            grid=(pairs,),
+            grid=(count, pairs),
             in_specs=[
-                pl.BlockSpec((SPAN, LANES), lambda p, t: (t[chunk], pairs + 2 + p)),
-                pl.BlockSpec((8, LANES), lambda p, t: (t[earlier] * lines + lines - 1, pairs + 2 + p)),
-                pl.BlockSpec((SPAN, 2 * NST), lambda p, t: (t[chunk], pairs // 2)),
-                pl.BlockSpec((8, 2 * NST), lambda p, t: (t[earlier] * lines + lines - 1, pairs // 2)),
-                pl.BlockSpec((SPAN, LANES), lambda p, t: (t[chunk], 2 * pairs + 2)),
-                pl.BlockSpec((8, LANES), lambda p, t: (0, p)),
+                pl.BlockSpec((SPAN, LANES), lambda c, p, t: (t[start - c], pairs + 2 + p)),
+                pl.BlockSpec((8, LANES), lambda c, p, t: (t[earlier(c)] * lines + lines - 1, pairs + 2 + p)),
+                pl.BlockSpec((SPAN, 2 * NST), lambda c, p, t: (t[start - c], pairs // 2)),
+                pl.BlockSpec((8, 2 * NST), lambda c, p, t: (t[earlier(c)] * lines + lines - 1, pairs // 2)),
+                pl.BlockSpec((SPAN, LANES), lambda c, p, t: (t[start - c], 2 * pairs + 2)),
+                pl.BlockSpec((8, LANES), lambda c, p, t: (0, p)),
                 flat,
                 head,
                 block,
                 block,
-                pl.BlockSpec((1, 1, NST, LANES), lambda p, t: (chunk, p, 0, 0)),
-                pl.BlockSpec((1, 1, NST, LANES), lambda p, t: (following, p, 0, 0)),
+                pl.BlockSpec((1, 1, NST, LANES), lambda c, p, t: (start - c, p, 0, 0)),
+                pl.BlockSpec((1, 1, NST, LANES), lambda c, p, t: (following(c), p, 0, 0)),
             ]
             + carries
             + [pl.BlockSpec(memory_space=pl.ANY)] * len(before),
             out_specs=[
-                pl.BlockSpec((SPAN, wide + LANES), lambda p, t: (t[chunk], 0)),
-                pl.BlockSpec((SPAN, LANES), lambda p, t: (t[chunk], 0)),
-                pl.BlockSpec((SPAN, 2 * NST), lambda p, t: (t[chunk], 0)),
+                pl.BlockSpec((SPAN, wide + LANES), lambda c, p, t: (t[start - c], 0)),
+                pl.BlockSpec((SPAN, LANES), lambda c, p, t: (t[start - c], 0)),
+                pl.BlockSpec((SPAN, 2 * NST), lambda c, p, t: (t[start - c], 0)),
             ]
             + carries,
             scratch_shapes=[
@@ -653,13 +663,13 @@
 
 
 class Scatter:
-    def __init__(self, arrays, axis):
+    def __init__(self, arrays, axis, phase=0):
         self.axis = axis
         size = lax.axis_size(axis)
         bits = [1 << k for k in range(size.bit_length() - 1)]
         upper = bits[1:]
         turned = upper[len(upper) // 2 :] + upper[: len(upper) // 2]
-        self.orders = [bits[:1] + (upper if k % 2 == 0 else turned) for k in range(len(arrays))]
+        self.orders = [bits[:1] + (upper if (k + phase) % 2 == 0 else turned) for k in range(len(arrays))]
         self.left = [bits[::-1] for _ in arrays]
         self.blocks = [
             a.reshape((2,) * len(bits) + (a.shape[0] // size,) + a.shape[1:]) for a in arrays
@@ -678,6 +688,36 @@
         while self.done < self.steps:
             self.step()
         return self.blocks
+
+
+def update_kernel(
+    pieces, widths, rate, decay, slot_ref, source_ref, param_ref, first_ref, second_ref,
+    grad_ref, param_out, first_out, second_out,
+):
+    for piece, width in zip(range(pieces), widths):
+        at = sum(widths[:piece])
+        own = slice(at, at + width)
+        grad = source_ref[slot_ref[piece], :, :width]
+        new = adamw_update(param_ref[:, own], grad, first_ref[:, own], second_ref[:, own], rate, decay)
+        grad_ref[:, own] = grad
+        param_out[:, own], first_out[:, own], second_out[:, own] = new
+
+
+def run_update(slots, sources, widths, param, first, second, rate, decay):
+    rows, total = param.shape
+    size = 16 if rows % 16 == 0 else rows
+    block = pl.BlockSpec((size, total), lambda r, t: (r, 0))
+    return pl.pallas_call(
+        functools.partial(update_kernel, len(widths), widths, rate, decay),
+        grid_spec=pltpu.PrefetchScalarGridSpec(
+            num_scalar_prefetch=1,
+            grid=(rows // size,),
+            in_specs=[pl.BlockSpec((sources.shape[0], size, sources.shape[2]), lambda r, t: (0, r, 0))] + [block] * 3,
+            out_specs=[block] * 4,
+        ),
+        out_shape=[jax.ShapeDtypeStruct(param.shape, jnp.float32)] * 4,
+        name="weight_update",
+    )(slots, sources, param, first, second)
 
 
 def adamw_update(param, grad, first, second, rate, decay):
@@ -826,31 +866,42 @@
     pull_sum = sum_near(pull_sum, "seq").reshape(length)
     stats = jnp.stack([scale, scale * scale * scale * (pull_sum / E)])
     stats = jnp.pad(stats, ((0, 6), (0, 0)))
+    out_grad_part = dot(upstream_low.T, normed_low)
+    out_scatter = Scatter([out_grad_part], "dp")
+    out_scatter.step()
     gate_low, mix_grad, gate_square, gain_rows = run_gate(projected, gated, mixed, normed_grad, chan, stats)
     gated_grad = gain_rows[0]
 
     branch_parts = send_near(out_half, "seq")
 
-    out_grad_part = dot(upstream_low.T, normed_low)
-    early = Scatter([out_grad_part, dot(hidden.T, gate_low)], "dp")
+    gate_scatter = Scatter([dot(hidden.T, gate_low)], "dp", 1)
+    gate_scatter.step()
     carried = (
         zeros((pairs, NST, LANES)), zeros((pairs, 8, LANES)), zeros((8, 2 * NST)),
         zeros((pairs, 8, LANES)), zeros((8, 2 * NST)), zeros((8, LANES)),
     )
-    outputs = ()
-    ready = (gate_low,)
-    for turn in range(chunks):
-        if early.done < early.steps and turn != 2:
-            early.step()
+    outputs, early = (), (out_scatter, gate_scatter)
+    calls = [(chunks - 1, chunks - 2 * (chunks // 4)), (2 * (chunks // 4) - 1, chunks // 4), (chunks // 4 - 1, chunks // 4)]
+    for turn, (start, count) in enumerate(calls):
+        ready = tuple(scatter.blocks[0] for scatter in early)
+        if turn < len(calls) - 1:
+            for scatter in early:
+                if scatter.done < scatter.steps:
+                    scatter.step()
+        else:
+            early_sums = jnp.concatenate(
+                [block.reshape(ranks, rows, wide) for scatter in early for block in scatter.finish()], axis=2
+            )
+            early_packed = pack_half(early_sums, jnp.max(jnp.abs(early_sums), axis=-1, keepdims=True))
+            early_slots = slots_of(early_sums, early_packed, "seq")
+            ready = (early_packed,)
         mix_grad = after(mix_grad, *ready)
         result = run_backward(
-            chunks - 1 - turn, table, projected, chan, shared_chan, head_rows, mixed, mix_grad, states, carried, outputs
+            start, count, table, projected, chan, shared_chan, head_rows, mixed, mix_grad, states, carried, outputs
         )
         outputs, carried = tuple(result[:3]), tuple(result[3:])
-        ready = tuple(early.blocks) if turn != 1 else ()
     conv_low, conv_square, shared_grad = outputs
     _, _, _, chan_grad, shared_chan_grad, head_grad = carried
-    early.finish()
 
     largest = jnp.max(gate_square.reshape(ranks, span) + jnp.sum(conv_square.reshape(ranks, span, LANES), axis=2), axis=1)
     bound = 0.1565 * math.sqrt(2 * wide + NHEADS) * jnp.sqrt(largest)
@@ -859,63 +910,50 @@
     lines_of_power = jnp.broadcast_to(power[:, None, None], (ranks, 8, 2 * NST))
     shared_sent = send_near(jnp.concatenate([shared_parts, lines_of_power], axis=1), "seq")
 
-    def hidden_rows(turn):
-        own = slice(turn * span, (turn + 1) * span)
-        return dot(gate_low[own], in_full[:, :wide].T) + dot(conv_low[own], in_full[:, wide + 2 * NST :].T)
-
-    hidden_parts, hidden_halves = [], []
-    for turn in range(1, ranks):
-        hidden_halves.append((hidden_rows(turn) * jnp.exp2(-power[turn])).astype(half))
-        hidden_parts.append(shift(hidden_halves[-1], "seq", ranks - turn))
+    factors = jnp.exp2(-power)[:, None, None]
+    hidden_part = dot(gate_low, in_full[:, :wide].T) + dot(conv_low, in_full[:, wide + 2 * NST :].T)
+    hidden_part = hidden_part.reshape(ranks, span, width)
+    hidden_half = (hidden_part * factors).astype(half)
+    hidden_parts = send_near(hidden_half, "seq")
+
     split = 4 * LANES
     conv_parts = [dot(hidden.T, conv_low[:, :split]), dot(hidden.T, conv_low[:, split:])]
     late = Scatter(conv_parts, "dp")
-    conv_own, normed_own = conv_low[:span], normed_low[:span]
+    normed_own = normed_low[:span]
     for turn in range(late.steps):
         if turn == 1:
-            conv_own, normed_own = after(conv_own, *late.blocks), after(normed_own, *late.blocks)
+            normed_own = after(normed_own, *late.blocks)
+            early_slots = [after(part, *late.blocks) for part in early_slots]
+            chan_grad, shared_chan_grad, head_grad = (
+                after(part, *late.blocks) for part in (chan_grad, shared_chan_grad, head_grad)
+            )
         late.step()
     shared_own = shared_parts[0]
     for part in shared_sent:
         shared_own = shared_own + part[:span]
     shared_own = shared_own.astype(low)
-    hidden_grad = dot(gate_low[:span], in_full[:, :wide].T) + dot(conv_own, in_full[:, wide + 2 * NST :].T)
+    shared_grad_part = dot(hidden_own.T, shared_own)
+    last = Scatter([shared_grad_part], "dp", 1)
+    for turn in range(last.steps):
+        if turn == last.steps - 1:
+            hidden_parts = [after(part, *last.blocks) for part in hidden_parts]
+            power_parts = [after(part, *last.blocks)[span, 0] for part in shared_sent]
+        last.step()
+    hidden_grad = hidden_part[0] + dot(shared_own, in_full[:, wide : wide + 2 * NST].T)
     branch = tokens + dot(normed_own, out_full.T)
     for part in branch_parts:
         branch = branch + part.astype(jnp.float32) * (1.0 / branch_factor)
     block_output = branch[None]
-    last = Scatter([dot(hidden_own.T, shared_own)], "dp")
-    last.finish()
 
     chan_grad = chan_grad.transpose(1, 0, 2).reshape(8, wide)
     kernel_grad, offset_grad = chan_grad[:CONVW], chan_grad[4]
     skip_grad = jnp.sum(chan_grad[5].reshape(heads, HDIM), axis=1)
     kernel_shared_grad, offset_shared_grad = shared_chan_grad[:CONVW], shared_chan_grad[4]
 
-    sums_all = jnp.concatenate(
-        [block.reshape(ranks, rows, -1) for block in (late.blocks + last.blocks + early.blocks)], axis=2
-    )
-    conv_wide = wide + LANES
-    packed_sums = pack_half(sums_all, jnp.max(jnp.abs(sums_all), axis=-1, keepdims=True))
-    hidden_parts = [after(part, packed_sums, block_output) for part in hidden_parts]
-    power_parts = [after(part, packed_sums)[span, 0] for part in shared_sent]
-    collected = sums_all
-    for turn in range(1, ranks):
-        arrived = shift(pick(packed_sums, (rank + turn) % ranks), "seq", turn)
-        collected = lax.dynamic_update_index_in_dim(
-            collected, unpack_half(arrived), (rank + ranks - turn) % ranks, 0
-        )
-    at = conv_wide + 2 * NST
-    shared_sum = sum(collected[j, :, wide:at] for j in range(ranks))
-    grad_in_weight = jnp.concatenate(
-        [collected[j, :, at + wide :] for j in range(ranks)]
-        + [collected[j, :, :wide] for j in range(ranks)]
-        + [shared_sum[:, LANES:], shared_sum[:, : LANES - spare]],
-        axis=1,
-    )
-    grad_out_weight = jnp.concatenate([collected[j, :, at : at + wide] for j in range(ranks)], axis=1)
-
-    hidden_grad = hidden_grad + dot(shared_own, in_full[:, wide : wide + 2 * NST].T)
+    late_sums = jnp.concatenate([block.reshape(ranks, rows, -1) for block in late.blocks + last.blocks], axis=2)
+    late_packed = pack_half(late_sums, jnp.max(jnp.abs(late_sums), axis=-1, keepdims=True))
+    late_slots = slots_of(late_sums, late_packed, "seq")
+
     for part, exponent in zip(hidden_parts, power_parts):
         hidden_grad = hidden_grad + part.astype(jnp.float32) * jnp.exp2(exponent)
     scaled = tokens * inverse
@@ -969,8 +1007,22 @@
     new_norm_gain, new_first_norm_gain, new_second_norm_gain = adamw_update(
         norm_gain, grad_norm_gain, first_norm_gain, second_norm_gain, rate_vector, 0.0
     )
-    new_in_weight, new_first_in_weight, new_second_in_weight = adamw_update(
-        in_weight, grad_in_weight, first_in_weight, second_in_weight, rate_matrix, weight_decay
+    place = (rank + ranks - jnp.arange(ranks, dtype=jnp.int32)) % ranks
+    early_f32 = early_slots[:1] + list(unpack_half(jnp.stack(early_slots[1:])))
+    late_f32 = late_slots[:1] + list(unpack_half(jnp.stack(late_slots[1:])))
+    shared_sum = late_f32[0][:, wide:]
+    for part in late_f32[1:]:
+        shared_sum = shared_sum + part[:, wide:]
+    shared_sum = jnp.concatenate([shared_sum[:, LANES:], shared_sum[:, :LANES]], axis=1)
+    sources = jnp.stack(
+        [part[:, wide:] for part in early_f32]
+        + [part[:, :wide] for part in late_f32]
+        + [jnp.pad(shared_sum, ((0, 0), (0, wide - shared_sum.shape[1])))]
+    )
+    slots = jnp.concatenate([place, place + ranks, jnp.full((1,), 2 * ranks)]).astype(jnp.int32)
+    widths = (wide,) * (2 * ranks) + (in_weight.shape[1] - 2 * E,)
+    grad_in_weight, new_in_weight, new_first_in_weight, new_second_in_weight = run_update(
+        slots, sources, widths, in_weight, first_in_weight, second_in_weight, rate_matrix, weight_decay
     )
     new_conv_weight, new_first_conv_weight, new_second_conv_weight = adamw_update(
         conv_weight, grad_conv_weight, first_conv_weight, second_conv_weight, rate_vector, 0.0
@@ -990,9 +1042,17 @@
     new_gated_gain, new_first_gated_gain, new_second_gated_gain = adamw_update(
         gated_gain, grad_gated_gain, first_gated_gain, second_gated_gain, rate_vector, 0.0
     )
-    new_out_weight, new_first_out_weight, new_second_out_weight = adamw_update(
-        out_weight, grad_out_weight, first_out_weight, second_out_weight, rate_matrix, weight_decay
-    )
+    grad_out_weight, new_out_weight, new_first_out_weight, new_second_out_weight = run_update(
+        place,
+        jnp.stack([part[:, :wide] for part in early_f32]),
+        (wide,) * ranks,
+        out_weight,
+        first_out_weight,
+        second_out_weight,
+        rate_matrix,
+        weight_decay,
+    )
+
     return (
         block_output,
         input_grad,

time: 601 us -> 604 us (level)
  the two profiles are of different devices: /device:TPU:16 before, /device:TPU:0 now
where the time goes in v2:
time: 604 us; the launch traced here: 593 us
  starting transfers between devices  160 us (26%)
  waiting for transfers between devices  152 us (25%)
  Pallas kernels  99.8 us (17%)
  local copies, waits for them, and re-layouts  65.6 us (11%)
  matrix products  55.2 us (9%)
  other arithmetic  54.9 us (9%)
    ppermute x32, starting transfers between devices, shift(): lax.ppermute(block, axis, [(i, (i + distance) % size) for i in range(size)])  115 us
    ppermute x32, waiting for transfers between devices, shift(): lax.ppermute(block, axis, [(i, (i + distance) % size) for i in range(size)])  56.6 us
    dot_general x12, matrix products, dot(): return jnp.dot(left, right, preferred_element_type=jnp.float32)  55.2 us
    pallas_call x3, Pallas kernels, run_backward(): pl.pallas_call(functools.partial(backward_kernel, start, chunks), grid_sp...  52 us
    ppermute x33, waiting for transfers between devices, swap(): lax.ppermute(block, axis, [(i, i ^ bit) for i in range(lax.axis_size(axis...  50 us
    ppermute x33, starting transfers between devices, swap(): lax.ppermute(block, axis, [(i, i ^ bit) for i in range(lax.axis_size(axis...  31.9 us
    ppermute x2, waiting for transfers between devices, near_parts(): far = lax.ppermute(across, axis, [(2, 3), (1, 0)])  30.2 us
    pallas_call x1, Pallas kernels, run_forward(): pl.pallas_call(forward_kernel, grid_spec=pltpu.PrefetchScalarGridSpec(num...  27.8 us
  transfers between devices with their start and end apart: 71, of which 31 were waited for; matrix products, arithmetic and copies ran while one was open for 24% of the time, Pallas kernels for 11%

profile of v2, /device:TPU:0, one launch (start us, length us, event | category | flops | bytes accessed | tf_op | source)
XLA Modules:
  0.0 592.8 jit_solution(11608801043468107020)
XLA Ops:
  74.3 8.0 %collective-permute-done.13 = bf16[2,1,1,96,1920]{4,3,2,1,0:T(8,128)(2,1)S(1)} collective-permute-done((bf16[2,1,1,96,1920]{4,3,2,1,0:T(8,128)(2,1)S(1)}, bf16[2,1,1,96,1920]{4,3,2,1,0:T(8,128)(2,1)S(1)}, u32[]{:S(2)}, u32[]{:S(2)}) %collective-permute-start.13) | collective-permute-done | bytes 737312 | tf_op jit(solution)/shard_map/ppermute | solution.py:46
  83.9 6.0 %collective-permute-done.10 = bf16[1,2,1,96,1920]{4,3,2,1,0:T(8,128)(2,1)S(1)} collective-permute-done((bf16[1,2,1,96,1920]{4,3,2,1,0:T(8,128)(2,1)S(1)}, bf16[1,2,1,96,1920]{4,3,2,1,0:T(8,128)(2,1)S(1)}, u32[]{:S(2)}, u32[]{:S(2)}) %collective-permute-start.10) | collective-permute-done | bytes 737312 | tf_op jit(solution)/shard_map/ppermute | solution.py:46
  92.4 10.6 %collective-permute-done.24 = bf16[256,1536]{1,0:T(8,128)(2,1)S(1)} collective-permute-done((bf16[256,1536]{1,0:T(8,128)(2,1)S(1)}, bf16[256,1536]{1,0:T(8,128)(2,1)S(1)}, u32[]{:S(2)}, u32[]{:S(2)}) %collective-permute-start.24) | collective-permute-done | bytes 786464 | tf_op jit(solution)/shard_map/ppermute | solution.py:42
  103.0 16.2 %collective-permute-done.22 = bf16[256,1536]{1,0:T(8,128)(2,1)S(1)} collective-permute-done((bf16[256,1536]{1,0:T(8,128)(2,1)}, bf16[256,1536]{1,0:T(8,128)(2,1)S(1)}, u32[]{:S(2)}, u32[]{:S(2)}) %collective-permute-start.22) | collective-permute-done | bytes 786464 | tf_op jit(solution)/shard_map/ppermute | solution.py:83
  124.6 8.7 %fusion.90.z_ref.x_ref.shared_ref.step_ref.x_before_ref.shared_before_ref = f32[1024,1920]{1,0:T(8,128)} fusion(bf16[1024,1536]{1,0:T(8,128)(2,1)S(1)} %bitcast.353, bf16[1536,1920]{1,0:T(8,128)(2,1)S(1)} %bitcast.372), kind=kOutput, calls=%fused_computation.355 | convolution fusion | flops 6039797760 | bytes 16908288 | tf_op jit(solution)/shard_map/dot_general | solution.py:735
  133.3 27.8 %mixer_forward.1 = (f32[1024,768]{1,0:T(8,128)}, f32[1024,768]{1,0:T(8,128)}, f32[4,6,128,128]{3,2,1,0:T(8,128)}, f32[1024,128]{1,0:T(8,128)}) custom-call(s32[5]{0:T(128)} %pad_add_fusion.table_ref, f32[1024,1920]{1,0:T(8,128)} %fusion.90.z_ref.x_ref.shared_ref.step_ref.x_before_ref.shared_before_ref, ...), custom_call_target="tpu_custom_call" | custom-call | tf_op jit(solution)/shard_map/mixer_forward/pallas_call | solution.py:505
  178.0 8.6 %collective-permute-done.25 = f32[4,2,128]{2,1,0:T(2,128)S(1)} collective-permute-done((f32[4,2,128]{2,1,0:T(2,128)S(1)}, f32[4,2,128]{2,1,0:T(2,128)S(1)}, u32[]{:S(2)}, u32[]{:S(2)}) %collective-permute-start.25) | collective-permute-done | bytes 4128 | tf_op jit(solution)/shard_map/ppermute | solution.py:36
  186.6 15.2 %collective-permute-done.26 = f32[4,2,128]{2,1,0:T(2,128)S(1)} collective-permute-done((f32[4,2,128]{2,1,0:T(2,128)S(1)}, f32[4,2,128]{2,1,0:T(2,128)S(1)}, u32[]{:S(2)}, u32[]{:S(2)}) %collective-permute-start.26) | collective-permute-done | bytes 4128 | tf_op jit(solution)/shard_map/ppermute | solution.py:36
  214.8 14.0 %collective-permute-done.29 = bf16[256,1536]{1,0:T(8,128)(2,1)S(1)} collective-permute-done((bf16[256,1536]{1,0:T(8,128)(2,1)}, bf16[256,1536]{1,0:T(8,128)(2,1)S(1)}, u32[]{:S(2)}, u32[]{:S(2)}) %collective-permute-start.29) | collective-permute-done | bytes 786464 | tf_op jit(solution)/shard_map/ppermute | solution.py:83
  250.8 8.4 %gate_backward.1 = (bf16[1024,768]{1,0:T(8,128)(2,1)}, f32[1024,768]{1,0:T(8,128)}, f32[1024,1]{1,0:T(8,128)}, f32[8,768]{1,0:T(8,128)}) custom-call(f32[1024,1920]{1,0:T(8,128)} %fusion.90.z_ref.x_ref.shared_ref.step_ref.x_before_ref.shared_before_ref, f32[1024,768]{1,0:T(8,128)} %get-tuple-element.114.gated_ref, f32[1024,768]{1,0:T(8,128)} %get-tuple-element.116.mixed_ref, ...), custom_call_target="tpu_custom_call" | custom-call | tf_op jit(solution)/shard_map/gate_backward/pallas_call | solution.py:557
  289.0 25.0 %mixer_backward.3 = (bf16[1024,896]{1,0:T(8,128)(2,1)}, f32[1024,128]{1,0:T(8,128)}, f32[1024,256]{1,0:T(8,128)}, f32[6,128,128]{2,1,0:T(8,128)}, f32[6,8,128]{2...) custom-call(s32[5]{0:T(128)} %pad_add_fusion.table_ref, ...), custom_call_target="tpu_custom_call" | custom-call | tf_op jit(solution)/shard_map/mixer_backward/pallas_call | solution.py:591
  319.9 13.3 %mixer_backward.4 = (bf16[1024,896]{1,0:T(8,128)(2,1)}, f32[1024,128]{1,0:T(8,128)}, f32[1024,256]{1,0:T(8,128)}, f32[6,128,128]{2,1,0:T(8,128)}, f32[6,8,128]{2...) custom-call(s32[5]{0:T(128)} %pad_add_fusion.table_ref, ...), custom_call_target="tpu_custom_call", output_to_operand_aliasing={{0}: (19, {}), {1}: (20, {}), {2}: (21, {})} | custom-call | tf_op jit(solution)/shard_map/mixer_backward/pallas_call | solution.py:591
  333.2 13.7 %mixer_backward.5 = (bf16[1024,896]{1,0:T(8,128)(2,1)}, f32[1024,128]{1,0:T(8,128)}, f32[1024,256]{1,0:T(8,128)}, f32[6,128,128]{2,1,0:T(8,128)}, f32[6,8,128]{2...) custom-call(s32[5]{0:T(128)} %pad_add_fusion.table_ref, ...), custom_call_target="tpu_custom_call", output_to_operand_aliasing={{0}: (19, {}), {1}: (20, {}), {2}: (21, {})} | custom-call | tf_op jit(solution)/shard_map/mixer_backward/pallas_call | solution.py:591
  346.9 5.8 fusion.16
  354.5 8.0 %fusion.5 = f32[1024,1536]{1,0:T(8,128)} fusion(bf16[1024,896]{1,0:T(8,128)(2,1)S(1)} %copy-done.11, bf16[1536,1920]{1,0:T(8,128)(2,1)} %bitcast.373), kind=kOutput, calls=%fused_computation.16 | convolution fusion | flops 2818572288 | bytes 10878976 | tf_op jit(solution)/shard_map/dot_general | solution.py:735
  370.5 5.5 convolution_add_fusion
  385.3 5.7 collective-permute-start.53
  397.7 5.8 collective-permute-done.40
  411.8 8.5 %collective-permute-done.51 = f32[2,192,256]{2,1,0:T(8,128)S(1)} collective-permute-done((f32[2,192,256]{2,1,0:T(8,128)S(1)}, f32[2,192,256]{2,1,0:T(8,128)S(1)}, u32[]{:S(2)}, u32[]{:S(2)}) %collective-permute-start.51) | collective-permute-done | bytes 393248 | tf_op jit(solution)/shard_map/ppermute | solution.py:46
  421.6 31.3 %collective-permute-start.44 = (f16[256,1536]{1,0:T(8,128)(2,1)}, f16[256,1536]{1,0:T(8,128)(2,1)}, u32[]{:S(2)}, u32[]{:S(2)}) collective-permute-start(f16[256,1536]{1,0:T(8,128)(2,1)} %get-tuple-element.216), channel_id=1, source_target_pairs={{0,2},{1,3},{2,0},{3,1},{4,6},{5,7},{6,4},{7,5},{8,10},{9,11},{10,... | collective-permute-start | bytes 2359304 | tf_op jit(solution)/shard_map/ppermute | solution.py:36
  454.2 25.0 %collective-permute-start.62 = (f16[48,1664]{1,0:T(8,128)(2,1)}, f16[48,1664]{1,0:T(8,128)(2,1)}, u32[]{:S(2)}, u32[]{:S(2)}) collective-permute-start(f16[48,1664]{1,0:T(8,128)(2,1)} %get-tuple-element.262), channel_id=1, source_target_pairs={{0,3},{1,0},{2,1},{3,2},{4,7},{5,4},{6,5},{7,6},{8,11},{9,8},{10,9... | collective-permute-start | bytes 479240 | tf_op jit(solution)/shard_map/ppermute | solution.py:36
  495.8 11.4 %collective-permute-done.61 = f16[48,1664]{1,0:T(8,128)(2,1)} collective-permute-done((f16[48,1664]{1,0:T(8,128)(2,1)}, f16[48,1664]{1,0:T(8,128)(2,1)}, u32[]{:S(2)}, u32[]{:S(2)}) %collective-permute-start.61) | collective-permute-done | bytes 159776 | tf_op jit(solution)/shard_map/ppermute | solution.py:36
  540.2 10.7 %collective-permute-start.59 = (f32[7,128]{1,0:T(8,128)S(1)}, f32[7,128]{1,0:T(8,128)S(1)}, u32[]{:S(2)}, u32[]{:S(2)}) collective-permute-start(f32[7,128]{1,0:T(8,128)S(1)} %get-tuple-element.297), channel_id=1, source_target_pairs={{0,3},{1,0},{2,1},{3,2},{4,7},{5,4},{6,5},{7,6},{8,11},{9,8},{10,9... | collective-permute-start | bytes 10760 | tf_op jit(solution)/shard_map/ppermute | solution.py:36
  585.9 6.7 %weight_update.2 = (f32[48,6448]{1,0:T(8,128)}, f32[48,6448]{1,0:T(8,128)}, f32[48,6448]{1,0:T(8,128)}, f32[48,6448]{1,0:T(8,128)}) custom-call(s32[9]{0:T(128)} %pad_add_fusion.1.slot_ref, f32[9,48,768]{2,1,0:T(8,128)} %fusion.34.source_ref, f32[48,6448]{1,0:T(8,128)} %param_ref.2, f32[48,6448]{1,0:T(8,128)} %first_ref.2, f32[48,6448]{1,0:T(8,128)} %second_ref.2), custom_call_target="tpu_custom_call" | custom-call | tf_op jit(solution)/shard_map/weight_update/pallas_call | solution.py:710
  (541 shorter events, 288.2 us)
Async XLA Ops:
  14.7 30.5 %collective-permute-start.6 = (bf16[48,2688]{1,0:T(8,128)(2,1)}, bf16[48,2688]{1,0:T(8,128)(2,1)}, u32[]{:S(2)}, u32[]{:S(2)}) collective-permute-start(bf16[48,2688]{1,0:T(8,128)(2,1)} %get-tuple-element.284), channel_id=1, source_target_pairs={{0,1},{1,2},{2,3},{3,0},{4,5},{5,6},{6,7},{7,4},{8,9},{9,10},{10,1... | collective-permute-start | bytes 774152 | tf_op jit(solution)/shard_map/ppermute | solution.py:36
  30.6 43.6 %collective-permute-start.21 = (bf16[256,1536]{1,0:T(8,128)(2,1)S(1)}, bf16[256,1536]{1,0:T(8,128)(2,1)}, u32[]{:S(2)}, u32[]{:S(2)}) collective-permute-start(bf16[256,1536]{1,0:T(8,128)(2,1)S(1)} %multiply_convert_fusion.3), channel_id=1, source_target_pairs={{0,2},{1,3},{2,0},{3,1},{4,6},{5,7},{6,4},{7,5},{8,10},{9,11},{10,... | collective-permute-start | bytes 2359304 | tf_op jit(solution)/shard_map/ppermute | solution.py:36
  31.7 60.7 %collective-permute-start.23 = (bf16[256,1536]{1,0:T(8,128)(2,1)S(1)}, bf16[256,1536]{1,0:T(8,128)(2,1)}, u32[]{:S(2)}, u32[]{:S(2)}) collective-permute-start(bf16[256,1536]{1,0:T(8,128)(2,1)S(1)} %multiply_convert_fusion.3), channel_id=1, source_target_pairs={{0,1},{1,2},{2,3},{4,5},{5,6},{6,7},{8,9},{9,10},{10,11},{12,13},{... | collective-permute-start | bytes 2359304 | tf_op jit(solution)/shard_map/ppermute | solution.py:42
  69.5 33.5 %collective-permute-start.24 = (bf16[256,1536]{1,0:T(8,128)(2,1)S(1)}, bf16[256,1536]{1,0:T(8,128)(2,1)S(1)}, u32[]{:S(2)}, u32[]{:S(2)}) collective-permute-start(bf16[256,1536]{1,0:T(8,128)(2,1)S(1)} %multiply_convert_fusion.3), channel_id=1, source_target_pairs={{1,0},{2,1},{3,2},{5,4},{6,5},{7,6},{9,8},{10,9},{11,10},{13,12},{... | collective-permute-start | bytes 2359304 | tf_op jit(solution)/shard_map/ppermute | solution.py:42
  82.3 37.0 %collective-permute-start.22 = (bf16[256,1536]{1,0:T(8,128)(2,1)}, bf16[256,1536]{1,0:T(8,128)(2,1)S(1)}, u32[]{:S(2)}, u32[]{:S(2)}) collective-permute-start(bf16[256,1536]{1,0:T(8,128)(2,1)} %collective-permute-done.21), channel_id=1, source_target_pairs={{2,3},{1,0},{6,7},{5,4},{10,11},{9,8},{14,15},{13,12},{18,19},{17,... | collective-permute-start | bytes 2359304 | tf_op jit(solution)/shard_map/ppermute | solution.py:83
  89.8 29.5 %collective-permute-start.14 = (bf16[2,2,1,96,1920]{4,3,2,1,0:T(8,128)(2,1)S(1)}, bf16[2,2,1,96,1920]{4,3,2,1,0:T(8,128)(2,1)S(1)}, u32[]{:S(2)}, u32[]{:S(2)}) collective-permute-start(bf16[2,2,1,96,1920]{4,3,2,1,0:T(8,128)(2,1)S(1)} %pad_maximum_fusion.3), channel_id=1, source_target_pairs={{0,4},{4,0},{8,12},{12,8},{16,20},{20,16},{24,28},{28,24},{1,5},{5... | collective-permute-start | bytes 4423688 | tf_op jit(solution)/shard_map/ppermute | solution.py:46
  90.2 29.5 %collective-permute-start.11 = (bf16[2,2,1,96,1920]{4,3,2,1,0:T(8,128)(2,1)S(1)}, bf16[2,2,1,96,1920]{4,3,2,1,0:T(8,128)(2,1)S(1)}, u32[]{:S(2)}, u32[]{:S(2)}) collective-permute-start(bf16[2,2,1,96,1920]{4,3,2,1,0:T(8,128)(2,1)S(1)} %pad_maximum_fusion.2), channel_id=1, source_target_pairs={{0,4},{4,0},{8,12},{12,8},{16,20},{20,16},{24,28},{28,24},{1,5},{5... | collective-permute-start | bytes 4423688 | tf_op jit(solution)/shard_map/ppermute | solution.py:46
  163.3 38.5 %collective-permute-start.28 = (bf16[256,1536]{1,0:T(8,128)(2,1)}, bf16[256,1536]{1,0:T(8,128)(2,1)}, u32[]{:S(2)}, u32[]{:S(2)}) collective-permute-start(bf16[256,1536]{1,0:T(8,128)(2,1)} %bitcast_convert_fusion), channel_id=1, source_target_pairs={{0,2},{1,3},{2,0},{3,1},{4,6},{5,7},{6,4},{7,5},{8,10},{9,11},{10,... | collective-permute-start | bytes 2359304 | tf_op jit(solution)/shard_map/ppermute | solution.py:36
  165.6 36.2 %collective-permute-start.26 = (f32[4,2,128]{2,1,0:T(2,128)S(1)}, f32[4,2,128]{2,1,0:T(2,128)S(1)}, u32[]{:S(2)}, u32[]{:S(2)}) collective-permute-start(f32[4,2,128]{2,1,0:T(2,128)S(1)} %bitcast.416), channel_id=1, source_target_pairs={{0,2},{1,3},{2,0},{3,1},{4,6},{5,7},{6,4},{7,5},{8,10},{9,11},{10,... | collective-permute-start | bytes 12296 | tf_op jit(solution)/shard_map/ppermute | solution.py:36
  168.3 41.8 %collective-permute-start.30 = (bf16[256,1536]{1,0:T(8,128)(2,1)}, bf16[256,1536]{1,0:T(8,128)(2,1)}, u32[]{:S(2)}, u32[]{:S(2)}) collective-permute-start(bf16[256,1536]{1,0:T(8,128)(2,1)} %bitcast_convert_fusion), channel_id=1, source_target_pairs={{0,1},{1,2},{2,3},{4,5},{5,6},{6,7},{8,9},{9,10},{10,11},{12,13},{... | collective-permute-start | bytes 2359304 | tf_op jit(solution)/shard_map/ppermute | solution.py:42
  176.5 38.3 %collective-permute-start.31 = (bf16[256,1536]{1,0:T(8,128)(2,1)}, bf16[256,1536]{1,0:T(8,128)(2,1)S(1)}, u32[]{:S(2)}, u32[]{:S(2)}) collective-permute-start(bf16[256,1536]{1,0:T(8,128)(2,1)} %bitcast_convert_fusion), channel_id=1, source_target_pairs={{1,0},{2,1},{3,2},{5,4},{6,5},{7,6},{9,8},{10,9},{11,10},{13,12},{... | collective-permute-start | bytes 2359304 | tf_op jit(solution)/shard_map/ppermute | solution.py:42
  271.5 42.6 %collective-permute-start.37 = (f32[2,192,768]{2,1,0:T(8,128)S(1)}, f32[2,192,768]{2,1,0:T(8,128)}, u32[]{:S(2)}, u32[]{:S(2)}) collective-permute-start(f32[2,192,768]{2,1,0:T(8,128)S(1)} %dynamic-slice_bitcast_fusion.5), channel_id=1, source_target_pairs={{0,8},{4,12},{8,0},{12,4},{16,24},{20,28},{24,16},{28,20},{1,9},{5... | collective-permute-start | bytes 3538952 | tf_op jit(solution)/shard_map/ppermute | solution.py:46
  276.9 40.5 %collective-permute-start.38 = (f32[2,192,768]{2,1,0:T(8,128)}, f32[2,192,768]{2,1,0:T(8,128)}, u32[]{:S(2)}, u32[]{:S(2)}) collective-permute-start(f32[2,192,768]{2,1,0:T(8,128)} %dynamic-slice_bitcast_fusion.4), channel_id=1, source_target_pairs={{0,16},{4,20},{8,24},{12,28},{16,0},{20,4},{24,8},{28,12},{1,17},{... | collective-permute-start | bytes 3538952 | tf_op jit(solution)/shard_map/ppermute | solution.py:46
  283.0 235.9 %collective-permute-start.45 = (f16[256,1536]{1,0:T(8,128)(2,1)}, f16[256,1536]{1,0:T(8,128)(2,1)}, u32[]{:S(2)}, u32[]{:S(2)}) collective-permute-start(f16[256,1536]{1,0:T(8,128)(2,1)} %get-tuple-element.215), channel_id=1, source_target_pairs={{0,1},{1,2},{2,3},{3,0},{4,5},{5,6},{6,7},{7,4},{8,9},{9,10},{10,1... | collective-permute-start | bytes 2359304 | tf_op jit(solution)/shard_map/ppermute | solution.py:36
  316.9 76.2 %collective-permute-start.39 = (f32[192,768]{1,0:T(8,128)}, f32[192,768]{1,0:T(8,128)}, u32[]{:S(2)}, u32[]{:S(2)}) collective-permute-start(f32[192,768]{1,0:T(8,128)} %dynamic-slice_bitcast_fusion.10), channel_id=1, source_target_pairs={{0,16},{4,20},{8,24},{12,28},{16,0},{20,4},{24,8},{28,12},{1,17},{... | collective-permute-start | bytes 1769480 | tf_op jit(solution)/shard_map/ppermute | solution.py:46
  385.3 36.3 %collective-permute-start.53 = (f16[256,1536]{1,0:T(8,128)(2,1)S(1)}, f16[256,1536]{1,0:T(8,128)(2,1)S(1)}, u32[]{:S(2)}, u32[]{:S(2)}) collective-permute-start(f16[256,1536]{1,0:T(8,128)(2,1)S(1)} %get-tuple-element.212), channel_id=1, source_target_pairs={{0,1},{1,2},{2,3},{3,0},{4,5},{5,6},{6,7},{7,4},{8,9},{9,10},{10,1... | collective-permute-start | bytes 2359304 | tf_op jit(solution)/shard_map/ppermute | solution.py:36
  393.1 61.0 %collective-permute-start.52 = (f16[256,1536]{1,0:T(8,128)(2,1)S(1)}, f16[256,1536]{1,0:T(8,128)(2,1)S(1)}, u32[]{:S(2)}, u32[]{:S(2)}) collective-permute-start(f16[256,1536]{1,0:T(8,128)(2,1)S(1)} %get-tuple-element.213), channel_id=1, source_target_pairs={{0,2},{1,3},{2,0},{3,1},{4,6},{5,7},{6,4},{7,5},{8,10},{9,11},{10,... | collective-permute-start | bytes 2359304 | tf_op jit(solution)/shard_map/ppermute | solution.py:36
  405.8 74.5 %collective-permute-start.49 = (f16[256,1536]{1,0:T(8,128)(2,1)S(1)}, f16[256,1536]{1,0:T(8,128)(2,1)S(1)}, u32[]{:S(2)}, u32[]{:S(2)}) collective-permute-start(f16[256,1536]{1,0:T(8,128)(2,1)S(1)} %get-tuple-element.211), channel_id=1, source_target_pairs={{0,3},{1,0},{2,1},{3,2},{4,7},{5,4},{6,5},{7,6},{8,11},{9,8},{10,9... | collective-permute-start | bytes 2359304 | tf_op jit(solution)/shard_map/ppermute | solution.py:36
  420.3 69.5 %collective-permute-start.41 = (f32[2,2,192,512]{3,2,1,0:T(8,128)}, f32[2,2,192,512]{3,2,1,0:T(8,128)}, u32[]{:S(2)}, u32[]{:S(2)}) collective-permute-start(f32[2,2,192,512]{3,2,1,0:T(8,128)} %dynamic-slice_bitcast_fusion.2), channel_id=1, source_target_pairs={{0,4},{4,0},{8,12},{12,8},{16,20},{20,16},{24,28},{28,24},{1,5},{5... | collective-permute-start | bytes 4718600 | tf_op jit(solution)/shard_map/ppermute | solution.py:46
  421.6 97.4 %collective-permute-start.44 = (f16[256,1536]{1,0:T(8,128)(2,1)}, f16[256,1536]{1,0:T(8,128)(2,1)}, u32[]{:S(2)}, u32[]{:S(2)}) collective-permute-start(f16[256,1536]{1,0:T(8,128)(2,1)} %get-tuple-element.216), channel_id=1, source_target_pairs={{0,2},{1,3},{2,0},{3,1},{4,6},{5,7},{6,4},{7,5},{8,10},{9,11},{10,... | collective-permute-start | bytes 2359304 | tf_op jit(solution)/shard_map/ppermute | solution.py:36
  454.2 38.1 %collective-permute-start.62 = (f16[48,1664]{1,0:T(8,128)(2,1)}, f16[48,1664]{1,0:T(8,128)(2,1)}, u32[]{:S(2)}, u32[]{:S(2)}) collective-permute-start(f16[48,1664]{1,0:T(8,128)(2,1)} %get-tuple-element.262), channel_id=1, source_target_pairs={{0,3},{1,0},{2,1},{3,2},{4,7},{5,4},{6,5},{7,6},{8,11},{9,8},{10,9... | collective-permute-start | bytes 479240 | tf_op jit(solution)/shard_map/ppermute | solution.py:36
  492.3 31.7 %collective-permute-start.43 = (f16[256,1536]{1,0:T(8,128)(2,1)}, f16[256,1536]{1,0:T(8,128)(2,1)}, u32[]{:S(2)}, u32[]{:S(2)}) collective-permute-start(f16[256,1536]{1,0:T(8,128)(2,1)} %get-tuple-element.214), channel_id=1, source_target_pairs={{0,3},{1,0},{2,1},{3,2},{4,7},{5,4},{6,5},{7,6},{8,11},{9,8},{10,9... | collective-permute-start | bytes 2359304 | tf_op jit(solution)/shard_map/ppermute | solution.py:36
  507.2 51.3 %collective-permute-start.65 = (f32[2,192,384]{2,1,0:T(8,128)}, f32[2,192,384]{2,1,0:T(8,128)}, u32[]{:S(2)}, u32[]{:S(2)}) collective-permute-start(f32[2,192,384]{2,1,0:T(8,128)} %dynamic-slice_bitcast_fusion.8), channel_id=1, source_target_pairs={{0,16},{4,20},{8,24},{12,28},{16,0},{20,4},{24,8},{28,12},{1,17},{... | collective-permute-start | bytes 1769480 | tf_op jit(solution)/shard_map/ppermute | solution.py:46
  508.7 42.3 %collective-permute-start.67 = (f32[192,256]{1,0:T(8,128)}, f32[192,256]{1,0:T(8,128)}, u32[]{:S(2)}, u32[]{:S(2)}) collective-permute-start(f32[192,256]{1,0:T(8,128)} %dynamic-slice_bitcast_fusion.15), channel_id=1, source_target_pairs={{0,8},{4,12},{8,0},{12,4},{16,24},{20,28},{24,16},{28,20},{1,9},{5... | collective-permute-start | bytes 589832 | tf_op jit(solution)/shard_map/ppermute | solution.py:46
  (124 other events, 1611.2 us)

commit v3 on v2

--- a/solution.py
+++ b/solution.py
@@ -16,6 +16,8 @@
 CONVW = 4
 SPAN = 256
 LANES = 128
+MIB = 2**20
+SEQ, DP = "seq", "dp"
 
 
 low = jnp.bfloat16
@@ -143,20 +145,6 @@
         jnp.concatenate(parts[2 * k : 2 * k + 2], axis=len(bits)).reshape(-1, block.shape[1])
         for k, block in enumerate(blocks)
     ]
-
-
-def scatter_bits(stacked, axis):
-    here, size = lax.axis_index(axis), lax.axis_size(axis)
-    bit = 1
-    rest = stacked
-    while bit < size:
-        pairs = rest.reshape((rest.shape[0] // 2, 2) + rest.shape[1:])
-        own = (here & bit) // bit
-        keep = lax.dynamic_index_in_dim(pairs, own, 1, keepdims=False)
-        send = lax.dynamic_index_in_dim(pairs, 1 - own, 1, keepdims=False)
-        rest = keep + swap(send, axis, bit)
-        bit *= 2
-    return rest[0]
 
 
 def halves(value):
@@ -544,6 +532,7 @@
             jax.ShapeDtypeStruct((chunks, pairs, NST, LANES), f32),
             jax.ShapeDtypeStruct((length, LANES), f32),
         ],
+        compiler_params=pltpu.CompilerParams(vmem_limit_bytes=20 * MIB),
         name="mixer_forward",
     )(table, projected, projected, projected, projected, chan, shared_chan, head_rows)
 
@@ -565,6 +554,7 @@
             jax.ShapeDtypeStruct((length, 1), f32),
             jax.ShapeDtypeStruct((8, wide), f32),
         ],
+        compiler_params=pltpu.CompilerParams(vmem_limit_bytes=20 * MIB),
         name="gate_backward",
     )(projected, gated, mixed, up, chan, stats)
 
@@ -647,6 +637,7 @@
         ]
         + carried_shapes,
         input_output_aliases={19 + k: k for k in range(len(before))},
+        compiler_params=pltpu.CompilerParams(vmem_limit_bytes=50 * MIB),
         name="mixer_backward",
     )(
         table, projected, projected, projected, projected, projected, chan, shared_chan, head_rows,
@@ -716,6 +707,7 @@
             out_specs=[block] * 4,
         ),
         out_shape=[jax.ShapeDtypeStruct(param.shape, jnp.float32)] * 4,
+        compiler_params=pltpu.CompilerParams(vmem_limit_bytes=20 * MIB),
         name="weight_update",
     )(slots, sources, param, first, second)
 
@@ -723,8 +715,8 @@
 def adamw_update(param, grad, first, second, rate, decay):
     first_new = beta_one * first + (1.0 - beta_one) * grad
     second_new = beta_two * second + (1.0 - beta_two) * grad * grad
-    corrected_first = first_new / (1.0 - beta_one**adam_step)
-    corrected_second = second_new / (1.0 - beta_two**adam_step)
+    corrected_first = first_new * (1.0 / (1.0 - beta_one**adam_step))
+    corrected_second = second_new * (1.0 / (1.0 - beta_two**adam_step))
     param_new = param - rate * (
         corrected_first / (jnp.sqrt(corrected_second) + adam_eps) + decay * param
     )
@@ -766,8 +758,8 @@
     first_out_weight,
     second_out_weight,
 ):
-    ranks, rank = lax.axis_size("seq"), lax.axis_index("seq")
-    groups = lax.axis_size("dp")
+    ranks, rank = lax.axis_size(SEQ), lax.axis_index(SEQ)
+    groups = lax.axis_size(DP)
     devices = ranks * groups
     wide, heads = E // ranks, NHEADS // ranks
     rows = in_weight.shape[0]
@@ -784,8 +776,8 @@
     filled = packed.shape[0]
     lines = -(-filled // LANES)
     packed = jnp.pad(packed, (0, lines * LANES - filled)).reshape(lines, LANES)
-    small_line = gather_direct(packed, "seq")
-    small = gather_bits(small_line, "dp")
+    small_line = gather_direct(packed, SEQ)
+    small = gather_bits(small_line, DP)
     small = small.reshape(devices, lines * LANES)
     norm_float = small[:, :rows].reshape(-1)
     kernel_float = small[:, rows : rows + CONVW * taps].reshape(devices, CONVW, taps)
@@ -815,7 +807,7 @@
     columns = 2 * NST + 2 * wide + LANES
     weights_arrived = []
     for turn in range(1, ranks):
-        weights_arrived.append(shift(for_rank((rank + turn) % ranks), "seq", turn))
+        weights_arrived.append(shift(for_rank((rank + turn) % ranks), SEQ, turn))
 
     tokens, upstream = block_input[0], cotangent[0]
     span = tokens.shape[0]
@@ -830,11 +822,11 @@
             weight_rows, weights_arrived[turn - 1], (rank + ranks - turn) % ranks, 0
         )
     weight_rows = weight_rows.reshape(ranks * rows, columns + wide)
-    in_full, out_full = gather_rows([weight_rows[:, :columns], weight_rows[:, columns:]], "dp")
-
-    line_parts = near_parts(hidden_own, "seq")
+    in_full, out_full = gather_rows([weight_rows[:, :columns], weight_rows[:, columns:]], DP)
+
+    line_parts = near_parts(hidden_own, SEQ)
     line_parts = [after(part, in_full, out_full) for part in line_parts]
-    up_parts = near_parts(after(upstream.astype(low), *line_parts), "seq")
+    up_parts = near_parts(after(upstream.astype(low), *line_parts), SEQ)
     hidden = jnp.stack(line_parts).reshape(length, width)
 
     projected = dot(hidden, in_full)
@@ -854,7 +846,7 @@
     zeros = functools.partial(jnp.zeros, dtype=jnp.float32)
     gated, mixed, states, squares = run_forward(table, projected, chan, shared_chan, head_rows)
     packed_length = (ranks, span // LANES, LANES)
-    square_sum = sum_near(jnp.sum(squares, axis=1).reshape(packed_length), "seq").reshape(length)
+    square_sum = sum_near(jnp.sum(squares, axis=1).reshape(packed_length), SEQ).reshape(length)
     scale = lax.rsqrt(square_sum / E + norm_eps)
     normed_low = (gated * scale[:, None] * gated_own).astype(low)
     branch_factor = 2.0 ** (14 - math.ceil(math.log2(0.17 * math.sqrt(E * wide))))
@@ -863,18 +855,18 @@
     upstream_low = jnp.stack([after(part, out_half) for part in up_parts]).reshape(length, width)
     normed_grad = dot(upstream_low, out_full)
     pull_sum = jnp.sum(normed_grad * gated_own * gated, axis=1).reshape(packed_length)
-    pull_sum = sum_near(pull_sum, "seq").reshape(length)
+    pull_sum = sum_near(pull_sum, SEQ).reshape(length)
     stats = jnp.stack([scale, scale * scale * scale * (pull_sum / E)])
     stats = jnp.pad(stats, ((0, 6), (0, 0)))
     out_grad_part = dot(upstream_low.T, normed_low)
-    out_scatter = Scatter([out_grad_part], "dp")
+    out_scatter = Scatter([out_grad_part], DP)
     out_scatter.step()
     gate_low, mix_grad, gate_square, gain_rows = run_gate(projected, gated, mixed, normed_grad, chan, stats)
     gated_grad = gain_rows[0]
 
-    branch_parts = send_near(out_half, "seq")
-
-    gate_scatter = Scatter([dot(hidden.T, gate_low)], "dp", 1)
+    branch_parts = send_near(out_half, SEQ)
+
+    gate_scatter = Scatter([dot(hidden.T, gate_low)], DP, 1)
     gate_scatter.step()
     carried = (
         zeros((pairs, NST, LANES)), zeros((pairs, 8, LANES)), zeros((8, 2 * NST)),
@@ -893,7 +885,7 @@
                 [block.reshape(ranks, rows, wide) for scatter in early for block in scatter.finish()], axis=2
             )
             early_packed = pack_half(early_sums, jnp.max(jnp.abs(early_sums), axis=-1, keepdims=True))
-            early_slots = slots_of(early_sums, early_packed, "seq")
+            early_slots = slots_of(early_sums, early_packed, SEQ)
             ready = (early_packed,)
         mix_grad = after(mix_grad, *ready)
         result = run_backward(
@@ -908,17 +900,17 @@
     power = jnp.clip(jnp.ceil(jnp.log2(bound)) - 14.0, -120.0, 120.0)
     shared_parts = shared_grad.reshape(ranks, span, 2 * NST)
     lines_of_power = jnp.broadcast_to(power[:, None, None], (ranks, 8, 2 * NST))
-    shared_sent = send_near(jnp.concatenate([shared_parts, lines_of_power], axis=1), "seq")
+    shared_sent = send_near(jnp.concatenate([shared_parts, lines_of_power], axis=1), SEQ)
 
     factors = jnp.exp2(-power)[:, None, None]
     hidden_part = dot(gate_low, in_full[:, :wide].T) + dot(conv_low, in_full[:, wide + 2 * NST :].T)
     hidden_part = hidden_part.reshape(ranks, span, width)
     hidden_half = (hidden_part * factors).astype(half)
-    hidden_parts = send_near(hidden_half, "seq")
+    hidden_parts = send_near(hidden_half, SEQ)
 
     split = 4 * LANES
     conv_parts = [dot(hidden.T, conv_low[:, :split]), dot(hidden.T, conv_low[:, split:])]
-    late = Scatter(conv_parts, "dp")
+    late = Scatter(conv_parts, DP)
     normed_own = normed_low[:span]
     for turn in range(late.steps):
         if turn == 1:
@@ -933,7 +925,7 @@
         shared_own = shared_own + part[:span]
     shared_own = shared_own.astype(low)
     shared_grad_part = dot(hidden_own.T, shared_own)
-    last = Scatter([shared_grad_part], "dp", 1)
+    last = Scatter([shared_grad_part], DP, 1)
     for turn in range(last.steps):
         if turn == last.steps - 1:
             hidden_parts = [after(part, *last.blocks) for part in hidden_parts]
@@ -952,7 +944,7 @@
 
     late_sums = jnp.concatenate([block.reshape(ranks, rows, -1) for block in late.blocks + last.blocks], axis=2)
     late_packed = pack_half(late_sums, jnp.max(jnp.abs(late_sums), axis=-1, keepdims=True))
-    late_slots = slots_of(late_sums, late_packed, "seq")
+    late_slots = slots_of(late_sums, late_packed, SEQ)
 
     for part, exponent in zip(hidden_parts, power_parts):
         hidden_grad = hidden_grad + part.astype(jnp.float32) * jnp.exp2(exponent)
@@ -991,8 +983,11 @@
     norm_terms = norm_terms.reshape(groups, ranks, norm_lines, LANES)
     term_lines += norm_lines
     terms = jnp.concatenate([norm_terms, terms], axis=2).reshape(groups, ranks * term_lines, LANES)
-    summed = scatter_bits(terms, "dp").reshape(ranks, term_lines, LANES)
-    summed = exchange_sum(summed, "seq").reshape(-1)
+    small_scatter = Scatter([terms], DP)
+    for _ in range(small_scatter.steps):
+        small_scatter.step()
+    summed = small_scatter.blocks[0].reshape(ranks, term_lines, LANES)
+    summed = exchange_sum(summed, SEQ).reshape(-1)
     grad_norm_gain = summed[:rows]
     at = norm_lines * LANES
     grad_conv_weight = summed[at : at + CONVW * taps].reshape(CONVW, taps)
@@ -1097,75 +1092,75 @@
 
 def solution(mesh):
     in_specs = (
-        P("dp", "seq", None),
-        P("dp", "seq", None),
-        P(("dp", "seq")),
-        P(("dp", "seq"), None),
-        P(None, ("dp", "seq")),
-        P(("dp", "seq")),
-        P(),
-        P(),
-        P(),
-        P(("dp", "seq")),
-        P(("dp", "seq"), None),
-        P(("dp", "seq")),
-        P(("dp", "seq")),
-        P(("dp", "seq"), None),
-        P(("dp", "seq"), None),
-        P(None, ("dp", "seq")),
-        P(None, ("dp", "seq")),
-        P(("dp", "seq")),
-        P(("dp", "seq")),
-        P(),
-        P(),
-        P(),
-        P(),
-        P(),
-        P(),
-        P(("dp", "seq")),
-        P(("dp", "seq")),
-        P(("dp", "seq"), None),
-        P(("dp", "seq"), None),
+        P(DP, SEQ, None),
+        P(DP, SEQ, None),
+        P((DP, SEQ)),
+        P((DP, SEQ), None),
+        P(None, (DP, SEQ)),
+        P((DP, SEQ)),
+        P(),
+        P(),
+        P(),
+        P((DP, SEQ)),
+        P((DP, SEQ), None),
+        P((DP, SEQ)),
+        P((DP, SEQ)),
+        P((DP, SEQ), None),
+        P((DP, SEQ), None),
+        P(None, (DP, SEQ)),
+        P(None, (DP, SEQ)),
+        P((DP, SEQ)),
+        P((DP, SEQ)),
+        P(),
+        P(),
+        P(),
+        P(),
+        P(),
+        P(),
+        P((DP, SEQ)),
+        P((DP, SEQ)),
+        P((DP, SEQ), None),
+        P((DP, SEQ), None),
     )
     out_specs = (
-        P("dp", "seq", None),
-        P("dp", "seq", None),
-        P(("dp", "seq")),
-        P(("dp", "seq"), None),
-        P(None, ("dp", "seq")),
-        P(("dp", "seq")),
-        P(),
-        P(),
-        P(),
-        P(("dp", "seq")),
-        P(("dp", "seq"), None),
-        P(("dp", "seq")),
-        P(("dp", "seq")),
-        P(("dp", "seq")),
-        P(("dp", "seq"), None),
-        P(("dp", "seq"), None),
-        P(("dp", "seq"), None),
-        P(None, ("dp", "seq")),
-        P(None, ("dp", "seq")),
-        P(None, ("dp", "seq")),
-        P(("dp", "seq")),
-        P(("dp", "seq")),
-        P(("dp", "seq")),
-        P(),
-        P(),
-        P(),
-        P(),
-        P(),
-        P(),
-        P(),
-        P(),
-        P(),
-        P(("dp", "seq")),
-        P(("dp", "seq")),
-        P(("dp", "seq")),
-        P(("dp", "seq"), None),
-        P(("dp", "seq"), None),
-        P(("dp", "seq"), None),
+        P(DP, SEQ, None),
+        P(DP, SEQ, None),
+        P((DP, SEQ)),
+        P((DP, SEQ), None),
+        P(None, (DP, SEQ)),
+        P((DP, SEQ)),
+        P(),
+        P(),
+        P(),
+        P((DP, SEQ)),
+        P((DP, SEQ), None),
+        P((DP, SEQ)),
+        P((DP, SEQ)),
+        P((DP, SEQ)),
+        P((DP, SEQ), None),
+        P((DP, SEQ), None),
+        P((DP, SEQ), None),
+        P(None, (DP, SEQ)),
+        P(None, (DP, SEQ)),
+        P(None, (DP, SEQ)),
+        P((DP, SEQ)),
+        P((DP, SEQ)),
+        P((DP, SEQ)),
+        P(),
+        P(),
+        P(),
+        P(),
+        P(),
+        P(),
+        P(),
+        P(),
+        P(),
+        P((DP, SEQ)),
+        P((DP, SEQ)),
+        P((DP, SEQ)),
+        P((DP, SEQ), None),
+        P((DP, SEQ), None),
+        P((DP, SEQ), None),
     )
 
     return jax.shard_map(body, mesh=mesh, in_specs=in_specs, out_specs=out_specs, check_vma=False)

time: 604 us -> 573 us (0.949)
  Pallas kernels: 99.8 us -> 82 us
  waiting for transfers between devices: 152 us -> 169 us
  local copies, waits for them, and re-layouts: 65.6 us -> 57 us
    ppermute x32, waiting for transfers between devices: 56.6 us -> 69.8 us  [shift(): lax.ppermute(block, axis, [(i, (i + distance) % size) for i in range(size)])]
    ppermute x4, waiting for transfers between devices: 15.4 us -> 22.4 us  [step_to(): return lax.ppermute(block, axis, route)]
    dot_general x12, matrix products: 55.2 us -> 49.2 us  [dot(): return jnp.dot(left, right, preferred_element_type=jnp.float32)]
    unnamed x165 -> x159, local copies, waits for them, and re-layouts: 16.8 us -> 18.9 us
    squeeze x15 -> x16, local copies, waits for them, and re-layouts: 10.7 us -> 12.5 us  [halve(): send = lax.dynamic_index_in_dim(block, 1 - own, place, keepdims=False)]
    add x15 -> x18, other arithmetic: 16.2 us -> 17.7 us  [halve(): return (keep + swap(send, axis, bit), [b for b in left if b != bit])]
  transfers between devices with their start and end apart: 71 -> 71, of which waited for: 31 -> 31; matrix products, arithmetic and copies ran while one was open for 24% -> 22% of each run, Pallas kernels for 11% -> 10%
where the time goes in v3:
time: 573 us; the launch traced here: 568 us
  waiting for transfers between devices  169 us (29%)
  starting transfers between devices  155 us (27%)
  Pallas kernels  82 us (14%)
  local copies, waits for them, and re-layouts  57 us (10%)
  other arithmetic  51.2 us (9%)
  matrix products  49.2 us (9%)
    ppermute x32, starting transfers between devices, shift(): lax.ppermute(block, axis, [(i, (i + distance) % size) for i in range(size)])  113 us
    ppermute x32, waiting for transfers between devices, shift(): lax.ppermute(block, axis, [(i, (i + distance) % size) for i in range(size)])  69.8 us
    dot_general x12, matrix products, dot(): return jnp.dot(left, right, preferred_element_type=jnp.float32)  49.2 us
    pallas_call x3, Pallas kernels, run_backward(): pl.pallas_call(functools.partial(backward_kernel, start, chunks), grid_sp...  48.5 us
    ppermute x33, waiting for transfers between devices, swap(): lax.ppermute(block, axis, [(i, i ^ bit) for i in range(lax.axis_size(axis...  46.3 us
    ppermute x2, waiting for transfers between devices, near_parts(): far = lax.ppermute(across, axis, [(2, 3), (1, 0)])  30.2 us
    ppermute x33, starting transfers between devices, swap(): lax.ppermute(block, axis, [(i, i ^ bit) for i in range(lax.axis_size(axis...  28.1 us
    pallas_call x1, Pallas kernels, run_forward(): pl.pallas_call(forward_kernel, grid_spec=pltpu.PrefetchScalarGridSpec(num...  24 us
  transfers between devices with their start and end apart: 71, of which 31 were waited for; matrix products, arithmetic and copies ran while one was open for 22% of the time, Pallas kernels for 10%

profile of v3, /device:TPU:0, one launch (start us, length us, event | category | flops | bytes accessed | tf_op | source)
XLA Modules:
  0.0 567.7 jit_solution(17436728366915532545)
XLA Ops:
  3.6 5.1 collective-permute-start.2
  66.2 8.1 %collective-permute-done.21 = bf16[256,1536]{1,0:T(8,128)(2,1)} collective-permute-done((bf16[256,1536]{1,0:T(8,128)(2,1)S(1)}, bf16[256,1536]{1,0:T(8,128)(2,1)}, u32[]{:S(2)}, u32[]{:S(2)}) %collective-permute-start.21) | collective-permute-done | bytes 786464 | tf_op jit(solution)/shard_map/ppermute | solution.py:38
  85.7 17.4 %collective-permute-done.24 = bf16[256,1536]{1,0:T(8,128)(2,1)S(1)} collective-permute-done((bf16[256,1536]{1,0:T(8,128)(2,1)S(1)}, bf16[256,1536]{1,0:T(8,128)(2,1)S(1)}, u32[]{:S(2)}, u32[]{:S(2)}) %collective-permute-start.24) | collective-permute-done | bytes 786464 | tf_op jit(solution)/shard_map/ppermute | solution.py:44
  103.1 16.2 %collective-permute-done.22 = bf16[256,1536]{1,0:T(8,128)(2,1)S(1)} collective-permute-done((bf16[256,1536]{1,0:T(8,128)(2,1)}, bf16[256,1536]{1,0:T(8,128)(2,1)S(1)}, u32[]{:S(2)}, u32[]{:S(2)}) %collective-permute-start.22) | collective-permute-done | bytes 786464 | tf_op jit(solution)/shard_map/ppermute | solution.py:85
  123.6 6.6 %fusion.92.z_ref.x_ref.shared_ref.step_ref.x_before_ref.shared_before_ref = f32[1024,1920]{1,0:T(8,128)S(1)} fusion(bf16[1024,1536]{1,0:T(8,128)(2,1)S(1)} %bitcast.371, bf16[1536,1920]{1,0:T(8,128)(2,1)S(1)} %bitcast.389), kind=kOutput, calls=%fused_computation.361 | convolution fusion | flops 6039797760 | bytes 16908288 | tf_op jit(solution)/shard_map/dot_general | solution.py:727
  130.2 24.0 %mixer_forward.1 = (f32[1024,768]{1,0:T(8,128)S(1)}, f32[1024,768]{1,0:T(8,128)S(1)}, f32[4,6,128,128]{3,2,1,0:T(8,128)S(1)}, f32[1024,128]{1,0:T(8,128)S(1)}) custom-call(s32[5]{0:T(128)S(1)} %pad_add_fusion.table_ref, f32[1024,1920]{1,0:T(8,128)S(1)} %fusion.92.z_ref.x_ref.shared_ref.step_ref.x_before_ref.shared_before_ref, ...), custom_call_target="tpu_custom_call" | custom-call | tf_op jit(solution)/shard_map/mixer_forward/pallas_call | solution.py:493
  174.0 8.6 %collective-permute-done.25 = f32[4,2,128]{2,1,0:T(2,128)S(1)} collective-permute-done((f32[4,2,128]{2,1,0:T(2,128)S(1)}, f32[4,2,128]{2,1,0:T(2,128)S(1)}, u32[]{:S(2)}, u32[]{:S(2)}) %collective-permute-start.25) | collective-permute-done | bytes 4128 | tf_op jit(solution)/shard_map/ppermute | solution.py:38
  182.5 15.2 %collective-permute-done.26 = f32[4,2,128]{2,1,0:T(2,128)S(1)} collective-permute-done((f32[4,2,128]{2,1,0:T(2,128)S(1)}, f32[4,2,128]{2,1,0:T(2,128)S(1)}, u32[]{:S(2)}, u32[]{:S(2)}) %collective-permute-start.26) | collective-permute-done | bytes 4128 | tf_op jit(solution)/shard_map/ppermute | solution.py:38
  205.7 5.0 collective-permute-done.31
  210.7 14.0 %collective-permute-done.29 = bf16[256,1536]{1,0:T(8,128)(2,1)S(1)} collective-permute-done((bf16[256,1536]{1,0:T(8,128)(2,1)S(1)}, bf16[256,1536]{1,0:T(8,128)(2,1)S(1)}, u32[]{:S(2)}, u32[]{:S(2)}) %collective-permute-start.29) | collective-permute-done | bytes 786464 | tf_op jit(solution)/shard_map/ppermute | solution.py:85
  276.4 23.2 %mixer_backward.3 = (bf16[1024,896]{1,0:T(8,128)(2,1)}, f32[1024,128]{1,0:T(8,128)S(1)}, f32[1024,256]{1,0:T(8,128)S(1)}, f32[6,128,128]{2,1,0:T(8,128)S(1)}, f3...) custom-call(s32[5]{0:T(128)S(1)} %pad_add_fusion.table_ref, ...), custom_call_target="tpu_custom_call" | custom-call | tf_op jit(solution)/shard_map/mixer_backward/pallas_call | solution.py:581
  305.4 12.3 %mixer_backward.4 = (bf16[1024,896]{1,0:T(8,128)(2,1)}, f32[1024,128]{1,0:T(8,128)S(1)}, f32[1024,256]{1,0:T(8,128)S(1)}, f32[6,128,128]{2,1,0:T(8,128)S(1)}, f3...) custom-call(s32[5]{0:T(128)S(1)} %pad_add_fusion.table_ref, ...), custom_call_target="tpu_custom_call", output_to_operand_aliasing={{0}: (19, {}), {1}: (20, {}), {2}: (21, {})} | custom-call | tf_op jit(solution)/shard_map/mixer_backward/pallas_call | solution.py:581
  317.7 13.0 %mixer_backward.5 = (bf16[1024,896]{1,0:T(8,128)(2,1)}, f32[1024,128]{1,0:T(8,128)S(1)}, f32[1024,256]{1,0:T(8,128)S(1)}, f32[6,128,128]{2,1,0:T(8,128)}, f32[6,...) custom-call(s32[5]{0:T(128)S(1)} %pad_add_fusion.table_ref, ...), custom_call_target="tpu_custom_call", output_to_operand_aliasing={{0}: (19, {}), {1}: (20, {}), {2}: (21, {})} | custom-call | tf_op jit(solution)/shard_map/mixer_backward/pallas_call | solution.py:581
  337.5 7.9 %fusion.5 = f32[1024,1536]{1,0:T(8,128)} fusion(bf16[1024,896]{1,0:T(8,128)(2,1)S(1)} %copy-done.29, bf16[1536,1920]{1,0:T(8,128)(2,1)} %bitcast.390), kind=kOutput, calls=%fused_computation.16 | convolution fusion | flops 2818572288 | bytes 10878976 | tf_op jit(solution)/shard_map/dot_general | solution.py:727
  353.1 5.5 convolution_add_fusion
  363.5 5.2 collective-permute-done.47
  368.7 5.7 %collective-permute-start.53 = (f16[256,1536]{1,0:T(8,128)(2,1)S(1)}, f16[256,1536]{1,0:T(8,128)(2,1)S(1)}, u32[]{:S(2)}, u32[]{:S(2)}) collective-permute-start(f16[256,1536]{1,0:T(8,128)(2,1)S(1)} %get-tuple-element.212), channel_id=1, source_target_pairs={{0,1},{1,2},{2,3},{3,0},{4,5},{5,6},{6,7},{7,4},{8,9},{9,10},{10,1... | collective-permute-start | bytes 2359304 | tf_op jit(solution)/shard_map/ppermute | solution.py:38
  380.4 7.1 %collective-permute-done.40 = f32[192,768]{1,0:T(8,128)S(1)} collective-permute-done((f32[192,768]{1,0:T(8,128)S(1)}, f32[192,768]{1,0:T(8,128)S(1)}, u32[]{:S(2)}, u32[]{:S(2)}) %collective-permute-start.40) | collective-permute-done | bytes 589856 | tf_op jit(solution)/shard_map/ppermute | solution.py:48
  394.8 9.2 %collective-permute-done.51 = f32[2,192,256]{2,1,0:T(8,128)S(1)} collective-permute-done((f32[2,192,256]{2,1,0:T(8,128)S(1)}, f32[2,192,256]{2,1,0:T(8,128)S(1)}, u32[]{:S(2)}, u32[]{:S(2)}) %collective-permute-start.51) | collective-permute-done | bytes 393248 | tf_op jit(solution)/shard_map/ppermute | solution.py:48
  406.0 30.4 %collective-permute-start.44 = (f16[256,1536]{1,0:T(8,128)(2,1)}, f16[256,1536]{1,0:T(8,128)(2,1)}, u32[]{:S(2)}, u32[]{:S(2)}) collective-permute-start(f16[256,1536]{1,0:T(8,128)(2,1)} %get-tuple-element.216), channel_id=1, source_target_pairs={{0,2},{1,3},{2,0},{3,1},{4,6},{5,7},{6,4},{7,5},{8,10},{9,11},{10,... | collective-permute-start | bytes 2359304 | tf_op jit(solution)/shard_map/ppermute | solution.py:38
  437.6 25.0 %collective-permute-start.62 = (f16[48,1664]{1,0:T(8,128)(2,1)}, f16[48,1664]{1,0:T(8,128)(2,1)}, u32[]{:S(2)}, u32[]{:S(2)}) collective-permute-start(f16[48,1664]{1,0:T(8,128)(2,1)} %get-tuple-element.262), channel_id=1, source_target_pairs={{0,3},{1,0},{2,1},{3,2},{4,7},{5,4},{6,5},{7,6},{8,11},{9,8},{10,9... | collective-permute-start | bytes 479240 | tf_op jit(solution)/shard_map/ppermute | solution.py:38
  477.8 13.5 %collective-permute-done.61 = f16[48,1664]{1,0:T(8,128)(2,1)} collective-permute-done((f16[48,1664]{1,0:T(8,128)(2,1)}, f16[48,1664]{1,0:T(8,128)(2,1)}, u32[]{:S(2)}, u32[]{:S(2)}) %collective-permute-start.61) | collective-permute-done | bytes 159776 | tf_op jit(solution)/shard_map/ppermute | solution.py:38
  499.1 9.0 %collective-permute-done.43 = f16[256,1536]{1,0:T(8,128)(2,1)} collective-permute-done((f16[256,1536]{1,0:T(8,128)(2,1)}, f16[256,1536]{1,0:T(8,128)(2,1)}, u32[]{:S(2)}, u32[]{:S(2)}) %collective-permute-start.43) | collective-permute-done | bytes 786464 | tf_op jit(solution)/shard_map/ppermute | solution.py:38
  520.0 8.6 %collective-permute-start.59 = (f32[7,128]{1,0:T(8,128)S(1)}, f32[7,128]{1,0:T(8,128)S(1)}, u32[]{:S(2)}, u32[]{:S(2)}) collective-permute-start(f32[7,128]{1,0:T(8,128)S(1)} %get-tuple-element.297), channel_id=1, source_target_pairs={{0,3},{1,0},{2,1},{3,2},{4,7},{5,4},{6,5},{7,6},{8,11},{9,8},{10,9... | collective-permute-start | bytes 10760 | tf_op jit(solution)/shard_map/ppermute | solution.py:38
  (538 shorter events, 267.0 us)
Async XLA Ops:
  31.3 43.0 %collective-permute-start.21 = (bf16[256,1536]{1,0:T(8,128)(2,1)S(1)}, bf16[256,1536]{1,0:T(8,128)(2,1)}, u32[]{:S(2)}, u32[]{:S(2)}) collective-permute-start(bf16[256,1536]{1,0:T(8,128)(2,1)S(1)} %multiply_convert_fusion.3), channel_id=1, source_target_pairs={{0,2},{1,3},{2,0},{3,1},{4,6},{5,7},{6,4},{7,5},{8,10},{9,11},{10,... | collective-permute-start | bytes 2359304 | tf_op jit(solution)/shard_map/ppermute | solution.py:38
  32.4 53.2 %collective-permute-start.23 = (bf16[256,1536]{1,0:T(8,128)(2,1)S(1)}, bf16[256,1536]{1,0:T(8,128)(2,1)}, u32[]{:S(2)}, u32[]{:S(2)}) collective-permute-start(bf16[256,1536]{1,0:T(8,128)(2,1)S(1)} %multiply_convert_fusion.3), channel_id=1, source_target_pairs={{0,1},{1,2},{2,3},{4,5},{5,6},{6,7},{8,9},{9,10},{10,11},{12,13},{... | collective-permute-start | bytes 2359304 | tf_op jit(solution)/shard_map/ppermute | solution.py:44
  62.8 40.3 %collective-permute-start.24 = (bf16[256,1536]{1,0:T(8,128)(2,1)S(1)}, bf16[256,1536]{1,0:T(8,128)(2,1)S(1)}, u32[]{:S(2)}, u32[]{:S(2)}) collective-permute-start(bf16[256,1536]{1,0:T(8,128)(2,1)S(1)} %multiply_convert_fusion.3), channel_id=1, source_target_pairs={{1,0},{2,1},{3,2},{5,4},{6,5},{7,6},{9,8},{10,9},{11,10},{13,12},{... | collective-permute-start | bytes 2359304 | tf_op jit(solution)/shard_map/ppermute | solution.py:44
  76.2 43.1 %collective-permute-start.22 = (bf16[256,1536]{1,0:T(8,128)(2,1)}, bf16[256,1536]{1,0:T(8,128)(2,1)S(1)}, u32[]{:S(2)}, u32[]{:S(2)}) collective-permute-start(bf16[256,1536]{1,0:T(8,128)(2,1)} %collective-permute-done.21), channel_id=1, source_target_pairs={{2,3},{1,0},{6,7},{5,4},{10,11},{9,8},{14,15},{13,12},{18,19},{17,... | collective-permute-start | bytes 2359304 | tf_op jit(solution)/shard_map/ppermute | solution.py:85
  83.1 36.4 %collective-permute-start.14 = (bf16[2,2,1,96,1920]{4,3,2,1,0:T(8,128)(2,1)S(1)}, bf16[2,2,1,96,1920]{4,3,2,1,0:T(8,128)(2,1)S(1)}, u32[]{:S(2)}, u32[]{:S(2)}) collective-permute-start(bf16[2,2,1,96,1920]{4,3,2,1,0:T(8,128)(2,1)S(1)} %pad_maximum_fusion.3), channel_id=1, source_target_pairs={{0,4},{4,0},{8,12},{12,8},{16,20},{20,16},{24,28},{28,24},{1,5},{5... | collective-permute-start | bytes 4423688 | tf_op jit(solution)/shard_map/ppermute | solution.py:48
  83.4 36.4 %collective-permute-start.11 = (bf16[2,2,1,96,1920]{4,3,2,1,0:T(8,128)(2,1)S(1)}, bf16[2,2,1,96,1920]{4,3,2,1,0:T(8,128)(2,1)S(1)}, u32[]{:S(2)}, u32[]{:S(2)}) collective-permute-start(bf16[2,2,1,96,1920]{4,3,2,1,0:T(8,128)(2,1)S(1)} %pad_maximum_fusion.2), channel_id=1, source_target_pairs={{0,4},{4,0},{8,12},{12,8},{16,20},{20,16},{24,28},{28,24},{1,5},{5... | collective-permute-start | bytes 4423688 | tf_op jit(solution)/shard_map/ppermute | solution.py:48
  159.4 38.3 %collective-permute-start.28 = (bf16[256,1536]{1,0:T(8,128)(2,1)S(1)}, bf16[256,1536]{1,0:T(8,128)(2,1)S(1)}, u32[]{:S(2)}, u32[]{:S(2)}) collective-permute-start(bf16[256,1536]{1,0:T(8,128)(2,1)S(1)} %bitcast_convert_fusion), channel_id=1, source_target_pairs={{0,2},{1,3},{2,0},{3,1},{4,6},{5,7},{6,4},{7,5},{8,10},{9,11},{10,... | collective-permute-start | bytes 2359304 | tf_op jit(solution)/shard_map/ppermute | solution.py:38
  161.7 36.0 %collective-permute-start.26 = (f32[4,2,128]{2,1,0:T(2,128)S(1)}, f32[4,2,128]{2,1,0:T(2,128)S(1)}, u32[]{:S(2)}, u32[]{:S(2)}) collective-permute-start(f32[4,2,128]{2,1,0:T(2,128)S(1)} %bitcast.432), channel_id=1, source_target_pairs={{0,2},{1,3},{2,0},{3,1},{4,6},{5,7},{6,4},{7,5},{8,10},{9,11},{10,... | collective-permute-start | bytes 12296 | tf_op jit(solution)/shard_map/ppermute | solution.py:38
  164.4 41.3 %collective-permute-start.30 = (bf16[256,1536]{1,0:T(8,128)(2,1)S(1)}, bf16[256,1536]{1,0:T(8,128)(2,1)}, u32[]{:S(2)}, u32[]{:S(2)}) collective-permute-start(bf16[256,1536]{1,0:T(8,128)(2,1)S(1)} %bitcast_convert_fusion), channel_id=1, source_target_pairs={{0,1},{1,2},{2,3},{4,5},{5,6},{6,7},{8,9},{9,10},{10,11},{12,13},{... | collective-permute-start | bytes 2359304 | tf_op jit(solution)/shard_map/ppermute | solution.py:44
  172.6 38.1 %collective-permute-start.31 = (bf16[256,1536]{1,0:T(8,128)(2,1)S(1)}, bf16[256,1536]{1,0:T(8,128)(2,1)S(1)}, u32[]{:S(2)}, u32[]{:S(2)}) collective-permute-start(bf16[256,1536]{1,0:T(8,128)(2,1)S(1)} %bitcast_convert_fusion), channel_id=1, source_target_pairs={{1,0},{2,1},{3,2},{5,4},{6,5},{7,6},{9,8},{10,9},{11,10},{13,12},{... | collective-permute-start | bytes 2359304 | tf_op jit(solution)/shard_map/ppermute | solution.py:44
  262.1 37.5 %collective-permute-start.37 = (f32[2,192,768]{2,1,0:T(8,128)}, f32[2,192,768]{2,1,0:T(8,128)}, u32[]{:S(2)}, u32[]{:S(2)}) collective-permute-start(f32[2,192,768]{2,1,0:T(8,128)} %dynamic-slice_bitcast_fusion.5), channel_id=1, source_target_pairs={{0,8},{4,12},{8,0},{12,4},{16,24},{20,28},{24,16},{28,20},{1,9},{5... | collective-permute-start | bytes 3538952 | tf_op jit(solution)/shard_map/ppermute | solution.py:48
  267.4 35.6 %collective-permute-start.38 = (f32[2,192,768]{2,1,0:T(8,128)}, f32[2,192,768]{2,1,0:T(8,128)}, u32[]{:S(2)}, u32[]{:S(2)}) collective-permute-start(f32[2,192,768]{2,1,0:T(8,128)} %dynamic-slice_bitcast_fusion.4), channel_id=1, source_target_pairs={{0,16},{4,20},{8,24},{12,28},{16,0},{20,4},{24,8},{28,12},{1,17},{... | collective-permute-start | bytes 3538952 | tf_op jit(solution)/shard_map/ppermute | solution.py:48
  273.5 225.5 %collective-permute-start.45 = (f16[256,1536]{1,0:T(8,128)(2,1)}, f16[256,1536]{1,0:T(8,128)(2,1)}, u32[]{:S(2)}, u32[]{:S(2)}) collective-permute-start(f16[256,1536]{1,0:T(8,128)(2,1)} %get-tuple-element.215), channel_id=1, source_target_pairs={{0,1},{1,2},{2,3},{3,0},{4,5},{5,6},{6,7},{7,4},{8,9},{9,10},{10,1... | collective-permute-start | bytes 2359304 | tf_op jit(solution)/shard_map/ppermute | solution.py:38
  302.2 73.6 %collective-permute-start.39 = (f32[192,768]{1,0:T(8,128)}, f32[192,768]{1,0:T(8,128)}, u32[]{:S(2)}, u32[]{:S(2)}) collective-permute-start(f32[192,768]{1,0:T(8,128)} %dynamic-slice_bitcast_fusion.10), channel_id=1, source_target_pairs={{0,16},{4,20},{8,24},{12,28},{16,0},{20,4},{24,8},{28,12},{1,17},{... | collective-permute-start | bytes 1769480 | tf_op jit(solution)/shard_map/ppermute | solution.py:48
  363.5 29.5 %collective-permute-start.42 = (f32[2,2,192,384]{3,2,1,0:T(8,128)S(1)}, f32[2,2,192,384]{3,2,1,0:T(8,128)S(1)}, u32[]{:S(2)}, u32[]{:S(2)}) collective-permute-start(f32[2,2,192,384]{3,2,1,0:T(8,128)S(1)} %copy-done.48), channel_id=1, source_target_pairs={{0,4},{4,0},{8,12},{12,8},{16,20},{20,16},{24,28},{28,24},{1,5},{5... | collective-permute-start | bytes 3538952 | tf_op jit(solution)/shard_map/ppermute | solution.py:48
  368.7 37.3 %collective-permute-start.53 = (f16[256,1536]{1,0:T(8,128)(2,1)S(1)}, f16[256,1536]{1,0:T(8,128)(2,1)S(1)}, u32[]{:S(2)}, u32[]{:S(2)}) collective-permute-start(f16[256,1536]{1,0:T(8,128)(2,1)S(1)} %get-tuple-element.212), channel_id=1, source_target_pairs={{0,1},{1,2},{2,3},{3,0},{4,5},{5,6},{6,7},{7,4},{8,9},{9,10},{10,1... | collective-permute-start | bytes 2359304 | tf_op jit(solution)/shard_map/ppermute | solution.py:38
  375.8 61.8 %collective-permute-start.52 = (f16[256,1536]{1,0:T(8,128)(2,1)S(1)}, f16[256,1536]{1,0:T(8,128)(2,1)S(1)}, u32[]{:S(2)}, u32[]{:S(2)}) collective-permute-start(f16[256,1536]{1,0:T(8,128)(2,1)S(1)} %get-tuple-element.213), channel_id=1, source_target_pairs={{0,2},{1,3},{2,0},{3,1},{4,6},{5,7},{6,4},{7,5},{8,10},{9,11},{10,... | collective-permute-start | bytes 2359304 | tf_op jit(solution)/shard_map/ppermute | solution.py:38
  389.8 74.0 %collective-permute-start.49 = (f16[256,1536]{1,0:T(8,128)(2,1)S(1)}, f16[256,1536]{1,0:T(8,128)(2,1)S(1)}, u32[]{:S(2)}, u32[]{:S(2)}) collective-permute-start(f16[256,1536]{1,0:T(8,128)(2,1)S(1)} %get-tuple-element.211), channel_id=1, source_target_pairs={{0,3},{1,0},{2,1},{3,2},{4,7},{5,4},{6,5},{7,6},{8,11},{9,8},{10,9... | collective-permute-start | bytes 2359304 | tf_op jit(solution)/shard_map/ppermute | solution.py:38
  404.0 67.1 %collective-permute-start.41 = (f32[2,2,192,512]{3,2,1,0:T(8,128)}, f32[2,2,192,512]{3,2,1,0:T(8,128)}, u32[]{:S(2)}, u32[]{:S(2)}) collective-permute-start(f32[2,2,192,512]{3,2,1,0:T(8,128)} %dynamic-slice_bitcast_fusion.2), channel_id=1, source_target_pairs={{0,4},{4,0},{8,12},{12,8},{16,20},{20,16},{24,28},{28,24},{1,5},{5... | collective-permute-start | bytes 4718600 | tf_op jit(solution)/shard_map/ppermute | solution.py:48
  406.0 93.0 %collective-permute-start.44 = (f16[256,1536]{1,0:T(8,128)(2,1)}, f16[256,1536]{1,0:T(8,128)(2,1)}, u32[]{:S(2)}, u32[]{:S(2)}) collective-permute-start(f16[256,1536]{1,0:T(8,128)(2,1)} %get-tuple-element.216), channel_id=1, source_target_pairs={{0,2},{1,3},{2,0},{3,1},{4,6},{5,7},{6,4},{7,5},{8,10},{9,11},{10,... | collective-permute-start | bytes 2359304 | tf_op jit(solution)/shard_map/ppermute | solution.py:38
  437.6 36.8 %collective-permute-start.62 = (f16[48,1664]{1,0:T(8,128)(2,1)}, f16[48,1664]{1,0:T(8,128)(2,1)}, u32[]{:S(2)}, u32[]{:S(2)}) collective-permute-start(f16[48,1664]{1,0:T(8,128)(2,1)} %get-tuple-element.262), channel_id=1, source_target_pairs={{0,3},{1,0},{2,1},{3,2},{4,7},{5,4},{6,5},{7,6},{8,11},{9,8},{10,9... | collective-permute-start | bytes 479240 | tf_op jit(solution)/shard_map/ppermute | solution.py:38
  474.4 33.6 %collective-permute-start.43 = (f16[256,1536]{1,0:T(8,128)(2,1)}, f16[256,1536]{1,0:T(8,128)(2,1)}, u32[]{:S(2)}, u32[]{:S(2)}) collective-permute-start(f16[256,1536]{1,0:T(8,128)(2,1)} %get-tuple-element.214), channel_id=1, source_target_pairs={{0,3},{1,0},{2,1},{3,2},{4,7},{5,4},{6,5},{7,6},{8,11},{9,8},{10,9... | collective-permute-start | bytes 2359304 | tf_op jit(solution)/shard_map/ppermute | solution.py:38
  491.3 46.2 %collective-permute-start.65 = (f32[2,192,384]{2,1,0:T(8,128)}, f32[2,192,384]{2,1,0:T(8,128)}, u32[]{:S(2)}, u32[]{:S(2)}) collective-permute-start(f32[2,192,384]{2,1,0:T(8,128)} %dynamic-slice_bitcast_fusion.8), channel_id=1, source_target_pairs={{0,16},{4,20},{8,24},{12,28},{16,0},{20,4},{24,8},{28,12},{1,17},{... | collective-permute-start | bytes 1769480 | tf_op jit(solution)/shard_map/ppermute | solution.py:48
  491.9 36.7 %collective-permute-start.67 = (f32[192,256]{1,0:T(8,128)}, f32[192,256]{1,0:T(8,128)}, u32[]{:S(2)}, u32[]{:S(2)}) collective-permute-start(f32[192,256]{1,0:T(8,128)} %dynamic-slice_bitcast_fusion.15), channel_id=1, source_target_pairs={{0,8},{4,12},{8,0},{12,4},{16,24},{20,28},{24,16},{28,20},{1,9},{5... | collective-permute-start | bytes 589832 | tf_op jit(solution)/shard_map/ppermute | solution.py:48
  (121 other events, 1281.9 us)

commit v4 on v3

--- a/solution.py
+++ b/solution.py
@@ -22,7 +22,6 @@
 
 low = jnp.bfloat16
 half = jnp.float16
-highest = lax.Precision.HIGHEST
 beta_one = 0.9
 beta_two = 0.95
 adam_step = 10.0
@@ -172,16 +171,12 @@
     )
 
 
-def exact_dot(left, right):
-    return jnp.dot(left, right, precision=highest, preferred_element_type=jnp.float32)
-
-
 def softplus(value):
     small = jnp.exp(-jnp.abs(value))
     ratio = small / (2.0 + small)
     square = ratio * ratio
-    series = jnp.full_like(square, 1.0 / 17.0)
-    for power in (15, 13, 11, 9, 7, 5, 3, 1):
+    series = jnp.full_like(square, 1.0 / 15.0)
+    for power in (13, 11, 9, 7, 5, 3, 1):
         series = series * square + 1.0 / power
     return jnp.maximum(value, 0.0) + 2.0 * ratio * series
 
@@ -222,12 +217,19 @@
     return total
 
 
+def running_sum(chosen, value):
+    ones = jnp.where(chosen, 1.0, 0.0).astype(low)
+    return jnp.dot(
+        jnp.concatenate([ones] * 3, axis=1), jnp.concatenate(thirds(value), axis=0), preferred_element_type=jnp.float32
+    )
+
+
 def step_sizes(raw, heads):
     delta = softplus(raw + heads[0:1])
     change = -delta * jnp.exp(heads[1:2])
     size = raw.shape[0]
     below = lax.broadcasted_iota(jnp.int32, (size, size), 0) >= lax.broadcasted_iota(jnp.int32, (size, size), 1)
-    return delta, change, exact_dot(below.astype(jnp.float32), change)
+    return delta, change, running_sum(below, change)
 
 
 def forward_kernel(
@@ -473,7 +475,7 @@
         shared_chan_grad_ref[4:5, :] += jnp.sum(grad_s, axis=0, keepdims=True)
 
         above = lax.broadcasted_iota(jnp.int32, (size, size), 0) <= lax.broadcasted_iota(jnp.int32, (size, size), 1)
-        change_grad = exact_dot(above.astype(jnp.float32), run_grad[...]) + last_grad[0:1, :]
+        change_grad = running_sum(above, run_grad[...]) + last_grad[0:1, :]
         rate = jnp.exp(head_ref[1:2, :])
         raw = step_ref[...] + head_ref[0:1, :]
         raw_grad = (delta_grad[...] - change_grad * rate) * jax.nn.sigmoid(raw)

time: 573 us -> 572 us (level)
  transfers between devices with their start and end apart: 71 -> 71, of which waited for: 31 -> 31; matrix products, arithmetic and copies ran while one was open for 22% -> 22% of each run, Pallas kernels for 10% -> 9%
where the time goes in v4:
time: 572 us; the launch traced here: 566 us
  waiting for transfers between devices  168 us (29%)
  starting transfers between devices  155 us (27%)
  Pallas kernels  80.4 us (14%)
  local copies, waits for them, and re-layouts  57.1 us (10%)
  other arithmetic  51.2 us (9%)
  matrix products  49.1 us (9%)
    ppermute x32, starting transfers between devices, shift(): lax.ppermute(block, axis, [(i, (i + distance) % size) for i in range(size)])  113 us
    ppermute x32, waiting for transfers between devices, shift(): lax.ppermute(block, axis, [(i, (i + distance) % size) for i in range(size)])  69.7 us
    dot_general x12, matrix products, dot(): return jnp.dot(left, right, preferred_element_type=jnp.float32)  49.1 us
    pallas_call x3, Pallas kernels, run_backward(): pl.pallas_call(functools.partial(backward_kernel, start, chunks), grid_sp...  47.4 us
    ppermute x33, waiting for transfers between devices, swap(): lax.ppermute(block, axis, [(i, i ^ bit) for i in range(lax.axis_size(axis...  46.2 us
    ppermute x2, waiting for transfers between devices, near_parts(): far = lax.ppermute(across, axis, [(2, 3), (1, 0)])  30.2 us
    ppermute x33, starting transfers between devices, swap(): lax.ppermute(block, axis, [(i, i ^ bit) for i in range(lax.axis_size(axis...  28.1 us
    pallas_call x1, Pallas kernels, run_forward(): pl.pallas_call(forward_kernel, grid_spec=pltpu.PrefetchScalarGridSpec(num...  23.5 us
  transfers between devices with their start and end apart: 71, of which 31 were waited for; matrix products, arithmetic and copies ran while one was open for 22% of the time, Pallas kernels for 9%

profile of v4, /device:TPU:0, one launch (start us, length us, event | category | flops | bytes accessed | tf_op | source)
XLA Modules:
  0.0 566.4 jit_solution(3313680988155041612)
XLA Ops:
  3.6 5.1 collective-permute-start.2
  66.2 8.1 %collective-permute-done.21 = bf16[256,1536]{1,0:T(8,128)(2,1)} collective-permute-done((bf16[256,1536]{1,0:T(8,128)(2,1)S(1)}, bf16[256,1536]{1,0:T(8,128)(2,1)}, u32[]{:S(2)}, u32[]{:S(2)}) %collective-permute-start.21) | collective-permute-done | bytes 786464 | tf_op jit(solution)/shard_map/ppermute | solution.py:37
  85.7 17.4 %collective-permute-done.24 = bf16[256,1536]{1,0:T(8,128)(2,1)S(1)} collective-permute-done((bf16[256,1536]{1,0:T(8,128)(2,1)S(1)}, bf16[256,1536]{1,0:T(8,128)(2,1)S(1)}, u32[]{:S(2)}, u32[]{:S(2)}) %collective-permute-start.24) | collective-permute-done | bytes 786464 | tf_op jit(solution)/shard_map/ppermute | solution.py:43
  103.1 16.2 %collective-permute-done.22 = bf16[256,1536]{1,0:T(8,128)(2,1)S(1)} collective-permute-done((bf16[256,1536]{1,0:T(8,128)(2,1)}, bf16[256,1536]{1,0:T(8,128)(2,1)S(1)}, u32[]{:S(2)}, u32[]{:S(2)}) %collective-permute-start.22) | collective-permute-done | bytes 786464 | tf_op jit(solution)/shard_map/ppermute | solution.py:84
  123.6 6.6 %fusion.92.z_ref.x_ref.shared_ref.step_ref.x_before_ref.shared_before_ref = f32[1024,1920]{1,0:T(8,128)S(1)} fusion(bf16[1024,1536]{1,0:T(8,128)(2,1)S(1)} %bitcast.371, bf16[1536,1920]{1,0:T(8,128)(2,1)S(1)} %bitcast.389), kind=kOutput, calls=%fused_computation.361 | convolution fusion | flops 6039797760 | bytes 16908288 | tf_op jit(solution)/shard_map/dot_general | solution.py:729
  130.2 23.5 %mixer_forward.1 = (f32[1024,768]{1,0:T(8,128)S(1)}, f32[1024,768]{1,0:T(8,128)S(1)}, f32[4,6,128,128]{3,2,1,0:T(8,128)S(1)}, f32[1024,128]{1,0:T(8,128)S(1)}) custom-call(s32[5]{0:T(128)S(1)} %pad_add_fusion.table_ref, f32[1024,1920]{1,0:T(8,128)S(1)} %fusion.92.z_ref.x_ref.shared_ref.step_ref.x_before_ref.shared_before_ref, ...), custom_call_target="tpu_custom_call" | custom-call | tf_op jit(solution)/shard_map/mixer_forward/pallas_call | solution.py:495
  173.4 8.5 %collective-permute-done.25 = f32[4,2,128]{2,1,0:T(2,128)S(1)} collective-permute-done((f32[4,2,128]{2,1,0:T(2,128)S(1)}, f32[4,2,128]{2,1,0:T(2,128)S(1)}, u32[]{:S(2)}, u32[]{:S(2)}) %collective-permute-start.25) | collective-permute-done | bytes 4128 | tf_op jit(solution)/shard_map/ppermute | solution.py:37
  182.0 15.2 %collective-permute-done.26 = f32[4,2,128]{2,1,0:T(2,128)S(1)} collective-permute-done((f32[4,2,128]{2,1,0:T(2,128)S(1)}, f32[4,2,128]{2,1,0:T(2,128)S(1)}, u32[]{:S(2)}, u32[]{:S(2)}) %collective-permute-start.26) | collective-permute-done | bytes 4128 | tf_op jit(solution)/shard_map/ppermute | solution.py:37
  205.2 5.0 collective-permute-done.31
  210.2 14.0 %collective-permute-done.29 = bf16[256,1536]{1,0:T(8,128)(2,1)S(1)} collective-permute-done((bf16[256,1536]{1,0:T(8,128)(2,1)S(1)}, bf16[256,1536]{1,0:T(8,128)(2,1)S(1)}, u32[]{:S(2)}, u32[]{:S(2)}) %collective-permute-start.29) | collective-permute-done | bytes 786464 | tf_op jit(solution)/shard_map/ppermute | solution.py:84
  275.9 22.7 %mixer_backward.3 = (bf16[1024,896]{1,0:T(8,128)(2,1)}, f32[1024,128]{1,0:T(8,128)S(1)}, f32[1024,256]{1,0:T(8,128)S(1)}, f32[6,128,128]{2,1,0:T(8,128)S(1)}, f3...) custom-call(s32[5]{0:T(128)S(1)} %pad_add_fusion.table_ref, ...), custom_call_target="tpu_custom_call" | custom-call | tf_op jit(solution)/shard_map/mixer_backward/pallas_call | solution.py:583
  304.4 12.0 %mixer_backward.4 = (bf16[1024,896]{1,0:T(8,128)(2,1)}, f32[1024,128]{1,0:T(8,128)S(1)}, f32[1024,256]{1,0:T(8,128)S(1)}, f32[6,128,128]{2,1,0:T(8,128)S(1)}, f3...) custom-call(s32[5]{0:T(128)S(1)} %pad_add_fusion.table_ref, ...), custom_call_target="tpu_custom_call", output_to_operand_aliasing={{0}: (19, {}), {1}: (20, {}), {2}: (21, {})} | custom-call | tf_op jit(solution)/shard_map/mixer_backward/pallas_call | solution.py:583
  316.4 12.7 %mixer_backward.5 = (bf16[1024,896]{1,0:T(8,128)(2,1)}, f32[1024,128]{1,0:T(8,128)S(1)}, f32[1024,256]{1,0:T(8,128)S(1)}, f32[6,128,128]{2,1,0:T(8,128)}, f32[6,...) custom-call(s32[5]{0:T(128)S(1)} %pad_add_fusion.table_ref, ...), custom_call_target="tpu_custom_call", output_to_operand_aliasing={{0}: (19, {}), {1}: (20, {}), {2}: (21, {})} | custom-call | tf_op jit(solution)/shard_map/mixer_backward/pallas_call | solution.py:583
  335.9 7.9 %fusion.5 = f32[1024,1536]{1,0:T(8,128)} fusion(bf16[1024,896]{1,0:T(8,128)(2,1)S(1)} %copy-done.29, bf16[1536,1920]{1,0:T(8,128)(2,1)} %bitcast.390), kind=kOutput, calls=%fused_computation.16 | convolution fusion | flops 2818572288 | bytes 10878976 | tf_op jit(solution)/shard_map/dot_general | solution.py:729
  351.4 5.5 convolution_add_fusion
  361.9 5.2 collective-permute-done.47
  367.1 5.7 %collective-permute-start.53 = (f16[256,1536]{1,0:T(8,128)(2,1)S(1)}, f16[256,1536]{1,0:T(8,128)(2,1)S(1)}, u32[]{:S(2)}, u32[]{:S(2)}) collective-permute-start(f16[256,1536]{1,0:T(8,128)(2,1)S(1)} %get-tuple-element.212), channel_id=1, source_target_pairs={{0,1},{1,2},{2,3},{3,0},{4,5},{5,6},{6,7},{7,4},{8,9},{9,10},{10,1... | collective-permute-start | bytes 2359304 | tf_op jit(solution)/shard_map/ppermute | solution.py:37
  378.7 7.1 %collective-permute-done.40 = f32[192,768]{1,0:T(8,128)S(1)} collective-permute-done((f32[192,768]{1,0:T(8,128)S(1)}, f32[192,768]{1,0:T(8,128)S(1)}, u32[]{:S(2)}, u32[]{:S(2)}) %collective-permute-start.40) | collective-permute-done | bytes 589856 | tf_op jit(solution)/shard_map/ppermute | solution.py:47
  393.2 9.1 %collective-permute-done.51 = f32[2,192,256]{2,1,0:T(8,128)S(1)} collective-permute-done((f32[2,192,256]{2,1,0:T(8,128)S(1)}, f32[2,192,256]{2,1,0:T(8,128)S(1)}, u32[]{:S(2)}, u32[]{:S(2)}) %collective-permute-start.51) | collective-permute-done | bytes 393248 | tf_op jit(solution)/shard_map/ppermute | solution.py:47
  404.3 30.4 %collective-permute-start.44 = (f16[256,1536]{1,0:T(8,128)(2,1)}, f16[256,1536]{1,0:T(8,128)(2,1)}, u32[]{:S(2)}, u32[]{:S(2)}) collective-permute-start(f16[256,1536]{1,0:T(8,128)(2,1)} %get-tuple-element.216), channel_id=1, source_target_pairs={{0,2},{1,3},{2,0},{3,1},{4,6},{5,7},{6,4},{7,5},{8,10},{9,11},{10,... | collective-permute-start | bytes 2359304 | tf_op jit(solution)/shard_map/ppermute | solution.py:37
  436.0 25.0 %collective-permute-start.62 = (f16[48,1664]{1,0:T(8,128)(2,1)}, f16[48,1664]{1,0:T(8,128)(2,1)}, u32[]{:S(2)}, u32[]{:S(2)}) collective-permute-start(f16[48,1664]{1,0:T(8,128)(2,1)} %get-tuple-element.262), channel_id=1, source_target_pairs={{0,3},{1,0},{2,1},{3,2},{4,7},{5,4},{6,5},{7,6},{8,11},{9,8},{10,9... | collective-permute-start | bytes 479240 | tf_op jit(solution)/shard_map/ppermute | solution.py:37
  476.1 13.5 %collective-permute-done.61 = f16[48,1664]{1,0:T(8,128)(2,1)} collective-permute-done((f16[48,1664]{1,0:T(8,128)(2,1)}, f16[48,1664]{1,0:T(8,128)(2,1)}, u32[]{:S(2)}, u32[]{:S(2)}) %collective-permute-start.61) | collective-permute-done | bytes 159776 | tf_op jit(solution)/shard_map/ppermute | solution.py:37
  497.5 8.9 %collective-permute-done.43 = f16[256,1536]{1,0:T(8,128)(2,1)} collective-permute-done((f16[256,1536]{1,0:T(8,128)(2,1)}, f16[256,1536]{1,0:T(8,128)(2,1)}, u32[]{:S(2)}, u32[]{:S(2)}) %collective-permute-start.43) | collective-permute-done | bytes 786464 | tf_op jit(solution)/shard_map/ppermute | solution.py:37
  518.3 8.8 %collective-permute-start.59 = (f32[7,128]{1,0:T(8,128)S(1)}, f32[7,128]{1,0:T(8,128)S(1)}, u32[]{:S(2)}, u32[]{:S(2)}) collective-permute-start(f32[7,128]{1,0:T(8,128)S(1)} %get-tuple-element.297), channel_id=1, source_target_pairs={{0,3},{1,0},{2,1},{3,2},{4,7},{5,4},{6,5},{7,6},{8,11},{9,8},{10,9... | collective-permute-start | bytes 10760 | tf_op jit(solution)/shard_map/ppermute | solution.py:37
  (538 shorter events, 267.1 us)
Async XLA Ops:
  31.3 43.0 %collective-permute-start.21 = (bf16[256,1536]{1,0:T(8,128)(2,1)S(1)}, bf16[256,1536]{1,0:T(8,128)(2,1)}, u32[]{:S(2)}, u32[]{:S(2)}) collective-permute-start(bf16[256,1536]{1,0:T(8,128)(2,1)S(1)} %multiply_convert_fusion.3), channel_id=1, source_target_pairs={{0,2},{1,3},{2,0},{3,1},{4,6},{5,7},{6,4},{7,5},{8,10},{9,11},{10,... | collective-permute-start | bytes 2359304 | tf_op jit(solution)/shard_map/ppermute | solution.py:37
  32.4 53.2 %collective-permute-start.23 = (bf16[256,1536]{1,0:T(8,128)(2,1)S(1)}, bf16[256,1536]{1,0:T(8,128)(2,1)}, u32[]{:S(2)}, u32[]{:S(2)}) collective-permute-start(bf16[256,1536]{1,0:T(8,128)(2,1)S(1)} %multiply_convert_fusion.3), channel_id=1, source_target_pairs={{0,1},{1,2},{2,3},{4,5},{5,6},{6,7},{8,9},{9,10},{10,11},{12,13},{... | collective-permute-start | bytes 2359304 | tf_op jit(solution)/shard_map/ppermute | solution.py:43
  62.8 40.3 %collective-permute-start.24 = (bf16[256,1536]{1,0:T(8,128)(2,1)S(1)}, bf16[256,1536]{1,0:T(8,128)(2,1)S(1)}, u32[]{:S(2)}, u32[]{:S(2)}) collective-permute-start(bf16[256,1536]{1,0:T(8,128)(2,1)S(1)} %multiply_convert_fusion.3), channel_id=1, source_target_pairs={{1,0},{2,1},{3,2},{5,4},{6,5},{7,6},{9,8},{10,9},{11,10},{13,12},{... | collective-permute-start | bytes 2359304 | tf_op jit(solution)/shard_map/ppermute | solution.py:43
  76.2 43.1 %collective-permute-start.22 = (bf16[256,1536]{1,0:T(8,128)(2,1)}, bf16[256,1536]{1,0:T(8,128)(2,1)S(1)}, u32[]{:S(2)}, u32[]{:S(2)}) collective-permute-start(bf16[256,1536]{1,0:T(8,128)(2,1)} %collective-permute-done.21), channel_id=1, source_target_pairs={{2,3},{1,0},{6,7},{5,4},{10,11},{9,8},{14,15},{13,12},{18,19},{17,... | collective-permute-start | bytes 2359304 | tf_op jit(solution)/shard_map/ppermute | solution.py:84
  83.1 36.4 %collective-permute-start.14 = (bf16[2,2,1,96,1920]{4,3,2,1,0:T(8,128)(2,1)S(1)}, bf16[2,2,1,96,1920]{4,3,2,1,0:T(8,128)(2,1)S(1)}, u32[]{:S(2)}, u32[]{:S(2)}) collective-permute-start(bf16[2,2,1,96,1920]{4,3,2,1,0:T(8,128)(2,1)S(1)} %pad_maximum_fusion.3), channel_id=1, source_target_pairs={{0,4},{4,0},{8,12},{12,8},{16,20},{20,16},{24,28},{28,24},{1,5},{5... | collective-permute-start | bytes 4423688 | tf_op jit(solution)/shard_map/ppermute | solution.py:47
  83.4 36.4 %collective-permute-start.11 = (bf16[2,2,1,96,1920]{4,3,2,1,0:T(8,128)(2,1)S(1)}, bf16[2,2,1,96,1920]{4,3,2,1,0:T(8,128)(2,1)S(1)}, u32[]{:S(2)}, u32[]{:S(2)}) collective-permute-start(bf16[2,2,1,96,1920]{4,3,2,1,0:T(8,128)(2,1)S(1)} %pad_maximum_fusion.2), channel_id=1, source_target_pairs={{0,4},{4,0},{8,12},{12,8},{16,20},{20,16},{24,28},{28,24},{1,5},{5... | collective-permute-start | bytes 4423688 | tf_op jit(solution)/shard_map/ppermute | solution.py:47
  158.9 38.3 %collective-permute-start.28 = (bf16[256,1536]{1,0:T(8,128)(2,1)S(1)}, bf16[256,1536]{1,0:T(8,128)(2,1)S(1)}, u32[]{:S(2)}, u32[]{:S(2)}) collective-permute-start(bf16[256,1536]{1,0:T(8,128)(2,1)S(1)} %bitcast_convert_fusion), channel_id=1, source_target_pairs={{0,2},{1,3},{2,0},{3,1},{4,6},{5,7},{6,4},{7,5},{8,10},{9,11},{10,... | collective-permute-start | bytes 2359304 | tf_op jit(solution)/shard_map/ppermute | solution.py:37
  161.2 36.0 %collective-permute-start.26 = (f32[4,2,128]{2,1,0:T(2,128)S(1)}, f32[4,2,128]{2,1,0:T(2,128)S(1)}, u32[]{:S(2)}, u32[]{:S(2)}) collective-permute-start(f32[4,2,128]{2,1,0:T(2,128)S(1)} %bitcast.432), channel_id=1, source_target_pairs={{0,2},{1,3},{2,0},{3,1},{4,6},{5,7},{6,4},{7,5},{8,10},{9,11},{10,... | collective-permute-start | bytes 12296 | tf_op jit(solution)/shard_map/ppermute | solution.py:37
  163.9 41.3 %collective-permute-start.30 = (bf16[256,1536]{1,0:T(8,128)(2,1)S(1)}, bf16[256,1536]{1,0:T(8,128)(2,1)}, u32[]{:S(2)}, u32[]{:S(2)}) collective-permute-start(bf16[256,1536]{1,0:T(8,128)(2,1)S(1)} %bitcast_convert_fusion), channel_id=1, source_target_pairs={{0,1},{1,2},{2,3},{4,5},{5,6},{6,7},{8,9},{9,10},{10,11},{12,13},{... | collective-permute-start | bytes 2359304 | tf_op jit(solution)/shard_map/ppermute | solution.py:43
  172.1 38.1 %collective-permute-start.31 = (bf16[256,1536]{1,0:T(8,128)(2,1)S(1)}, bf16[256,1536]{1,0:T(8,128)(2,1)S(1)}, u32[]{:S(2)}, u32[]{:S(2)}) collective-permute-start(bf16[256,1536]{1,0:T(8,128)(2,1)S(1)} %bitcast_convert_fusion), channel_id=1, source_target_pairs={{1,0},{2,1},{3,2},{5,4},{6,5},{7,6},{9,8},{10,9},{11,10},{13,12},{... | collective-permute-start | bytes 2359304 | tf_op jit(solution)/shard_map/ppermute | solution.py:43
  261.5 37.0 %collective-permute-start.37 = (f32[2,192,768]{2,1,0:T(8,128)}, f32[2,192,768]{2,1,0:T(8,128)}, u32[]{:S(2)}, u32[]{:S(2)}) collective-permute-start(f32[2,192,768]{2,1,0:T(8,128)} %dynamic-slice_bitcast_fusion.5), channel_id=1, source_target_pairs={{0,8},{4,12},{8,0},{12,4},{16,24},{20,28},{24,16},{28,20},{1,9},{5... | collective-permute-start | bytes 3538952 | tf_op jit(solution)/shard_map/ppermute | solution.py:47
  266.8 35.1 %collective-permute-start.38 = (f32[2,192,768]{2,1,0:T(8,128)}, f32[2,192,768]{2,1,0:T(8,128)}, u32[]{:S(2)}, u32[]{:S(2)}) collective-permute-start(f32[2,192,768]{2,1,0:T(8,128)} %dynamic-slice_bitcast_fusion.4), channel_id=1, source_target_pairs={{0,16},{4,20},{8,24},{12,28},{16,0},{20,4},{24,8},{28,12},{1,17},{... | collective-permute-start | bytes 3538952 | tf_op jit(solution)/shard_map/ppermute | solution.py:47
  272.9 224.5 %collective-permute-start.45 = (f16[256,1536]{1,0:T(8,128)(2,1)}, f16[256,1536]{1,0:T(8,128)(2,1)}, u32[]{:S(2)}, u32[]{:S(2)}) collective-permute-start(f16[256,1536]{1,0:T(8,128)(2,1)} %get-tuple-element.215), channel_id=1, source_target_pairs={{0,1},{1,2},{2,3},{3,0},{4,5},{5,6},{6,7},{7,4},{8,9},{9,10},{10,1... | collective-permute-start | bytes 2359304 | tf_op jit(solution)/shard_map/ppermute | solution.py:37
  301.1 72.9 %collective-permute-start.39 = (f32[192,768]{1,0:T(8,128)}, f32[192,768]{1,0:T(8,128)}, u32[]{:S(2)}, u32[]{:S(2)}) collective-permute-start(f32[192,768]{1,0:T(8,128)} %dynamic-slice_bitcast_fusion.10), channel_id=1, source_target_pairs={{0,16},{4,20},{8,24},{12,28},{16,0},{20,4},{24,8},{28,12},{1,17},{... | collective-permute-start | bytes 1769480 | tf_op jit(solution)/shard_map/ppermute | solution.py:47
  361.9 29.5 %collective-permute-start.42 = (f32[2,2,192,384]{3,2,1,0:T(8,128)S(1)}, f32[2,2,192,384]{3,2,1,0:T(8,128)S(1)}, u32[]{:S(2)}, u32[]{:S(2)}) collective-permute-start(f32[2,2,192,384]{3,2,1,0:T(8,128)S(1)} %copy-done.48), channel_id=1, source_target_pairs={{0,4},{4,0},{8,12},{12,8},{16,20},{20,16},{24,28},{28,24},{1,5},{5... | collective-permute-start | bytes 3538952 | tf_op jit(solution)/shard_map/ppermute | solution.py:47
  367.1 37.2 %collective-permute-start.53 = (f16[256,1536]{1,0:T(8,128)(2,1)S(1)}, f16[256,1536]{1,0:T(8,128)(2,1)S(1)}, u32[]{:S(2)}, u32[]{:S(2)}) collective-permute-start(f16[256,1536]{1,0:T(8,128)(2,1)S(1)} %get-tuple-element.212), channel_id=1, source_target_pairs={{0,1},{1,2},{2,3},{3,0},{4,5},{5,6},{6,7},{7,4},{8,9},{9,10},{10,1... | collective-permute-start | bytes 2359304 | tf_op jit(solution)/shard_map/ppermute | solution.py:37
  374.1 61.9 %collective-permute-start.52 = (f16[256,1536]{1,0:T(8,128)(2,1)S(1)}, f16[256,1536]{1,0:T(8,128)(2,1)S(1)}, u32[]{:S(2)}, u32[]{:S(2)}) collective-permute-start(f16[256,1536]{1,0:T(8,128)(2,1)S(1)} %get-tuple-element.213), channel_id=1, source_target_pairs={{0,2},{1,3},{2,0},{3,1},{4,6},{5,7},{6,4},{7,5},{8,10},{9,11},{10,... | collective-permute-start | bytes 2359304 | tf_op jit(solution)/shard_map/ppermute | solution.py:37
  388.1 74.1 %collective-permute-start.49 = (f16[256,1536]{1,0:T(8,128)(2,1)S(1)}, f16[256,1536]{1,0:T(8,128)(2,1)S(1)}, u32[]{:S(2)}, u32[]{:S(2)}) collective-permute-start(f16[256,1536]{1,0:T(8,128)(2,1)S(1)} %get-tuple-element.211), channel_id=1, source_target_pairs={{0,3},{1,0},{2,1},{3,2},{4,7},{5,4},{6,5},{7,6},{8,11},{9,8},{10,9... | collective-permute-start | bytes 2359304 | tf_op jit(solution)/shard_map/ppermute | solution.py:37
  402.3 67.1 %collective-permute-start.41 = (f32[2,2,192,512]{3,2,1,0:T(8,128)}, f32[2,2,192,512]{3,2,1,0:T(8,128)}, u32[]{:S(2)}, u32[]{:S(2)}) collective-permute-start(f32[2,2,192,512]{3,2,1,0:T(8,128)} %dynamic-slice_bitcast_fusion.2), channel_id=1, source_target_pairs={{0,4},{4,0},{8,12},{12,8},{16,20},{20,16},{24,28},{28,24},{1,5},{5... | collective-permute-start | bytes 4718600 | tf_op jit(solution)/shard_map/ppermute | solution.py:47
  404.3 93.1 %collective-permute-start.44 = (f16[256,1536]{1,0:T(8,128)(2,1)}, f16[256,1536]{1,0:T(8,128)(2,1)}, u32[]{:S(2)}, u32[]{:S(2)}) collective-permute-start(f16[256,1536]{1,0:T(8,128)(2,1)} %get-tuple-element.216), channel_id=1, source_target_pairs={{0,2},{1,3},{2,0},{3,1},{4,6},{5,7},{6,4},{7,5},{8,10},{9,11},{10,... | collective-permute-start | bytes 2359304 | tf_op jit(solution)/shard_map/ppermute | solution.py:37
  436.0 36.8 %collective-permute-start.62 = (f16[48,1664]{1,0:T(8,128)(2,1)}, f16[48,1664]{1,0:T(8,128)(2,1)}, u32[]{:S(2)}, u32[]{:S(2)}) collective-permute-start(f16[48,1664]{1,0:T(8,128)(2,1)} %get-tuple-element.262), channel_id=1, source_target_pairs={{0,3},{1,0},{2,1},{3,2},{4,7},{5,4},{6,5},{7,6},{8,11},{9,8},{10,9... | collective-permute-start | bytes 479240 | tf_op jit(solution)/shard_map/ppermute | solution.py:37
  472.8 33.6 %collective-permute-start.43 = (f16[256,1536]{1,0:T(8,128)(2,1)}, f16[256,1536]{1,0:T(8,128)(2,1)}, u32[]{:S(2)}, u32[]{:S(2)}) collective-permute-start(f16[256,1536]{1,0:T(8,128)(2,1)} %get-tuple-element.214), channel_id=1, source_target_pairs={{0,3},{1,0},{2,1},{3,2},{4,7},{5,4},{6,5},{7,6},{8,11},{9,8},{10,9... | collective-permute-start | bytes 2359304 | tf_op jit(solution)/shard_map/ppermute | solution.py:37
  489.6 46.3 %collective-permute-start.65 = (f32[2,192,384]{2,1,0:T(8,128)}, f32[2,192,384]{2,1,0:T(8,128)}, u32[]{:S(2)}, u32[]{:S(2)}) collective-permute-start(f32[2,192,384]{2,1,0:T(8,128)} %dynamic-slice_bitcast_fusion.8), channel_id=1, source_target_pairs={{0,16},{4,20},{8,24},{12,28},{16,0},{20,4},{24,8},{28,12},{1,17},{... | collective-permute-start | bytes 1769480 | tf_op jit(solution)/shard_map/ppermute | solution.py:47
  490.3 36.8 %collective-permute-start.67 = (f32[192,256]{1,0:T(8,128)}, f32[192,256]{1,0:T(8,128)}, u32[]{:S(2)}, u32[]{:S(2)}) collective-permute-start(f32[192,256]{1,0:T(8,128)} %dynamic-slice_bitcast_fusion.15), channel_id=1, source_target_pairs={{0,8},{4,12},{8,0},{12,4},{16,24},{20,28},{24,16},{28,20},{1,9},{5... | collective-permute-start | bytes 589832 | tf_op jit(solution)/shard_map/ppermute | solution.py:47
  (121 other events, 1281.6 us)
